TPU v7x, 32 devices: a whole 2x2x4 slice. The times are simulated.
32 devices in a mesh: seq: 16 (over z, x, core), tp: 2 (over y).
Axes of the slice: x: 2, y: 2, z: 4, core: 2. Of those that a mesh axis runs over, the one named last changes fastest.
Arguments:
- hidden: bfloat16 [8192, 4096], P('seq', 'tp'), may hold values from -6 to 6
- w_query: bfloat16 [4096, 4096], P(None, 'tp'), may hold values from -0.09375 to 0.09375
- w_key: bfloat16 [4096, 1024], P(None, 'tp'), may hold values from -0.09375 to 0.09375
- w_value: bfloat16 [4096, 1024], P(None, 'tp'), may hold values from -0.09375 to 0.09375
- w_out: bfloat16 [4096, 4096], P('tp'), may hold values from -0.09375 to 0.09375
- cache_keys: bfloat16 [256, 64, 1024], P('seq', None, 'tp'), may hold values from -52 to 52
- cache_values: bfloat16 [256, 64, 1024], P('seq', None, 'tp'), may hold values from -6 to 6
- cached_len: int32 [16], replicated, may hold values from 0 to 2048, as said below
- page_table: int32 [256, 2], P('seq'), may hold values from 0 to 31, as said below
Outputs:
- attn_out: bfloat16 [8192, 4096], P('seq', 'tp')
Inputs may be any that keep to these rules, and one draw needn't show every extreme that they name: `cached_len`: cached tokens of each request; some request has exactly 2048. `page_table`: row b is (r, j): pool block b holds request r's cached positions j * 64 to j * 64 + 63. Request r owns exactly ceil(cached_len[r] / 64) blocks, with places 0 to that count - 1, each once; every pool block is owned; the 16 blocks of one index of seq hold at most 2 blocks of any one request, and some index holds exactly 2 of some request.
All inputs are finite; a program needn't handle non-finite values.
Results may differ from a plain program's by a relative error of at most 0.019.
Values may be sent and summed in bfloat16 or wider, within the bound.
No kernel may reach another device: no remote copies, remote signals or barrier semaphores. Data moves between devices by JAX's collectives and lax.ppermute only.
A program may use at most 256 MiB of HBM per device.

v0:
```python
import math

import jax
import jax.numpy as jnp
from jax import lax
from jax.sharding import PartitionSpec as P

HD = 128
NEW = 512
CTX = 2048


ROPE_BASE = 1000000.0
masked_score = -1e30


def norm_rope(values, positions):
    values = values * lax.rsqrt(jnp.mean(values * values, axis=-1, keepdims=True) + 1e-06)
    half_width = values.shape[-1] // 2
    freqs = jnp.exp(
        jnp.arange(half_width, dtype=jnp.float32) * (-2.0 * math.log(ROPE_BASE) / values.shape[-1])
    )
    angles = positions.astype(jnp.float32)[:, None] * freqs[None, :]
    cosine = jnp.cos(angles)[:, None, :]
    sine = jnp.sin(angles)[:, None, :]
    first = values[..., :half_width]
    second = values[..., half_width:]
    return jnp.concatenate(
        [first * cosine - second * sine, second * cosine + first * sine], axis=-1
    )


def pick_rows(match, slot_count):
    ranking = jnp.cumsum(match.astype(jnp.int32)) - 1
    slot_ids = jnp.arange(slot_count, dtype=jnp.int32)
    chosen = match[None, :] & (ranking[None, :] == slot_ids[:, None])
    row_ids = jnp.arange(match.shape[0], dtype=jnp.int32)
    picked = jnp.sum(jnp.where(chosen, row_ids[None, :], 0), axis=1)
    present = jnp.any(chosen, axis=1)
    return (picked, present)


def on_device(
    hidden, w_query, w_key, w_value, w_out, cache_keys, cache_values, cached_len, page_table
):
    tokens_here = hidden.shape[0]
    query_heads = w_query.shape[1] // HD
    kv_heads = w_key.shape[1] // HD
    group = query_heads // kv_heads
    block_len = cache_keys.shape[1]
    width_kv = cache_keys.shape[2]
    span_count = NEW // tokens_here
    device = lax.axis_index("seq")
    request = device // span_count
    span = device % span_count
    length = cached_len[request]
    positions = length + span * tokens_here + jnp.arange(tokens_here, dtype=jnp.int32)
    piece = lax.all_gather(hidden, "tp", axis=1, tiled=True)

    def project(weight):
        return jnp.dot(piece, weight, preferred_element_type=jnp.float32)

    query_sum = project(w_query)
    key_sum = project(w_key)
    value_sum = project(w_value)
    queries = norm_rope(query_sum.reshape(tokens_here, query_heads, HD), positions).astype(
        jnp.bfloat16
    )
    grouped = (
        queries.reshape(tokens_here, kv_heads, group, HD)
        .transpose(1, 2, 0, 3)
        .reshape(kv_heads, group * tokens_here, HD)
    )
    fresh_keys = (
        norm_rope(key_sum.reshape(tokens_here, kv_heads, HD), positions)
        .astype(jnp.bfloat16)
        .reshape(tokens_here, kv_heads * HD)
    )
    fresh_values = value_sum.astype(jnp.bfloat16)
    row_query = span * tokens_here + jnp.arange(group * tokens_here, dtype=jnp.int32) % tokens_here

    def attend(state, keys, values, valid):
        keys = keys.reshape(-1, kv_heads, HD)
        values = values.reshape(-1, kv_heads, HD)
        scores = jnp.einsum(
            "krd,nkd->krn", grouped, keys, preferred_element_type=jnp.float32
        ) * HD ** (-0.5)
        scores = jnp.where(valid[None], scores, masked_score)
        running, total, accum = state
        newest = jnp.maximum(running, jnp.max(scores, axis=-1))
        weights = jnp.where(valid[None], jnp.exp(scores - newest[..., None]), 0.0)
        rescale = jnp.exp(running - newest)
        total = total * rescale + jnp.sum(weights, axis=-1)
        accum = accum * rescale[..., None] + jnp.einsum(
            "krn,nkd->krd", weights.astype(jnp.bfloat16), values, preferred_element_type=jnp.float32
        )
        return (newest, total, accum)

    state = (
        jnp.full((kv_heads, group * tokens_here), masked_score, jnp.float32),
        jnp.zeros((kv_heads, group * tokens_here), jnp.float32),
        jnp.zeros((kv_heads, group * tokens_here, HD), jnp.float32),
    )
    carry = state
    piece_keys = lax.all_gather(cache_keys[None], "seq", axis=0, tiled=True)
    piece_values = lax.all_gather(cache_values[None], "seq", axis=0, tiled=True)
    piece_table = lax.all_gather(page_table[None], "seq", axis=0, tiled=True)
    piece_fresh_k = lax.all_gather(fresh_keys[None], "seq", axis=0, tiled=True)
    piece_fresh_v = lax.all_gather(fresh_values[None], "seq", axis=0, tiled=True)
    source_count = piece_keys.shape[0]
    block_count = source_count * piece_keys.shape[1]
    per_peer = max(1, CTX // block_len // lax.axis_size("seq"))
    slot_count = min(block_count, source_count * per_peer)
    flat_table = piece_table.reshape(block_count, 2)
    places = flat_table[:, 1]
    match = (flat_table[:, 0] == request) & (places * block_len < length)
    picked, present = pick_rows(match, slot_count)
    keys_taken = piece_keys.reshape(block_count, block_len, width_kv)[picked].reshape(
        slot_count * block_len, width_kv
    )
    values_taken = piece_values.reshape(block_count, block_len, width_kv)[picked].reshape(
        slot_count * block_len, width_kv
    )
    key_pos = places[picked][:, None] * block_len + jnp.arange(block_len, dtype=jnp.int32)[None, :]
    valid = (present[:, None] & (key_pos < length)).reshape(1, slot_count * block_len)
    carry = attend(carry, keys_taken, values_taken, valid)
    sources = jnp.arange(source_count, dtype=jnp.int32)
    source_count = sources.shape[0]
    slot_count = min(source_count, span_count)
    match = (sources // span_count == request) & (sources % span_count <= span)
    picked, present = pick_rows(match, slot_count)
    keys_taken = piece_fresh_k[picked].reshape(slot_count * tokens_here, width_kv)
    values_taken = piece_fresh_v[picked].reshape(slot_count * tokens_here, width_kv)
    key_index = (sources[picked] % span_count)[:, None] * tokens_here + jnp.arange(
        tokens_here, dtype=jnp.int32
    )[None, :]
    live = jnp.broadcast_to(present[:, None], key_index.shape).reshape(-1)
    valid = live[None, :] & (key_index.reshape(-1)[None, :] <= row_query[:, None])
    state = attend(carry, keys_taken, values_taken, valid)
    running, total, accum = state
    attended = (accum / total[..., None]).astype(jnp.bfloat16)
    attended = (
        attended.reshape(kv_heads, group, tokens_here, HD)
        .transpose(2, 0, 1, 3)
        .reshape(tokens_here, query_heads * HD)
    )
    partial_out = jnp.dot(attended, w_out, preferred_element_type=jnp.float32)
    return lax.psum_scatter(partial_out.astype(jnp.bfloat16), "tp", scatter_dimension=1, tiled=True)


def solution(mesh):
    in_specs = (
        P("seq", "tp"),
        P(None, "tp"),
        P(None, "tp"),
        P(None, "tp"),
        P("tp", None),
        P("seq", None, "tp"),
        P("seq", None, "tp"),
        P(),
        P("seq", None),
    )
    out_specs = P("seq", "tp")
    return jax.shard_map(
        on_device, mesh=mesh, in_specs=in_specs, out_specs=out_specs, check_vma=False
    )
```

profile of v0, /device:TPU:8, one launch (start us, length us, event | category | flops | bytes accessed | tf_op | source)
XLA Modules:
  0.0 615.8 jit_solution(7555049823054470965)
XLA Ops:
  9.8 57.1 %all-gather.11.cloned.1.call-done = bf16[512,4096]{1,0:T(8,128)(2,1)} async-done(((bf16[512,2048]{1,0:T(8,128)(2,1)}), bf16[512,4096]{1,0:T(8,128)(2,1)}) %all-gather.11.cloned.1.call-update) | async-done | bytes 4194320 | tf_op jit(solution)/shard_map/all_gather | solution.py:58
  66.8 5.9 multiply_reduce_fusion.1
  74.2 6.6 %convolution_convert_fusion.1 = bf16[512,512]{1,0:T(8,128)(2,1)} fusion(bf16[512,4096]{1,0:T(8,128)(2,1)} %all-gather.11.cloned.1.call-done, bf16[4096,512]{1,0:T(8,128)(2,1)} %param.12), kind=kOutput, calls=%fused_computation.30 | convolution fusion | flops 2147745792 | bytes 8912896 | tf_op jit(solution)/shard_map/dot_general | solution.py:61
  82.3 19.2 %all-gather.4 = s32[16,16,2]{1,2,0:T(2,128)S(1)} all-gather(s32[1,16,2]{1,2,0:T(2,128)S(1)} %bitcast.60), channel_id=2, replica_groups=mesh['seq'=16,'tp'=2] {'seq'}, dimensions={0}, use_global_device_ids=true | all-gather | bytes 2176 | tf_op jit(solution)/shard_map/all_gather | solution.py:107
  109.8 12.9 %convolution_bitcast_fusion = f32[64,8,16,128]{3,1,2,0:T(8,128)S(1)} fusion(bf16[512,4096]{1,0:T(8,128)(2,1)} %all-gather.11.cloned.1.call-done, bf16[4096,2048]{1,0:T(8,128)(2,1)} %param.10), kind=kOutput, calls=%fused_computation.24 | convolution fusion | flops 8589934592 | bytes 25165824 | tf_op jit(solution)/shard_map/dot_general | solution.py:61
  127.0 4.1 broadcast_multiply_fusion
  134.9 13.7 %all-gather.13.cloned.1.call-done = bf16[16,512,512]{2,1,0:T(8,128)(2,1)} async-done(((bf16[1,512,512]{2,1,0:T(8,128)(2,1)}), bf16[16,512,512]{2,1,0:T(8,128)(2,1)}) %all-gather.13.cloned.1.call-update) | async-done | bytes 8388624 | tf_op jit(solution)/shard_map/all_gather | solution.py:108
  148.6 75.3 %all-gather.19.cloned.1.call-done = bf16[8192,512]{1,0:T(8,128)(2,1)} async-done(((bf16[512,512]{1,0:T(8,128)(2,1)}), bf16[8192,512]{1,0:T(8,128)(2,1)}) %all-gather.19.cloned.1.call-update) | async-done | bytes 8388624 | tf_op jit(solution)/shard_map/all_gather | solution.py:109
  224.0 2.2 constant_dynamic-slice_fusion
  228.3 2.1 copy.100
  230.4 8.6 %fusion.6 = (f32[4,2048]{1,0:T(4,128)S(1)}, f32[4,2048,512]{1,2,0:T(8,128)}) fusion(pred[2048,512]{0,1:T(8,128)(4,1)S(1)} %fusion.12, bf16[4,2048,128]{2,1,0:T(8,128)(2,1)S(1)} %bitcast.49, bf16[512,4,128]{0,2,1:T(8,128)(2,1)} %bitcast.53), kind=kOutput, calls=%fused_computation.12 | convolution fusion | flops 1086316544 | bytes 20480000 | tf_op jit(solution)/shard_map/krd,nkd->krn/dot_general | solution.py:85
  239.0 111.0 %all-gather.15.cloned.1.call-done = bf16[256,64,512]{2,1,0:T(8,128)(2,1)} async-done(((bf16[16,64,512]{2,1,0:T(8,128)(2,1)}), bf16[256,64,512]{2,1,0:T(8,128)(2,1)}) %all-gather.15.cloned.1.call-update) | async-done | bytes 16777232 | tf_op jit(solution)/shard_map/all_gather | solution.py:105
  349.9 7.8 %gather_fusion.1 = bf16[32,64,512]{2,1,0:T(8,128)(2,1)} fusion(bf16[256,64,512]{2,1,0:T(8,128)(2,1)} %all-gather.15.cloned.1.call-done, s32[1024]{0:T(1024)S(1)} %pad_clamp_fusion), kind=kCustom, calls=%fused_computation.1 | custom fusion | bytes 4194432 | tf_op jit(solution)/shard_map/gather | solution.py:118
  357.7 4.0 reshape_reshape.12
  361.7 25.6 %fusion = (f32[4,2048]{1,0:T(4,128)S(1)}, f32[4,2048,2048]{1,2,0:T(8,128)}) fusion(pred[2048]{0:T(1024)(128)(4,1)S(1)} %and.107, bf16[4,2048,128]{2,1,0:T(8,128)(2,1)S(1)} %bitcast.50, bf16[2048,4,128]{2,1,0:T(4,128)(2,1)} %reshape_reshape.12), kind=kOutput, calls=%fused_computation.5 | convolution fusion | flops 4345290752 | bytes 71337984 | tf_op jit(solution)/shard_map/krd,nkd->krn/dot_general | solution.py:85
  387.4 8.1 %fusion.7 = f32[4,2048]{1,0:T(4,128)S(1)} fusion(f32[4,2048,512]{1,2,0:T(8,128)} %get-tuple-element.45, f32[4,2048]{1,0:T(4,128)S(1)} %get-tuple-element.34, pred[2048,512]{0,1:T(8,128)(4,1)S(1)} %fusion.12), kind=kLoop, calls=%fused_computation.13 | loop fusion | flops 20963328 | bytes 17891328 | tf_op jit(solution)/shard_map/reduce_sum | solution.py:93
  395.5 10.6 %fusion.9 = f32[4,2048,128]{2,1,0:T(8,128)} fusion(bf16[512,4,128]{0,2,1:T(8,128)(2,1)S(1)} %bitcast.57, f32[4,2048,512]{1,2,0:T(8,128)} %get-tuple-element.45, f32[4,2048]{1,0:T(4,128)S(1)} %get-tuple-element.34, pred[2048,512]{0,1:T(8,128)(4,1)S(1)} %fusion.12), kind=kOutput, calls=%fused_computation.15 | convolution fusion | flops 1094713344 | bytes 22577152 | tf_op jit(solution)/shard_map/krn,nkd->krd/dot_general | solution.py:94
  406.1 71.0 %all-gather.17.cloned.1.call-done = bf16[256,64,512]{2,1,0:T(8,128)(2,1)} async-done(((bf16[16,64,512]{2,1,0:T(8,128)(2,1)}), bf16[256,64,512]{2,1,0:T(8,128)(2,1)}) %all-gather.17.cloned.1.call-update) | async-done | bytes 16777232 | tf_op jit(solution)/shard_map/all_gather | solution.py:106
  477.0 6.4 %gather_fusion.2 = bf16[32,64,512]{2,1,0:T(8,128)(2,1)S(1)} fusion(bf16[256,64,512]{2,1,0:T(8,128)(2,1)} %all-gather.17.cloned.1.call-done, s32[1024]{0:T(1024)S(1)} %pad_clamp_fusion), kind=kCustom, calls=%fused_computation.2 | custom fusion | bytes 4194432 | tf_op jit(solution)/shard_map/gather | solution.py:121
  485.5 21.6 %fusion.1 = f32[4,2048]{1,0:T(4,128)S(1)} fusion(f32[4,2048,2048]{1,2,0:T(8,128)} %get-tuple-element.43, f32[4,2048]{1,0:T(4,128)S(1)} %get-tuple-element.35, pred[2048]{0:T(1024)(128)(4,1)S(1)} %and.107), kind=kLoop, calls=%fused_computation.6 | loop fusion | flops 83877888 | bytes 67176448 | tf_op jit(solution)/shard_map/reduce_sum | solution.py:93
  507.2 30.3 %divide_convert_fusion = bf16[4,2048,128]{2,1,0:T(8,128)(2,1)} fusion(f32[4,2048,128]{2,1,0:T(8,128)} %fusion.9, f32[4,2048,2048]{1,2,0:T(8,128)} %get-tuple-element.43, f32[4,2048]{1,0:T(4,128)S(1)} %get-tuple-element.35, pred[2048]{0:T(1024)(128)(4,1)S(1)} %and.107, bf16[2048,4,128]{2,1,0:T(4,128)(2,1)S(1)} %copy-done.1, ...), kind=kOutput, calls=%fused_computation.18 | convolution fusion | flops 4384096256 | bytes 75630592 | tf_op jit(solution)/shard_map/krn,nkd->krd/dot_general | solution.py:94
  537.6 2.8 copy.93
  540.3 13.9 %convolution_convert_fusion = bf16[512,4096]{1,0:T(8,128)(2,1)} fusion(bf16[512,2048]{0,1:T(8,128)(2,1)S(1)} %bitcast.55, bf16[2048,4096]{1,0:T(8,128)(2,1)} %param.13), kind=kOutput, calls=%fused_computation.17 | convolution fusion | flops 8592031744 | bytes 23068672 | tf_op jit(solution)/shard_map/dot_general | solution.py:147
  554.3 54.5 %reduce-scatter.2.cloned.1.call-done = bf16[512,2048]{1,0:T(8,128)(2,1)} async-done(((bf16[512,4096]{1,0:T(8,128)(2,1)}), bf16[512,2048]{1,0:T(8,128)(2,1)}) %reduce-scatter.2.cloned.1.call-update) | async-done | bytes 2097168 | tf_op jit(solution)/shard_map/reduce_scatter | solution.py:148
  (69 shorter events, 24.9 us)
Async XLA Ops:
  6.5 60.3 %all-gather.11.cloned.1.call-start = ((), (), s32[]{:S(2)}) async-start(), calls=%async_computation.1 | async-start | bytes 6291456 | tf_op jit(solution)/shard_map/all_gather | solution.py:58
  7.3 141.4 %all-gather.13.cloned.1.call-start = ((), (), s32[]{:S(2)}) async-start(), calls=%async_computation.2 | async-start | bytes 8912896 | tf_op jit(solution)/shard_map/all_gather | solution.py:108
  74.1 8.2 %copy-start.3 = (s32[16,2]{0,1:T(2,128)S(1)}, s32[16,2]{0,1:T(2,128)}, u32[]{:S(2)}) copy-start(s32[16,2]{0,1:T(2,128)} %param.17) | copy-start | bytes 388
  74.1 149.9 %all-gather.19.cloned.1.call-start = ((), (), s32[]{:S(2)}) async-start(), calls=%async_computation.6 | async-start | bytes 8912896 | tf_op jit(solution)/shard_map/all_gather | solution.py:109
  80.8 269.1 %all-gather.15.cloned.1.call-start = ((), (), s32[]{:S(2)}) async-start(), calls=%async_computation.4 | async-start | bytes 17825792 | tf_op jit(solution)/shard_map/all_gather | solution.py:105
  81.4 395.7 %all-gather.17.cloned.1.call-start = ((), (), s32[]{:S(2)}) async-start(), calls=%async_computation.5 | async-start | bytes 17825792 | tf_op jit(solution)/shard_map/all_gather | solution.py:106
  82.0 526.8 %reduce-scatter.2.cloned.1.call-start = ((), (), s32[]{:S(2)}) async-start(), calls=%async_computation.3 | async-start | bytes 6291456 | tf_op jit(solution)/shard_map/reduce_scatter | solution.py:148
  123.6 2.0 copy-start
  387.4 8.1 %copy-start.2 = (bf16[1,512,512]{1,2,0:T(8,128)(2,1)S(1)}, bf16[1,512,512]{1,2,0:T(8,128)(2,1)}, u32[]{:S(2)}) copy-start(bf16[1,512,512]{1,2,0:T(8,128)(2,1)} %copy.100) | copy-start | bytes 1572868
  485.5 21.7 %copy-start.1 = (bf16[2048,4,128]{2,1,0:T(4,128)(2,1)S(1)}, bf16[2048,4,128]{2,1,0:T(4,128)(2,1)}, u32[]{:S(2)}) copy-start(bf16[2048,4,128]{2,1,0:T(4,128)(2,1)} %reshape_reshape.13) | copy-start | bytes 6291460
Sparse Core Ops, SparseCore 0:
  8.9 57.8 all-gather.10
  74.2 74.3 all-gather.12
  150.8 73.1 all-gather.18
  226.0 123.8 all-gather.14
  351.9 125.0 all-gather.16
  554.4 54.3 reduce-scatter.1
where the time goes:
time: 622 us; the launch traced here: 616 us
  waiting for transfers between devices  384 us (62%)
  matrix products  114 us (18%)
  other arithmetic  44.7 us (7%)
  local copies, waits for them, and re-layouts  37.3 us (6%)
  blocking collectives  19.2 us (3%)
  between operations  15.7 us (3%)
    all_gather x1, waiting for transfers between devices, on_device(): piece_keys = lax.all_gather(cache_keys[None], 'seq', axis=0, tiled=True)  111 us
    all_gather x1, waiting for transfers between devices, on_device(): lax.all_gather(fresh_values[None], 'seq', axis=0, tiled=True)  75.3 us
    all_gather x1, waiting for transfers between devices, on_device(): piece_values = lax.all_gather(cache_values[None], 'seq', axis=0, tiled=True)  71 us
    all_gather x1, waiting for transfers between devices, on_device(): piece = lax.all_gather(hidden, 'tp', axis=1, tiled=True)  57.1 us
    reduce_scatter x1, waiting for transfers between devices, on_device(): lax.psum_scatter(partial_out.astype(jnp.bfloat16), 'tp', scatter_dimensio...  54.5 us
    dot_general x2, matrix products, attend(): jnp.einsum('krn,nkd->krd', weights.astype(jnp.bfloat16), values, preferre...  40.9 us
    dot_general x2, matrix products, attend(): jnp.einsum('krd,nkd->krn', grouped, keys, preferred_element_type=jnp.floa...  34.3 us
    reduce_sum x2, other arithmetic, attend(): total = total * rescale + jnp.sum(weights, axis=-1)  29.7 us
  transfers between devices with their start and end apart: 6, of which 6 were waited for; matrix products, arithmetic and copies ran while one was open for 18% of the time, Pallas kernels for 0%

commit v1 on v0

v1 whole, which is shorter than its diff:
```python
import math

import jax
import jax.numpy as jnp
from jax import lax
from jax.experimental import pallas as pl
from jax.experimental.pallas import tpu as pltpu
from jax.sharding import PartitionSpec as P

HD = 128
NEW = 512
CTX = 2048
ROPE_BASE = 1000000.0
masked_score = -1e30
VMEM_LIMIT = 56 * 1024 * 1024
BF16 = jnp.bfloat16
F32 = jnp.float32


def params(count):
    return pltpu.CompilerParams(
        dimension_semantics=("arbitrary",) * count, vmem_limit_bytes=VMEM_LIMIT
    )


def pick_blocks(page_table, cache_keys, cache_values, head, seq, per_peer):
    blocks, block_len, _ = cache_keys.shape

    def body(table, keys, values, out, index, sem):
        for slot in range(seq * per_peer):
            index[slot] = 0
        counts = index.at[pl.ds(seq * per_peer, seq)]
        for r in range(seq):
            counts[r] = 0

        def place(b, carry):
            request = table[b, 0]
            taken = counts[request]
            index[request * per_peer + jnp.minimum(taken, per_peer - 1)] = b
            counts[request] = taken + 1
            return carry

        lax.fori_loop(0, blocks, place, 0)
        for r in range(seq):
            for k in range(per_peer):
                b = index[r * per_peer + k]
                for which, source in enumerate((keys, values)):
                    pltpu.make_async_copy(
                        source.at[b, :, pl.ds(head * HD, HD)],
                        out.at[r, which, pl.ds(k * block_len, block_len), :],
                        sem,
                    ).start()
        pltpu.make_async_copy(out, out, sem).wait()

    return pl.pallas_call(
        body,
        in_specs=[
            pl.BlockSpec(memory_space=pltpu.SMEM),
            pl.BlockSpec(memory_space=pl.ANY),
            pl.BlockSpec(memory_space=pl.ANY),
        ],
        out_specs=pl.BlockSpec(memory_space=pl.ANY),
        out_shape=jax.ShapeDtypeStruct((seq, 2, per_peer * block_len, HD), BF16),
        scratch_shapes=[pltpu.SMEM((seq * per_peer + seq,), jnp.int32), pltpu.SemaphoreType.DMA],
        name="pick_blocks",
    )(page_table, cache_keys, cache_values)


def project_own(row_block, x, weight):
    tokens, depth = x.shape
    width = weight.shape[1]
    step = min(512, width)

    def body(rows, x_ref, w_ref, o_ref):
        o_ref[...] = jnp.dot(x_ref[...], w_ref[...], preferred_element_type=F32)

    return pl.pallas_call(
        body,
        grid_spec=pltpu.PrefetchScalarGridSpec(
            num_scalar_prefetch=1,
            grid=(width // step,),
            in_specs=[
                pl.BlockSpec((tokens, depth), lambda n, rows: (0, 0)),
                pl.BlockSpec((depth, step), lambda n, rows: (rows[0], n)),
            ],
            out_specs=pl.BlockSpec((tokens, step), lambda n, rows: (0, n)),
        ),
        out_shape=jax.ShapeDtypeStruct((tokens, width), F32),
        compiler_params=params(1),
        name="project_own",
    )(row_block, x, weight)


def project_rest(row_blocks, pieces, weight, partial, cosine, sine, scale):
    tokens, depth = pieces[0].shape
    count = len(pieces)
    width = weight.shape[1]
    step = min(512, width)
    heads = step // HD

    def body(rows, *refs):
        x_refs = refs[:count]
        w_refs = refs[count : 2 * count]
        p_ref, c_ref, s_ref, o_ref = refs[2 * count :]
        total = p_ref[...]
        for x_ref, w_ref in zip(x_refs, w_refs):
            total = total + jnp.dot(x_ref[...], w_ref[...], preferred_element_type=F32)
        for h in range(heads):
            u = total[:, h * HD : (h + 1) * HD]
            if scale is not None:
                inverse = lax.rsqrt(jnp.mean(u * u, axis=-1, keepdims=True) + 1e-06) * scale
                u = u * inverse
                u = u * c_ref[...] + pltpu.roll(u, HD // 2, 1) * s_ref[...]
            o_ref[h] = u.astype(BF16)

    def weight_spec(i):
        return pl.BlockSpec((depth, step), lambda n, rows: (rows[i], n))

    return pl.pallas_call(
        body,
        grid_spec=pltpu.PrefetchScalarGridSpec(
            num_scalar_prefetch=1,
            grid=(width // step,),
            in_specs=[pl.BlockSpec((tokens, depth), lambda n, rows: (0, 0))] * count
            + [weight_spec(i) for i in range(count)]
            + [
                pl.BlockSpec((tokens, step), lambda n, rows: (0, n)),
                pl.BlockSpec((tokens, HD), lambda n, rows: (0, 0)),
                pl.BlockSpec((tokens, HD), lambda n, rows: (0, 0)),
            ],
            out_specs=pl.BlockSpec((heads, tokens, HD), lambda n, rows: (n, 0, 0)),
        ),
        out_shape=jax.ShapeDtypeStruct((width // HD, tokens, HD), BF16),
        compiler_params=params(1),
        name="project_rest",
    )(row_blocks, *pieces, *([weight] * count), partial, cosine, sine)


def attend(head, queries, fresh_keys, fresh_values, cached, bias, attended, group):
    heads, tokens, _ = queries.shape
    sources, _, rows, _ = cached.shape
    keys_count = sources * rows

    def body(q_ref, fk_ref, fv_ref, c_ref, b_ref, *rest):
        o_ref = rest[-1]
        q = q_ref[0]
        cached_keys = c_ref[:, 0].reshape(keys_count, HD)
        cached_values = c_ref[:, 1].reshape(keys_count, HD)
        contract = (((1,), (1,)), ((), ()))
        old = lax.dot_general(q, cached_keys, contract, preferred_element_type=F32) + b_ref[...]
        new = lax.dot_general(q, fk_ref[0], contract, preferred_element_type=F32)
        row = lax.broadcasted_iota(jnp.int32, (tokens, tokens), 0)
        col = lax.broadcasted_iota(jnp.int32, (tokens, tokens), 1)
        new = jnp.where(col <= row, new, masked_score)
        top = jnp.maximum(jnp.max(old, axis=1, keepdims=True), jnp.max(new, axis=1, keepdims=True))
        old = jnp.exp2(old - top)
        new = jnp.exp2(new - top)
        total = jnp.sum(old, axis=1, keepdims=True) + jnp.sum(new, axis=1, keepdims=True)
        mixed = jnp.dot(old.astype(BF16), cached_values, preferred_element_type=F32)
        mixed = mixed + jnp.dot(new.astype(BF16), fv_ref[0], preferred_element_type=F32)
        o_ref[...] = (mixed / total).astype(BF16)

    in_specs = [
        pl.BlockSpec((1, tokens, HD), lambda g: (head * group + g, 0, 0)),
        pl.BlockSpec((1, tokens, HD), lambda g: (head, 0, 0)),
        pl.BlockSpec((1, tokens, HD), lambda g: (head, 0, 0)),
        pl.BlockSpec(cached.shape, lambda g: (0, 0, 0, 0)),
        pl.BlockSpec((1, keys_count), lambda g: (0, 0)),
    ]
    operands = [queries, fresh_keys, fresh_values, cached, bias]
    aliases = {}
    if attended is not None:
        in_specs.append(pl.BlockSpec(memory_space=pl.ANY))
        operands.append(attended)
        aliases = {5: 0}
    return pl.pallas_call(
        body,
        grid=(group,),
        in_specs=in_specs,
        out_specs=pl.BlockSpec((tokens, HD), lambda g: (0, head * group + g)),
        out_shape=jax.ShapeDtypeStruct((tokens, heads * HD), BF16),
        input_output_aliases=aliases,
        compiler_params=params(1),
        name="attend",
    )(*operands)


def project_out(col_block, attended, weight, width, chunk, chunks, kind):
    tokens, depth = attended.shape
    rows = tokens // chunks
    step = min(512, width)
    steps = width // step

    def body(cols, x_ref, w_ref, o_ref):
        o_ref[...] = jnp.dot(x_ref[...], w_ref[...], preferred_element_type=F32).astype(kind)

    return pl.pallas_call(
        body,
        grid_spec=pltpu.PrefetchScalarGridSpec(
            num_scalar_prefetch=1,
            grid=(steps,),
            in_specs=[
                pl.BlockSpec((rows, depth), lambda n, cols: (chunk, 0)),
                pl.BlockSpec((depth, step), lambda n, cols: (0, cols[0] * steps + n)),
            ],
            out_specs=pl.BlockSpec((rows, step), lambda n, cols: (0, n)),
        ),
        out_shape=jax.ShapeDtypeStruct((rows, width), kind),
        compiler_params=params(1),
        name="project_out",
    )(col_block, attended, weight)


def rotation(length, tokens):
    half = HD // 2
    freqs = jnp.exp(jnp.arange(half, dtype=F32) * (-2.0 * math.log(ROPE_BASE) / HD))
    positions = (length + jnp.arange(tokens, dtype=jnp.int32)).astype(F32)
    angles = positions[:, None] * freqs[None, :]
    cosine = jnp.cos(angles)
    sine = jnp.sin(angles)
    return jnp.concatenate([cosine, cosine], axis=1), jnp.concatenate([-sine, sine], axis=1)


def on_device(
    hidden, w_query, w_key, w_value, w_out, cache_keys, cache_values, cached_len, page_table
):
    tokens = hidden.shape[0]
    assert tokens == NEW
    seq = lax.axis_size("seq")
    tp = lax.axis_size("tp")
    query_heads = w_query.shape[1] // HD
    kv_heads = w_key.shape[1] // HD
    group = query_heads // kv_heads
    block_len = cache_keys.shape[1]
    per_peer = max(1, CTX // block_len // seq)
    request = lax.axis_index("seq")
    rank = lax.axis_index("tp")
    length = cached_len[request]

    received = []
    for head in range(kv_heads):
        send = pick_blocks(page_table, cache_keys, cache_values, head, seq, per_peer)
        received.append(lax.all_to_all(send, "seq", 0, 0, tiled=True))
    table = lax.all_gather(page_table[None], "seq", axis=0, tiled=True)

    pieces = []
    for shift in range(1, tp):
        pairs = [(i, (i + shift) % tp) for i in range(tp)]
        pieces.append(lax.ppermute(hidden, "tp", pairs))
    own_row = jnp.reshape(rank, (1,)).astype(jnp.int32)
    rest_rows = jnp.stack([(rank - shift) % tp for shift in range(1, tp)]).astype(jnp.int32)
    cosine, sine = rotation(length, tokens)

    def project(weight, scale):
        partial = project_own(own_row, hidden, weight)
        return project_rest(rest_rows, pieces, weight, partial, cosine, sine, scale)

    queries = project(w_query, HD ** (-0.5) / math.log(2.0))
    fresh_keys = project(w_key, 1.0)
    fresh_values = project(w_value, None)

    mine = table[..., 0] == request
    before = jnp.tril(jnp.ones((mine.shape[1], mine.shape[1]), jnp.bool_), -1)
    slot = jnp.sum(mine[:, None, :] & before[None], axis=-1)
    filled = jnp.clip(length - table[..., 1] * block_len, 0, block_len)
    slots = jnp.arange(per_peer)
    here = mine[:, None, :] & (slot[:, None, :] == slots[None, :, None])
    filled = jnp.sum(jnp.where(here, filled[:, None, :], 0), axis=-1)
    bias = jnp.where(jnp.arange(block_len) < filled[..., None], 0.0, masked_score)
    bias = bias.astype(F32).reshape(1, seq * per_peer * block_len)

    attended = None
    for head in range(kv_heads):
        attended = attend(
            head, queries, fresh_keys, fresh_values, received[head], bias, attended, group
        )

    width = w_out.shape[1] // tp
    chunks = 4 if tp == 2 else 1
    arrived = []
    for chunk in range(chunks):
        for shift in range(1, tp):
            target = jnp.reshape((rank + shift) % tp, (1,)).astype(jnp.int32)
            part = project_out(target, attended, w_out, width, chunk, chunks, BF16)
            pairs = [(i, (i + shift) % tp) for i in range(tp)]
            arrived.append(lax.ppermute(part, "tp", pairs))
    own = project_out(own_row, attended, w_out, width, 0, 1, F32)
    rows = tokens // chunks
    out = []
    for chunk in range(chunks):
        total = own[chunk * rows : (chunk + 1) * rows]
        for shift in range(1, tp):
            total = total + arrived[chunk * (tp - 1) + shift - 1].astype(F32)
        out.append(total.astype(BF16))
    return jnp.concatenate(out, axis=0)


def solution(mesh):
    in_specs = (
        P("seq", "tp"),
        P(None, "tp"),
        P(None, "tp"),
        P(None, "tp"),
        P("tp", None),
        P("seq", None, "tp"),
        P("seq", None, "tp"),
        P(),
        P("seq", None),
    )
    out_specs = P("seq", "tp")
    return jax.shard_map(
        on_device, mesh=mesh, in_specs=in_specs, out_specs=out_specs, check_vma=False
    )
```

time: 622 us -> 375 us (0.60)
  waiting for transfers between devices: 384 us -> 34.7 us
  Pallas kernels: 0 us -> 274 us
  matrix products: 114 us -> 0 us
  other arithmetic: 44.7 us -> 8.44 us
  local copies, waits for them, and re-layouts: 37.3 us -> 3.69 us
  starting transfers between devices: 0.2 us -> 30.1 us
  between operations: 15.7 us -> 0.17 us
    all_gather x5 -> x0, waiting for transfers between devices: 328 us -> none  [the longest x1 111 us: on_device(): piece_keys = lax.all_gather(cache_keys[None], 'seq', axis=0, tiled=True)]
    pallas_call x0 -> x19, Pallas kernels: none -> 274 us  [the longest x4 136 us: pick_blocks(): pl.pallas_call(body, in_specs=[pl.BlockSpec(memory_space=pltpu.SMEM), pl....]
    dot_general x8 -> x0, matrix products: 114 us -> none  [the longest x2 40.9 us: attend(): jnp.einsum('krn,nkd->krd', weights.astype(jnp.bfloat16), values, preferre...]
    reduce_scatter x1 -> x0, waiting for transfers between devices: 54.5 us -> none  [on_device(): lax.psum_scatter(partial_out.astype(jnp.bfloat16), 'tp', scatter_dimensio...]
    ppermute x0 -> x5, waiting for transfers between devices: none -> 34.7 us  [the longest x4 34.7 us: on_device(): arrived.append(lax.ppermute(part, 'tp', pairs))]
    reduce_sum x5 -> x2, other arithmetic: 31.6 us -> 0.47 us  [the longest x1 0.35 us: on_device(): slot = jnp.sum(mine[:, None, :] & before[None], axis=-1)]
    all_to_all x0 -> x4, starting transfers between devices: none -> 24.5 us  [on_device(): received.append(lax.all_to_all(send, 'seq', 0, 0, tiled=True))]
    gather x4 -> x0, local copies, waits for them, and re-layouts: 17.2 us -> none  [the longest x1 7.77 us: on_device(): piece_keys.reshape(block_count, block_len, width_kv)[picked]]
  transfers between devices with their start and end apart: 6 -> 9, of which waited for: 6 -> 4; matrix products, arithmetic and copies ran while one was open for 18% -> 1% of each run, Pallas kernels for 0% -> 54%
where the time goes in v1:
time: 375 us; the launch traced here: 370 us
  Pallas kernels  274 us (73%)
  waiting for transfers between devices  34.7 us (9%)
  starting transfers between devices  30.1 us (8%)
  blocking collectives  18.6 us (5%)
  other arithmetic  8.44 us (2%)
    pallas_call x4, Pallas kernels, pick_blocks(): pl.pallas_call(body, in_specs=[pl.BlockSpec(memory_space=pltpu.SMEM), pl....  136 us
    pallas_call x4, Pallas kernels, attend(): pl.pallas_call(body, grid=(group,), in_specs=in_specs, out_specs=pl.Block...  63.1 us
    ppermute x4, waiting for transfers between devices, on_device(): arrived.append(lax.ppermute(part, 'tp', pairs))  34.7 us
    pallas_call x5, Pallas kernels, project_out(): pl.pallas_call(body, grid_spec=pltpu.PrefetchScalarGridSpec(num_scalar_pr...  32.3 us
    pallas_call x3, Pallas kernels, project_rest(): pl.pallas_call(body, grid_spec=pltpu.PrefetchScalarGridSpec(num_scalar_pr...  24.7 us
    all_to_all x4, starting transfers between devices, on_device(): received.append(lax.all_to_all(send, 'seq', 0, 0, tiled=True))  24.5 us
    all_gather x1, blocking collectives, on_device(): table = lax.all_gather(page_table[None], 'seq', axis=0, tiled=True)  18.6 us
    pallas_call x3, Pallas kernels, project_own(): pl.pallas_call(body, grid_spec=pltpu.PrefetchScalarGridSpec(num_scalar_pr...  18.2 us
  transfers between devices with their start and end apart: 9, of which 4 were waited for; matrix products, arithmetic and copies ran while one was open for 1% of the time, Pallas kernels for 54%

profile of v1, /device:TPU:8, one launch (start us, length us, event | category | flops | bytes accessed | tf_op | source)
XLA Modules:
  0.0 369.6 jit_solution(5525676113990311765)
XLA Ops:
  1.3 33.9 %pick_blocks.7 = bf16[16,2,128,128]{3,2,1,0:T(8,128)(2,1)} custom-call(s32[16,2]{1,0:T(8,128)} %copy.26.table, bf16[16,64,512]{2,1,0:T(8,128)(2,1)} %keys.7, bf16[16,64,512]{2,1,0:T(8,128)(2,1)} %values.7), custom_call_target="tpu_custom_call" | custom-call | tf_op jit(solution)/shard_map/pick_blocks/pallas_call | solution.py:55
  35.3 6.3 %all-to-all-start.3 = ((bf16[16,2,128,128]{3,2,1,0:T(8,128)(2,1)}), bf16[16,2,128,128]{3,2,1,0:T(8,128)(2,1)S(1)}, u32[]{:S(2)}, u32[]{:S(2)}) async-start(bf16[16,2,128,128]{3,2,1,0:T(8,128)(2,1)} %pick_blocks.7), calls=%async_computation.3 | async-start | bytes 2097152 | tf_op jit(solution)/shard_map/all_to_all | solution.py:243
  41.6 33.9 %pick_blocks.6 = bf16[16,2,128,128]{3,2,1,0:T(8,128)(2,1)} custom-call(s32[16,2]{1,0:T(8,128)} %copy.26.table, bf16[16,64,512]{2,1,0:T(8,128)(2,1)} %keys.7, bf16[16,64,512]{2,1,0:T(8,128)(2,1)} %values.7), custom_call_target="tpu_custom_call" | custom-call | tf_op jit(solution)/shard_map/pick_blocks/pallas_call | solution.py:55
  76.5 6.1 %all-to-all-start.2 = ((bf16[16,2,128,128]{3,2,1,0:T(8,128)(2,1)}), bf16[16,2,128,128]{3,2,1,0:T(8,128)(2,1)S(1)}, u32[]{:S(2)}, u32[]{:S(2)}) async-start(bf16[16,2,128,128]{3,2,1,0:T(8,128)(2,1)} %pick_blocks.6), calls=%async_computation.2 | async-start | bytes 2097152 | tf_op jit(solution)/shard_map/all_to_all | solution.py:243
  82.6 33.9 %pick_blocks.5 = bf16[16,2,128,128]{3,2,1,0:T(8,128)(2,1)} custom-call(s32[16,2]{1,0:T(8,128)} %copy.26.table, bf16[16,64,512]{2,1,0:T(8,128)(2,1)} %keys.7, bf16[16,64,512]{2,1,0:T(8,128)(2,1)} %values.7), custom_call_target="tpu_custom_call" | custom-call | tf_op jit(solution)/shard_map/pick_blocks/pallas_call | solution.py:55
  116.6 6.0 %all-to-all-start.1 = ((bf16[16,2,128,128]{3,2,1,0:T(8,128)(2,1)}), bf16[16,2,128,128]{3,2,1,0:T(8,128)(2,1)}, u32[]{:S(2)}, u32[]{:S(2)}) async-start(bf16[16,2,128,128]{3,2,1,0:T(8,128)(2,1)} %pick_blocks.5), calls=%async_computation.1 | async-start | bytes 2097152 | tf_op jit(solution)/shard_map/all_to_all | solution.py:243
  124.2 33.9 %pick_blocks.4 = bf16[16,2,128,128]{3,2,1,0:T(8,128)(2,1)} custom-call(s32[16,2]{1,0:T(8,128)} %copy.26.table, bf16[16,64,512]{2,1,0:T(8,128)(2,1)} %keys.7, bf16[16,64,512]{2,1,0:T(8,128)(2,1)} %values.7), custom_call_target="tpu_custom_call" | custom-call | tf_op jit(solution)/shard_map/pick_blocks/pallas_call | solution.py:55
  158.2 6.0 %all-to-all-start = ((bf16[16,2,128,128]{3,2,1,0:T(8,128)(2,1)}), bf16[16,2,128,128]{3,2,1,0:T(8,128)(2,1)}, u32[]{:S(2)}, u32[]{:S(2)}) async-start(bf16[16,2,128,128]{3,2,1,0:T(8,128)(2,1)} %pick_blocks.4), calls=%async_computation | async-start | bytes 2097152 | tf_op jit(solution)/shard_map/all_to_all | solution.py:243
  164.2 9.2 %project_own.3.refs_2_ = f32[512,2048]{1,0:T(8,128)} custom-call(s32[1]{0:T(128)} %bitcast.rows.cols, bf16[512,2048]{1,0:T(8,128)(2,1)} %x_ref.5, bf16[4096,2048]{1,0:T(8,128)(2,1)} %refs_1_.3), custom_call_target="tpu_custom_call" | custom-call | tf_op jit(solution)/shard_map/project_own/pallas_call | solution.py:77
  183.0 18.6 %all-gather.1 = s32[16,16,2]{1,2,0:T(2,128)S(1)} all-gather(s32[1,16,2]{1,2,0:T(2,128)S(1)} %bitcast.11), channel_id=2, replica_groups=mesh['seq'=16,'tp'=2] {'seq'}, dimensions={0}, use_global_device_ids=true | all-gather | bytes 2176 | tf_op jit(solution)/shard_map/all_gather | solution.py:244
  206.3 14.1 %project_rest.3.q_ref = bf16[16,512,128]{2,1,0:T(8,128)(2,1)} custom-call(s32[1]{0:T(128)} %bitcast.1.rows, bf16[512,2048]{1,0:T(8,128)(2,1)} %collective-permute-done.refs_0_, bf16[4096,2048]{1,0:T(8,128)(2,1)} %refs_1_.3, f32[512,2048]{1,0:T(8,128)} %project_own.3.refs_2_, f32[512,128]{1,0:T(8,128)} %get-tuple-element.14.refs_3_, ...), custom_call_target="tpu_custom_call" | custom-call | tf_op jit(solution)/shard_map/project_rest/pallas_call | solution.py:119
  220.4 6.0 %project_rest.4.fk_ref = bf16[4,512,128]{2,1,0:T(8,128)(2,1)} custom-call(s32[1]{0:T(128)} %bitcast.1.rows, bf16[512,2048]{1,0:T(8,128)(2,1)} %collective-permute-done.refs_0_, bf16[4096,512]{1,0:T(8,128)(2,1)} %refs_1_.4, f32[512,512]{1,0:T(8,128)} %project_own.4.refs_2_, f32[512,128]{1,0:T(8,128)} %get-tuple-element.14.refs_3_, ...), custom_call_target="tpu_custom_call" | custom-call | tf_op jit(solution)/shard_map/project_rest/pallas_call | solution.py:119
  231.1 15.7 %attend.4.rest_0_ = bf16[512,2048]{1,0:T(8,128)(2,1)} custom-call(bf16[16,512,128]{2,1,0:T(8,128)(2,1)} %project_rest.3.q_ref, bf16[4,512,128]{2,1,0:T(8,128)(2,1)} %project_rest.4.fk_ref, bf16[4,512,128]{2,1,0:T(8,128)(2,1)} %project_rest.5.fv_ref, bf16[16,2,128,128]{3,2,1,0:T(8,128)(2,1)} %copy-done.2, f32[1,2048]{1,0:T(1,128)} %select_n.44.b_ref), custom_call_target="tpu_custom_call" | custom-call | tf_op jit(solution)/shard_map/attend/pallas_call | solution.py:176
  246.8 15.7 %attend.5.rest_0_ = bf16[512,2048]{1,0:T(8,128)(2,1)} custom-call(bf16[16,512,128]{2,1,0:T(8,128)(2,1)} %project_rest.3.q_ref, bf16[4,512,128]{2,1,0:T(8,128)(2,1)} %project_rest.4.fk_ref, bf16[4,512,128]{2,1,0:T(8,128)(2,1)} %project_rest.5.fv_ref, bf16[16,2,128,128]{3,2,1,0:T(8,128)(2,1)} %copy-done.1, ...), custom_call_target="tpu_custom_call", output_to_operand_aliasing={{}: (5, {})} | custom-call | tf_op jit(solution)/shard_map/attend/pallas_call | solution.py:176
  262.5 15.7 %attend.6.rest_0_ = bf16[512,2048]{1,0:T(8,128)(2,1)} custom-call(bf16[16,512,128]{2,1,0:T(8,128)(2,1)} %project_rest.3.q_ref, bf16[4,512,128]{2,1,0:T(8,128)(2,1)} %project_rest.4.fk_ref, bf16[4,512,128]{2,1,0:T(8,128)(2,1)} %project_rest.5.fv_ref, bf16[16,2,128,128]{3,2,1,0:T(8,128)(2,1)} %all-to-all-done.1.c_ref, ...), custom_call_target="tpu_custom_call", output_to_operand_aliasing={{}: (5, {})} | custom-call | tf_op jit(solution)/shard_map/attend/pallas_call | solution.py:176
  278.2 15.9 %attend.7.x_ref = bf16[512,2048]{1,0:T(8,128)(2,1)} custom-call(bf16[16,512,128]{2,1,0:T(8,128)(2,1)} %project_rest.3.q_ref, bf16[4,512,128]{2,1,0:T(8,128)(2,1)} %project_rest.4.fk_ref, bf16[4,512,128]{2,1,0:T(8,128)(2,1)} %project_rest.5.fv_ref, bf16[16,2,128,128]{3,2,1,0:T(8,128)(2,1)} %all-to-all-done.c_ref, ...), custom_call_target="tpu_custom_call", output_to_operand_aliasing={{}: (5, {})} | custom-call | tf_op jit(solution)/shard_map/attend/pallas_call | solution.py:176
  294.1 5.7 %project_out.6 = bf16[128,2048]{1,0:T(8,128)(2,1)} custom-call(s32[1]{0:T(128)} %bitcast.6.cols, bf16[512,2048]{1,0:T(8,128)(2,1)} %attend.7.x_ref, bf16[2048,4096]{1,0:T(8,128)(2,1)} %w_ref.15), custom_call_target="tpu_custom_call" | custom-call | tf_op jit(solution)/shard_map/project_out/pallas_call | solution.py:197
  299.9 5.8 %project_out.7 = bf16[128,2048]{1,0:T(8,128)(2,1)} custom-call(s32[1]{0:T(128)} %bitcast.6.cols, bf16[512,2048]{1,0:T(8,128)(2,1)} %attend.7.x_ref, bf16[2048,4096]{1,0:T(8,128)(2,1)} %w_ref.15), custom_call_target="tpu_custom_call" | custom-call | tf_op jit(solution)/shard_map/project_out/pallas_call | solution.py:197
  305.6 5.8 %project_out.8 = bf16[128,2048]{1,0:T(8,128)(2,1)} custom-call(s32[1]{0:T(128)} %bitcast.6.cols, bf16[512,2048]{1,0:T(8,128)(2,1)} %attend.7.x_ref, bf16[2048,4096]{1,0:T(8,128)(2,1)} %w_ref.15), custom_call_target="tpu_custom_call" | custom-call | tf_op jit(solution)/shard_map/project_out/pallas_call | solution.py:197
  311.4 5.9 %project_out.9 = bf16[128,2048]{1,0:T(8,128)(2,1)} custom-call(s32[1]{0:T(128)} %bitcast.6.cols, bf16[512,2048]{1,0:T(8,128)(2,1)} %attend.7.x_ref, bf16[2048,4096]{1,0:T(8,128)(2,1)} %w_ref.15), custom_call_target="tpu_custom_call" | custom-call | tf_op jit(solution)/shard_map/project_out/pallas_call | solution.py:197
  321.4 9.1 %project_out.5 = f32[512,2048]{1,0:T(8,128)} custom-call(s32[1]{0:T(128)} %bitcast.rows.cols, bf16[512,2048]{1,0:T(8,128)(2,1)} %attend.7.x_ref, bf16[2048,4096]{1,0:T(8,128)(2,1)} %w_ref.15), custom_call_target="tpu_custom_call" | custom-call | tf_op jit(solution)/shard_map/project_out/pallas_call | solution.py:197
  332.1 11.2 %collective-permute-done.2 = bf16[128,2048]{1,0:T(8,128)(2,1)S(1)} collective-permute-done((bf16[128,2048]{1,0:T(8,128)(2,1)S(1)}, bf16[128,2048]{1,0:T(8,128)(2,1)S(1)}, u32[]{:S(2)}, u32[]{:S(2)}) %collective-permute-start.2) | collective-permute-done | bytes 524320 | tf_op jit(solution)/shard_map/ppermute | solution.py:286
  343.3 11.2 %collective-permute-done.3 = bf16[128,2048]{1,0:T(8,128)(2,1)S(1)} collective-permute-done((bf16[128,2048]{1,0:T(8,128)(2,1)S(1)}, bf16[128,2048]{1,0:T(8,128)(2,1)S(1)}, u32[]{:S(2)}, u32[]{:S(2)}) %collective-permute-start.3) | collective-permute-done | bytes 524320 | tf_op jit(solution)/shard_map/ppermute | solution.py:286
  354.5 10.6 %collective-permute-done.4 = bf16[128,2048]{1,0:T(8,128)(2,1)S(1)} collective-permute-done((bf16[128,2048]{1,0:T(8,128)(2,1)}, bf16[128,2048]{1,0:T(8,128)(2,1)S(1)}, u32[]{:S(2)}, u32[]{:S(2)}) %collective-permute-start.4) | collective-permute-done | bytes 524320 | tf_op jit(solution)/shard_map/ppermute | solution.py:286
  (47 shorter events, 33.0 us)
Async XLA Ops:
  35.3 40.2 %all-to-all-start.3 = ((bf16[16,2,128,128]{3,2,1,0:T(8,128)(2,1)}), bf16[16,2,128,128]{3,2,1,0:T(8,128)(2,1)S(1)}, u32[]{:S(2)}, u32[]{:S(2)}) async-start(bf16[16,2,128,128]{3,2,1,0:T(8,128)(2,1)} %pick_blocks.7), calls=%async_computation.3 | async-start | bytes 2097152 | tf_op jit(solution)/shard_map/all_to_all | solution.py:243
  75.5 47.1 %copy-start = (bf16[512,2048]{1,0:T(8,128)(2,1)S(1)}, bf16[512,2048]{1,0:T(8,128)(2,1)}, u32[]{:S(2)}) copy-start(bf16[512,2048]{1,0:T(8,128)(2,1)} %x_ref.5) | copy-start | bytes 6291460
  75.5 1.0 copy-start.2
  76.5 40.1 %all-to-all-start.2 = ((bf16[16,2,128,128]{3,2,1,0:T(8,128)(2,1)}), bf16[16,2,128,128]{3,2,1,0:T(8,128)(2,1)S(1)}, u32[]{:S(2)}, u32[]{:S(2)}) async-start(bf16[16,2,128,128]{3,2,1,0:T(8,128)(2,1)} %pick_blocks.6), calls=%async_computation.2 | async-start | bytes 2097152 | tf_op jit(solution)/shard_map/all_to_all | solution.py:243
  116.6 56.8 %copy-start.1 = (bf16[16,2,128,128]{3,2,1,0:T(8,128)(2,1)}, bf16[16,2,128,128]{3,2,1,0:T(8,128)(2,1)S(1)}, u32[]{:S(2)}) copy-start(bf16[16,2,128,128]{3,2,1,0:T(8,128)(2,1)S(1)} %all-to-all-done.2.c_ref) | copy-start | bytes 3145732
  116.6 41.6 %all-to-all-start.1 = ((bf16[16,2,128,128]{3,2,1,0:T(8,128)(2,1)}), bf16[16,2,128,128]{3,2,1,0:T(8,128)(2,1)}, u32[]{:S(2)}, u32[]{:S(2)}) async-start(bf16[16,2,128,128]{3,2,1,0:T(8,128)(2,1)} %pick_blocks.5), calls=%async_computation.1 | async-start | bytes 2097152 | tf_op jit(solution)/shard_map/all_to_all | solution.py:243
  122.6 83.7 %collective-permute-start = (bf16[512,2048]{1,0:T(8,128)(2,1)S(1)}, bf16[512,2048]{1,0:T(8,128)(2,1)}, u32[]{:S(2)}, u32[]{:S(2)}) collective-permute-start(bf16[512,2048]{1,0:T(8,128)(2,1)S(1)} %copy-done), channel_id=1, source_target_pairs={{0,1},{1,0},{2,3},{3,2},{4,5},{5,4},{6,7},{7,6},{8,9},{9,8},{10,11... | collective-permute-start | bytes 6291464 | tf_op jit(solution)/shard_map/ppermute | solution.py:249
  158.2 120.0 %all-to-all-start = ((bf16[16,2,128,128]{3,2,1,0:T(8,128)(2,1)}), bf16[16,2,128,128]{3,2,1,0:T(8,128)(2,1)}, u32[]{:S(2)}, u32[]{:S(2)}) async-start(bf16[16,2,128,128]{3,2,1,0:T(8,128)(2,1)} %pick_blocks.4), calls=%async_computation | async-start | bytes 2097152 | tf_op jit(solution)/shard_map/all_to_all | solution.py:243
  177.9 4.5 %copy-start.7 = (s32[16]{0:T(128)S(1)}, s32[16]{0:T(128)}, u32[]{:S(2)}) copy-start(s32[16]{0:T(128)} %param.16) | copy-start | bytes 196
  177.9 5.1 %copy-start.6 = (s32[16,2]{0,1:T(2,128)S(1)}, s32[16,2]{0,1:T(2,128)}, u32[]{:S(2)}) copy-start(s32[16,2]{0,1:T(2,128)} %param.17) | copy-start | bytes 388
  311.4 5.9 %copy-start.5 = (bf16[128,2048]{1,0:T(8,128)(2,1)S(1)}, bf16[128,2048]{1,0:T(8,128)(2,1)}, u32[]{:S(2)}) copy-start(bf16[128,2048]{1,0:T(8,128)(2,1)} %project_out.6) | copy-start | bytes 1572868
  311.4 6.4 %copy-start.4 = (bf16[128,2048]{1,0:T(8,128)(2,1)S(1)}, bf16[128,2048]{1,0:T(8,128)(2,1)}, u32[]{:S(2)}) copy-start(bf16[128,2048]{1,0:T(8,128)(2,1)} %project_out.7) | copy-start | bytes 1572868
  311.4 8.0 %copy-start.3 = (bf16[128,2048]{1,0:T(8,128)(2,1)S(1)}, bf16[128,2048]{1,0:T(8,128)(2,1)}, u32[]{:S(2)}) copy-start(bf16[128,2048]{1,0:T(8,128)(2,1)} %project_out.8) | copy-start | bytes 1572868
  317.3 14.7 %collective-permute-start.1 = (bf16[128,2048]{1,0:T(8,128)(2,1)S(1)}, bf16[128,2048]{1,0:T(8,128)(2,1)S(1)}, u32[]{:S(2)}, u32[]{:S(2)}) collective-permute-start(bf16[128,2048]{1,0:T(8,128)(2,1)S(1)} %copy-done.5), channel_id=1, source_target_pairs={{0,1},{1,0},{2,3},{3,2},{4,5},{5,4},{6,7},{7,6},{8,9},{9,8},{10,11... | collective-permute-start | bytes 1572872 | tf_op jit(solution)/shard_map/ppermute | solution.py:286
  317.8 25.5 %collective-permute-start.2 = (bf16[128,2048]{1,0:T(8,128)(2,1)S(1)}, bf16[128,2048]{1,0:T(8,128)(2,1)S(1)}, u32[]{:S(2)}, u32[]{:S(2)}) collective-permute-start(bf16[128,2048]{1,0:T(8,128)(2,1)S(1)} %copy-done.4), channel_id=1, source_target_pairs={{0,1},{1,0},{2,3},{3,2},{4,5},{5,4},{6,7},{7,6},{8,9},{9,8},{10,11... | collective-permute-start | bytes 1572872 | tf_op jit(solution)/shard_map/ppermute | solution.py:286
  319.4 35.2 %collective-permute-start.3 = (bf16[128,2048]{1,0:T(8,128)(2,1)S(1)}, bf16[128,2048]{1,0:T(8,128)(2,1)S(1)}, u32[]{:S(2)}, u32[]{:S(2)}) collective-permute-start(bf16[128,2048]{1,0:T(8,128)(2,1)S(1)} %copy-done.3), channel_id=1, source_target_pairs={{0,1},{1,0},{2,3},{3,2},{4,5},{5,4},{6,7},{7,6},{8,9},{9,8},{10,11... | collective-permute-start | bytes 1572872 | tf_op jit(solution)/shard_map/ppermute | solution.py:286
  319.9 45.3 %collective-permute-start.4 = (bf16[128,2048]{1,0:T(8,128)(2,1)}, bf16[128,2048]{1,0:T(8,128)(2,1)S(1)}, u32[]{:S(2)}, u32[]{:S(2)}) collective-permute-start(bf16[128,2048]{1,0:T(8,128)(2,1)} %project_out.9), channel_id=1, source_target_pairs={{0,1},{1,0},{2,3},{3,2},{4,5},{5,4},{6,7},{7,6},{8,9},{9,8},{10,11... | collective-permute-start | bytes 1572872 | tf_op jit(solution)/shard_map/ppermute | solution.py:286

commit v2 on v1

v2 whole, which is shorter than its diff:
```python
import math

import jax
import jax.numpy as jnp
from jax import lax
from jax.experimental import pallas as pl
from jax.experimental.pallas import tpu as pltpu
from jax.sharding import PartitionSpec as P

HD = 128
NEW = 512
CTX = 2048
ROPE_BASE = 1000000.0
masked_score = -1e30
VMEM_LIMIT = 56 * 1024 * 1024
BF16 = jnp.bfloat16
F32 = jnp.float32


def params(count):
    return pltpu.CompilerParams(
        dimension_semantics=("arbitrary",) * count, vmem_limit_bytes=VMEM_LIMIT
    )


def cost(flops, moved, exps=0):
    return pl.CostEstimate(flops=flops, bytes_accessed=moved, transcendentals=exps)


def pick_blocks(page_table, cached_len, cache_keys, cache_values, first, count, seq, per_peer):
    masked = first == 0
    width = count * HD
    blocks, block_len, _ = cache_keys.shape
    span = per_peer * block_len
    rows = 2 * span + (16 if masked else 0)

    def body(table, lengths, keys, values, out, index):
        for slot in range(seq * per_peer):
            index[slot] = 0
        tally = seq * per_peer
        for r in range(seq):
            index[tally + r] = 0

        def place(b, carry):
            r = table[b, 0]
            taken = index[tally + r]
            index[r * per_peer + jnp.minimum(taken, per_peer - 1)] = b
            index[tally + r] = taken + 1
            return carry

        lax.fori_loop(0, blocks, place, 0)
        lane = lax.broadcasted_iota(jnp.int32, (16, width), 1)
        for r in range(seq):
            mask = jnp.full((16, width), masked_score, F32)
            for k in range(per_peer):
                b = index[r * per_peer + k]
                out[r, k * block_len : (k + 1) * block_len, :] = keys[b]
                out[r, span + k * block_len : span + (k + 1) * block_len, :] = values[b]
                if masked:
                    filled = jnp.minimum(lengths[r] - table[b, 1] * block_len, block_len)
                    filled = jnp.where(index[tally + r] > k, filled, 0)
                    inside = (lane >= k * block_len) & (lane < k * block_len + filled)
                    mask = jnp.where(inside, 0.0, mask)
            if masked:
                out[r, 2 * span :, :] = mask.astype(BF16)

    part = pl.BlockSpec((blocks, block_len, width), lambda i: (0, 0, first // count))
    return pl.pallas_call(
        body,
        grid=(1,),
        in_specs=[
            pl.BlockSpec(memory_space=pltpu.SMEM),
            pl.BlockSpec(memory_space=pltpu.SMEM),
            part,
            part,
        ],
        out_specs=pl.BlockSpec((seq, rows, width), lambda i: (0, 0, 0)),
        out_shape=jax.ShapeDtypeStruct((seq, rows, width), BF16),
        scratch_shapes=[pltpu.SMEM((seq * per_peer + seq,), jnp.int32)],
        compiler_params=params(1),
        cost_estimate=cost(0, 2 * seq * rows * width * 2),
        name="pick_blocks",
    )(page_table, cached_len, cache_keys, cache_values)


def project_own(row_block, x, weight):
    tokens, depth = x.shape
    width = weight.shape[1]
    step = min(512, width)

    def body(rows, x_ref, w_ref, o_ref):
        o_ref[...] = jnp.dot(x_ref[...], w_ref[...], preferred_element_type=F32)

    return pl.pallas_call(
        body,
        grid_spec=pltpu.PrefetchScalarGridSpec(
            num_scalar_prefetch=1,
            grid=(width // step,),
            in_specs=[
                pl.BlockSpec((tokens, depth), lambda n, rows: (0, 0)),
                pl.BlockSpec((depth, step), lambda n, rows: (rows[0], n)),
            ],
            out_specs=pl.BlockSpec((tokens, step), lambda n, rows: (0, n)),
        ),
        out_shape=jax.ShapeDtypeStruct((tokens, width), F32),
        compiler_params=params(1),
        cost_estimate=cost(2 * tokens * depth * width, depth * width * 2 + tokens * width * 4),
        name="project_own",
    )(row_block, x, weight)


def project_rest(row_blocks, half, pieces, weight, partial, cosine, sine, scale):
    tokens, depth = pieces[0].shape
    count = len(pieces)
    width = weight.shape[1]
    step = min(512, width)
    heads = step // HD

    def body(rows, *refs):
        x_refs = refs[:count]
        w_refs = refs[count : 2 * count]
        p_ref, c_ref, s_ref, o_ref = refs[2 * count :]
        total = p_ref[...]
        for x_ref, w_ref in zip(x_refs, w_refs):
            total = total + jnp.dot(x_ref[...], w_ref[...], preferred_element_type=F32)
        for h in range(heads):
            u = total[:, h * HD : (h + 1) * HD]
            if scale is not None:
                inverse = lax.rsqrt(jnp.mean(u * u, axis=-1, keepdims=True) + 1e-06) * scale
                u = u * inverse
                u = u * c_ref[...] + pltpu.roll(u, HD // 2, 1) * s_ref[...]
            o_ref[h] = u.astype(BF16)

    def weight_spec(i):
        return pl.BlockSpec((depth, step), lambda n, rows: (rows[i], n))

    return pl.pallas_call(
        body,
        grid_spec=pltpu.PrefetchScalarGridSpec(
            num_scalar_prefetch=1,
            grid=(width // step,),
            in_specs=[pl.BlockSpec((tokens, depth), lambda n, rows: (0, 0))] * count
            + [weight_spec(i) for i in range(count)]
            + [
                pl.BlockSpec((tokens, step), lambda n, rows: (half, n)),
                pl.BlockSpec((tokens, HD), lambda n, rows: (half, 0)),
                pl.BlockSpec((tokens, HD), lambda n, rows: (half, 0)),
            ],
            out_specs=pl.BlockSpec((heads, tokens, HD), lambda n, rows: (n, 0, 0)),
        ),
        out_shape=jax.ShapeDtypeStruct((width // HD, tokens, HD), BF16),
        compiler_params=params(1),
        cost_estimate=cost(
            2 * tokens * depth * count * width, depth * count * width * 2 + tokens * width * 8
        ),
        name="project_rest",
    )(row_blocks, *pieces, *([weight] * count), partial, cosine, sine)


def attend(first, count, at, group, queries, fresh_keys, fresh_values, cached, bias, attended):
    heads, tokens, _ = queries.shape
    parts = len(fresh_keys)
    sources, all_rows, _ = cached.shape
    keys_count = bias.shape[1]
    rows = keys_count // sources
    early = tokens * (parts - 1)
    tile = 128
    contract = (((1,), (1,)), ((), ()))

    def body(*refs):
        q_ref, c_ref, b_ref = refs[:3]
        key_refs = refs[3 : 3 + parts]
        value_refs = refs[3 + parts : 3 + 2 * parts]
        o_ref, old_values, new_values = refs[-3:]

        @pl.when(pl.program_id(0) % group == 0)
        def _():
            old_values[:, :HD] = c_ref[:, rows : 2 * rows].reshape(keys_count, HD)
            old_values[:, HD:] = jnp.ones((keys_count, HD), BF16)
            for i in range(parts):
                new_values[i * tokens : (i + 1) * tokens, :HD] = value_refs[i][0]
            new_values[:, HD:] = jnp.ones((tokens * parts, HD), BF16)

        cached_keys = c_ref[:, :rows].reshape(keys_count, HD)

        def product(q, keys):
            return lax.dot_general(q, keys, contract, preferred_element_type=F32)

        def scores(t):
            q = q_ref[0, t * tile : (t + 1) * tile]
            width = (t + 1) * tile
            out = [product(q, cached_keys) + b_ref[...]]
            out += [product(q, ref[0]) for ref in key_refs[:-1]]
            row = lax.broadcasted_iota(jnp.int32, (tile, width), 0) + t * tile
            col = lax.broadcasted_iota(jnp.int32, (tile, width), 1)
            out.append(jnp.where(col <= row, product(q, key_refs[-1][0, :width]), masked_score))
            return out

        ahead = scores(0)
        for t in range(tokens // tile):
            now = ahead
            if (t + 1) * tile < tokens:
                ahead = scores(t + 1)
            top = jnp.max(now[0], axis=1, keepdims=True)
            for part in now[1:]:
                top = jnp.maximum(top, jnp.max(part, axis=1, keepdims=True))
            now = [jnp.exp2(part - top).astype(BF16) for part in now]
            mixed = jnp.dot(now[0], old_values[...], preferred_element_type=F32)
            start = 0
            for part in now[1:]:
                values = new_values[start : start + part.shape[1]]
                mixed = mixed + jnp.dot(part, values, preferred_element_type=F32)
                start += part.shape[1]
            o_ref[t * tile : (t + 1) * tile] = (mixed[:, :HD] / mixed[:, HD:]).astype(BF16)

    head_spec = pl.BlockSpec((1, tokens, HD), lambda g: (first + g // group, 0, 0))
    in_specs = [
        pl.BlockSpec((1, tokens, HD), lambda g: (first * group + g, 0, 0)),
        pl.BlockSpec((sources, all_rows, HD), lambda g: (0, 0, at + g // group)),
        pl.BlockSpec((1, keys_count), lambda g: (0, 0)),
    ] + [head_spec] * (2 * parts)
    operands = [queries, cached, bias] + list(fresh_keys) + list(fresh_values)
    aliases = {}
    if attended is not None:
        aliases = {len(operands): 0}
        in_specs.append(pl.BlockSpec(memory_space=pl.ANY))
        operands.append(attended)
    pairs = count * group * tokens * (keys_count + tokens * parts)
    return pl.pallas_call(
        body,
        grid=(count * group,),
        in_specs=in_specs,
        out_specs=pl.BlockSpec((tokens, HD), lambda g: (0, first * group + g)),
        out_shape=jax.ShapeDtypeStruct((tokens, heads * HD), BF16),
        scratch_shapes=[
            pltpu.VMEM((keys_count, 2 * HD), BF16),
            pltpu.VMEM((early + tokens, 2 * HD), BF16),
        ],
        input_output_aliases=aliases,
        compiler_params=params(1),
        cost_estimate=cost(8 * pairs * HD, 4 * count * keys_count * HD, pairs),
        name="attend",
    )(*operands)


def project_out(col_block, attended, weight, width, strips, kind):
    rows, depth = attended.shape
    strip = rows // strips
    step = min(1024, width)
    steps = width // step

    def body(cols, x_ref, w_ref, *o_refs):
        total = jnp.dot(x_ref[...], w_ref[...], preferred_element_type=F32).astype(kind)
        for i in range(strips):
            o_refs[i][...] = total[i * strip : (i + 1) * strip]

    return pl.pallas_call(
        body,
        grid_spec=pltpu.PrefetchScalarGridSpec(
            num_scalar_prefetch=1,
            grid=(steps,),
            in_specs=[
                pl.BlockSpec((rows, depth), lambda n, cols: (0, 0)),
                pl.BlockSpec((depth, step), lambda n, cols: (0, cols[0] * steps + n)),
            ],
            out_specs=[pl.BlockSpec((strip, step), lambda n, cols: (0, n))] * strips,
        ),
        out_shape=[jax.ShapeDtypeStruct((strip, width), kind)] * strips,
        compiler_params=params(1),
        cost_estimate=cost(2 * rows * depth * width, depth * width * 2 + rows * width * 4),
        name="project_out",
    )(col_block, attended, weight)


def combine(own, parts, index, total_rows, out):
    rows, width = own.shape

    def body(*refs):
        total = refs[0][...]
        for ref in refs[1 : 1 + len(parts)]:
            total = total + ref[...].astype(F32)
        refs[-1][...] = total.astype(BF16)

    step = min(1024, width)
    in_specs = [pl.BlockSpec((rows, step), lambda n: (0, n))] * (1 + len(parts))
    operands = [own] + list(parts)
    aliases = {}
    if out is not None:
        aliases = {len(operands): 0}
        in_specs.append(pl.BlockSpec(memory_space=pl.ANY))
        operands.append(out)
    return pl.pallas_call(
        body,
        grid=(width // step,),
        in_specs=in_specs,
        out_specs=pl.BlockSpec((rows, step), lambda n: (index, n)),
        out_shape=jax.ShapeDtypeStruct((total_rows, width), BF16),
        input_output_aliases=aliases,
        compiler_params=params(1),
        cost_estimate=cost(0, rows * width * 8),
        name="combine",
    )(*operands)


def rotation(length, tokens):
    half = HD // 2
    freqs = jnp.exp(jnp.arange(half, dtype=F32) * (-2.0 * math.log(ROPE_BASE) / HD))
    positions = (length + jnp.arange(tokens, dtype=jnp.int32)).astype(F32)
    angles = positions[:, None] * freqs[None, :]
    cosine = jnp.cos(angles)
    sine = jnp.sin(angles)
    return jnp.concatenate([cosine, cosine], axis=1), jnp.concatenate([-sine, sine], axis=1)


def on_device(
    hidden, w_query, w_key, w_value, w_out, cache_keys, cache_values, cached_len, page_table
):
    tokens = hidden.shape[0]
    assert tokens == NEW
    seq = lax.axis_size("seq")
    tp = lax.axis_size("tp")
    query_heads = w_query.shape[1] // HD
    kv_heads = w_key.shape[1] // HD
    group = query_heads // kv_heads
    block_len = cache_keys.shape[1]
    per_peer = max(1, CTX // block_len // seq)
    request = lax.axis_index("seq")
    rank = lax.axis_index("tp")
    length = cached_len[request]

    span = per_peer * block_len
    split = [(0, kv_heads - 1), (kv_heads - 1, 1)] if kv_heads > 1 else [(0, 1)]
    own_row = jnp.reshape(rank, (1,)).astype(jnp.int32)
    rest_rows = jnp.stack([(rank - shift) % tp for shift in range(1, tp)]).astype(jnp.int32)
    cosine, sine = rotation(length, tokens)

    def pick(first, count):
        return pick_blocks(
            page_table, cached_len, cache_keys, cache_values, first, count, seq, per_peer
        )

    def exchange(block):
        return lax.all_to_all(block, "seq", 0, 0, tiled=True)

    def swap(x, shift):
        return lax.ppermute(x, "tp", [(i, (i + shift) % tp) for i in range(tp)])

    half_tokens = tokens // 2
    received = [exchange(pick(*split[0]))]
    arrivals = []
    for half in range(2):
        mine = hidden[half * half_tokens : (half + 1) * half_tokens]
        if arrivals:
            mine, arrivals[0][0] = lax.optimization_barrier((mine, arrivals[0][0]))
        arrivals.append([swap(mine, shift) for shift in range(1, tp)])
    own_parts = [project_own(own_row, hidden, w) for w in (w_key, w_value, w_query)]

    def rest(half, parts):
        def one(weight, part, scale):
            return project_rest(
                rest_rows, half, arrivals[half], weight, part, cosine, sine, scale
            )

        return [
            one(w_key, parts[0], 1.0),
            one(w_value, parts[1], None),
            one(w_query, parts[2], HD ** (-0.5) / math.log(2.0)),
        ]

    fresh = [rest(0, own_parts), rest(1, own_parts)]
    for first, count in split[1:]:
        block, received[-1], fresh = lax.optimization_barrier(
            (pick(first, count), received[-1], fresh)
        )
        received.append(exchange(block))
    bias = received[0][:, 2 * span, :span].astype(F32).reshape(1, seq * span)
    attended = [None, None]

    def run(first, count, half):
        piece = 0 if first < split[0][1] else 1
        attended[half] = attend(
            first,
            count,
            first - split[piece][0],
            group,
            fresh[half][2],
            [fresh[i][0] for i in range(half + 1)],
            [fresh[i][1] for i in range(half + 1)],
            received[piece],
            bias,
            attended[half],
        )

    width = w_out.shape[1] // tp
    targets = [jnp.reshape((rank + s) % tp, (1,)).astype(jnp.int32) for s in range(1, tp)]
    strips = 2

    def out_parts(half):
        return [project_out(t, attended[half], w_out, width, strips, BF16) for t in targets]

    run(*split[0], 0)
    run(0, 1, 1)
    if len(split) > 1:
        received[1], attended[0], attended[1] = lax.optimization_barrier(
            (received[1], attended[0], attended[1])
        )
        run(*split[1], 0)
    other = [out_parts(0)]
    for head in range(1, kv_heads - 1):
        run(head, 1, 1)
    held = attended[1]
    if len(split) > 1:
        run(*split[1], 1)
    other.append(out_parts(1))
    own = [project_out(own_row, attended[half], w_out, width, strips, F32) for half in range(2)]
    sums = [[] for _ in range(2 * strips)]
    for shift in range(1, tp):
        for i in range(2 * strips):
            strip = other[i // strips][shift - 1][i % strips]
            if tp == 2 and i > 0:
                if i == 1:
                    strip, sums[0], held = lax.optimization_barrier((strip, sums[0], held))
                elif i == 2 * strips - 1:
                    strip, sums[i - 1], own = lax.optimization_barrier((strip, sums[i - 1], own))
                else:
                    strip, sums[i - 1] = lax.optimization_barrier((strip, sums[i - 1]))
            sums[i].append(swap(strip, shift))
    out = None
    for i in range(2 * strips):
        out = combine(own[i // strips][i % strips], sums[i], i, tokens, out)
    return out


def solution(mesh):
    in_specs = (
        P("seq", "tp"),
        P(None, "tp"),
        P(None, "tp"),
        P(None, "tp"),
        P("tp", None),
        P("seq", None, "tp"),
        P("seq", None, "tp"),
        P(),
        P("seq", None),
    )
    out_specs = P("seq", "tp")
    return jax.shard_map(
        on_device, mesh=mesh, in_specs=in_specs, out_specs=out_specs, check_vma=False
    )
```

time: 375 us -> 187 us (0.50); the launches traced: 370 us -> 186 us
  Pallas kernels: 274 us -> 135 us
  blocking collectives: 18.6 us -> 0 us
  waiting for transfers between devices: 34.7 us -> 21.3 us
  starting transfers between devices: 30.1 us -> 20.6 us
  other arithmetic: 8.44 us -> 4 us
    pallas_call x8 -> x12, Pallas kernels: 199 us -> 62.9 us  [the longest x6 48.3 us: attend(): pl.pallas_call(body, grid=(count * group,), in_specs=in_specs, out_specs=...]
    all_gather x1 -> x0, blocking collectives: 18.6 us -> none  [on_device(): table = lax.all_gather(page_table[None], 'seq', axis=0, tiled=True)]
    ppermute x5 -> x6, waiting for transfers between devices: 34.7 us -> 18.3 us  [swap(): return lax.ppermute(x, 'tp', [(i, (i + shift) % tp) for i in range(tp)])]
    all_to_all x4 -> x2, starting transfers between devices: 24.5 us -> 13 us  [exchange(): return lax.all_to_all(block, 'seq', 0, 0, tiled=True)]
    pallas_call x5 -> x4, Pallas kernels: 32.3 us -> 23.7 us  [project_out(): pl.pallas_call(body, grid_spec=pltpu.PrefetchScalarGridSpec(num_scalar_pr...]
    pallas_call x3 -> x6, Pallas kernels: 24.7 us -> 30 us  [project_rest(): pl.pallas_call(body, grid_spec=pltpu.PrefetchScalarGridSpec(num_scalar_pr...]
    ppermute x5 -> x6, starting transfers between devices: 5.64 us -> 7.64 us  [swap(): return lax.ppermute(x, 'tp', [(i, (i + shift) % tp) for i in range(tp)])]
  transfers between devices with their start and end apart: 9 -> 8, of which waited for: 4 -> 6; matrix products, arithmetic and copies ran while one was open for 1% -> 3% of each run, Pallas kernels for 54% -> 63%
where the time goes in v2:
time: 187 us; the launch traced here: 186 us
  Pallas kernels  135 us (72%)
  waiting for transfers between devices  21.3 us (11%)
  starting transfers between devices  20.6 us (11%)
  local copies, waits for them, and re-layouts  5.9 us (3%)
  other arithmetic  4 us (2%)
    pallas_call x6, Pallas kernels, attend(): pl.pallas_call(body, grid=(count * group,), in_specs=in_specs, out_specs=...  48.3 us
    pallas_call x6, Pallas kernels, project_rest(): pl.pallas_call(body, grid_spec=pltpu.PrefetchScalarGridSpec(num_scalar_pr...  30 us
    pallas_call x4, Pallas kernels, project_out(): pl.pallas_call(body, grid_spec=pltpu.PrefetchScalarGridSpec(num_scalar_pr...  23.7 us
    ppermute x6, waiting for transfers between devices, swap(): return lax.ppermute(x, 'tp', [(i, (i + shift) % tp) for i in range(tp)])  18.3 us
    pallas_call x3, Pallas kernels, project_own(): pl.pallas_call(body, grid_spec=pltpu.PrefetchScalarGridSpec(num_scalar_pr...  18 us
    all_to_all x2, starting transfers between devices, exchange(): return lax.all_to_all(block, 'seq', 0, 0, tiled=True)  13 us
    pallas_call x4, Pallas kernels, combine(): pl.pallas_call(body, grid=(width // step,), in_specs=in_specs, out_specs=...  8.38 us
    ppermute x6, starting transfers between devices, swap(): return lax.ppermute(x, 'tp', [(i, (i + shift) % tp) for i in range(tp)])  7.64 us
  transfers between devices with their start and end apart: 8, of which 6 were waited for; matrix products, arithmetic and copies ran while one was open for 3% of the time, Pallas kernels for 63%

profile of v2, /device:TPU:8, one launch (start us, length us, event | category | flops | bytes accessed | tf_op | source)
XLA Modules:
  0.0 186.5 jit_solution(15750421491843700460)
XLA Ops:
  1.3 3.8 %pick_blocks.3 = bf16[16,272,384]{2,1,0:T(8,128)(2,1)} custom-call(s32[16,2]{1,0:T(8,128)} %copy.17.table, s32[16]{0:T(128)} %lengths.3, bf16[16,64,512]{2,1,0:T(8,128)(2,1)} %keys.3, bf16[16,64,512]{2,1,0:T(8,128)(2,1)} %values.3), custom_call_target="tpu_custom_call" | custom-call | bytes 6684672 | tf_op jit(solution)/shard_map/pick_blocks/pallas_call | solution.py:68
  5.2 6.4 %all-to-all-start = ((bf16[16,272,384]{2,1,0:T(8,128)(2,1)}), bf16[16,272,384]{2,1,0:T(8,128)(2,1)}, u32[]{:S(2)}, u32[]{:S(2)}) async-start(bf16[16,272,384]{2,1,0:T(8,128)(2,1)} %pick_blocks.3), calls=%async_computation | async-start | bytes 6684672 | tf_op jit(solution)/shard_map/all_to_all | solution.py:343
  17.3 4.4 %project_own.4.refs_2_ = f32[512,512]{1,0:T(8,128)} custom-call(s32[1]{0:T(128)} %bitcast.2.rows.cols, bf16[512,2048]{1,0:T(8,128)(2,1)} %x_ref.5, bf16[4096,512]{1,0:T(8,128)(2,1)} %refs_1_.10), custom_call_target="tpu_custom_call" | custom-call | flops 1073741824 | bytes 3145728 | tf_op jit(solution)/shard_map/project_own/pallas_call | solution.py:94
  21.7 4.4 %project_own.3.refs_2_ = f32[512,512]{1,0:T(8,128)} custom-call(s32[1]{0:T(128)} %bitcast.2.rows.cols, bf16[512,2048]{1,0:T(8,128)(2,1)} %x_ref.5, bf16[4096,512]{1,0:T(8,128)(2,1)} %refs_1_.9), custom_call_target="tpu_custom_call" | custom-call | flops 1073741824 | bytes 3145728 | tf_op jit(solution)/shard_map/project_own/pallas_call | solution.py:94
  26.8 11.3 %collective-permute-done.refs_0_ = bf16[256,2048]{1,0:T(8,128)(2,1)S(1)} collective-permute-done((bf16[256,2048]{1,0:T(8,128)(2,1)}, bf16[256,2048]{1,0:T(8,128)(2,1)S(1)}, u32[]{:S(2)}, u32[]{:S(2)}) %collective-permute-start) | collective-permute-done | bytes 1048608 | tf_op jit(solution)/shard_map/ppermute | solution.py:346
  41.7 9.1 %project_own.5.refs_2_ = f32[512,2048]{1,0:T(8,128)} custom-call(s32[1]{0:T(128)} %bitcast.2.rows.cols, bf16[512,2048]{1,0:T(8,128)(2,1)} %x_ref.5, bf16[4096,2048]{1,0:T(8,128)(2,1)} %refs_1_.11), custom_call_target="tpu_custom_call" | custom-call | flops 4294967296 | bytes 12582912 | tf_op jit(solution)/shard_map/project_own/pallas_call | solution.py:94
  50.9 3.5 %project_rest.7.refs_4_.refs_5_ = bf16[4,256,128]{2,1,0:T(8,128)(2,1)} custom-call(s32[1]{0:T(128)} %bitcast.1.rows, bf16[256,2048]{1,0:T(8,128)(2,1)} %copy-done.1, bf16[4096,512]{1,0:T(8,128)(2,1)} %refs_1_.10, f32[512,512]{1,0:T(8,128)} %project_own.4.refs_2_, f32[512,128]{1,0:T(8,128)} %get-tuple-element.72.refs_3_, f32[512,128]{1,0:T(8,128)} %get-tuple-element.73.refs_4_), custom_call_target="tpu_custom_call" | custom-call | flops 536870912 | bytes 3145728 | tf_op jit(solution)/shard_map/project_rest/pallas_call | solution.py:137
  54.3 3.7 %project_rest.6.refs_3_ = bf16[4,256,128]{2,1,0:T(8,128)(2,1)} custom-call(s32[1]{0:T(128)} %bitcast.1.rows, bf16[256,2048]{1,0:T(8,128)(2,1)} %copy-done.1, bf16[4096,512]{1,0:T(8,128)(2,1)} %refs_1_.9, f32[512,512]{1,0:T(8,128)} %project_own.3.refs_2_, f32[512,128]{1,0:T(8,128)} %get-tuple-element.72.refs_3_, f32[512,128]{1,0:T(8,128)} %get-tuple-element.73.refs_4_), custom_call_target="tpu_custom_call" | custom-call | flops 536870912 | bytes 3145728 | tf_op jit(solution)/shard_map/project_rest/pallas_call | solution.py:137
  58.1 7.8 %project_rest.8.refs_0_ = bf16[16,256,128]{2,1,0:T(8,128)(2,1)} custom-call(s32[1]{0:T(128)} %bitcast.1.rows, bf16[256,2048]{1,0:T(8,128)(2,1)} %copy-done.1, bf16[4096,2048]{1,0:T(8,128)(2,1)} %refs_1_.11, f32[512,2048]{1,0:T(8,128)} %project_own.5.refs_2_, f32[512,128]{1,0:T(8,128)} %get-tuple-element.72.refs_3_, f32[512,128]{1,0:T(8,128)} %get-tuple-element.73.refs_4_), custom_call_target="tpu_custom_call" | custom-call | flops 2147483648 | bytes 12582912 | tf_op jit(solution)/shard_map/project_rest/pallas_call | solution.py:137
  66.8 3.5 %project_rest.10.refs_6_ = bf16[4,256,128]{2,1,0:T(8,128)(2,1)} custom-call(s32[1]{0:T(128)} %bitcast.1.rows, bf16[256,2048]{1,0:T(8,128)(2,1)} %copy-done.2, bf16[4096,512]{1,0:T(8,128)(2,1)} %refs_1_.10, f32[512,512]{1,0:T(8,128)} %project_own.4.refs_2_, f32[512,128]{1,0:T(8,128)} %get-tuple-element.72.refs_3_, f32[512,128]{1,0:T(8,128)} %get-tuple-element.73.refs_4_), custom_call_target="tpu_custom_call" | custom-call | flops 536870912 | bytes 3145728 | tf_op jit(solution)/shard_map/project_rest/pallas_call | solution.py:137
  70.3 3.7 %project_rest.9.refs_4_ = bf16[4,256,128]{2,1,0:T(8,128)(2,1)} custom-call(s32[1]{0:T(128)} %bitcast.1.rows, bf16[256,2048]{1,0:T(8,128)(2,1)} %copy-done.2, bf16[4096,512]{1,0:T(8,128)(2,1)} %refs_1_.9, f32[512,512]{1,0:T(8,128)} %project_own.3.refs_2_, f32[512,128]{1,0:T(8,128)} %get-tuple-element.72.refs_3_, f32[512,128]{1,0:T(8,128)} %get-tuple-element.73.refs_4_), custom_call_target="tpu_custom_call" | custom-call | flops 536870912 | bytes 3145728 | tf_op jit(solution)/shard_map/project_rest/pallas_call | solution.py:137
  74.0 7.8 %project_rest.11.refs_0_ = bf16[16,256,128]{2,1,0:T(8,128)(2,1)} custom-call(s32[1]{0:T(128)} %bitcast.1.rows, bf16[256,2048]{1,0:T(8,128)(2,1)} %copy-done.2, bf16[4096,2048]{1,0:T(8,128)(2,1)} %refs_1_.11, f32[512,2048]{1,0:T(8,128)} %project_own.5.refs_2_, f32[512,128]{1,0:T(8,128)} %get-tuple-element.72.refs_3_, f32[512,128]{1,0:T(8,128)} %get-tuple-element.73.refs_4_), custom_call_target="tpu_custom_call" | custom-call | flops 2147483648 | bytes 12582912 | tf_op jit(solution)/shard_map/project_rest/pallas_call | solution.py:137
  84.1 6.6 %all-to-all-start.1 = ((bf16[16,256,128]{2,1,0:T(8,128)(2,1)}), bf16[16,256,128]{2,1,0:T(8,128)(2,1)S(1)}, u32[]{:S(2)}, u32[]{:S(2)}) async-start(bf16[16,256,128]{2,1,0:T(8,128)(2,1)} %pick_blocks.2), calls=%async_computation.1 | async-start | bytes 2097152 | tf_op jit(solution)/shard_map/all_to_all | solution.py:343
  92.0 6.6 %attend.7.refs_7_ = bf16[256,2048]{1,0:T(8,128)(2,1)} custom-call(bf16[16,256,128]{2,1,0:T(8,128)(2,1)} %project_rest.11.refs_0_, bf16[16,272,384]{2,1,0:T(8,128)(2,1)} %all-to-all-done.refs_1_, f32[1,2048]{1,0:T(1,128)} %bitcast_convert_fusion.refs_2_, bf16[4,256,128]{2,1,0:T(8,128)(2,1)} %project_rest.6.refs_3_, bf16[4,256,128]{2,1,0:T(8,128)(2,1)} %project_rest.9.refs_4_, ...), custom_call_target="tpu_custom_call" | custom-call | flops 2684354560 | bytes 1048576 | tf_op jit(solution)/shard_map/attend/pallas_call | solution.py:229
  98.6 15.6 %attend.6.refs_5_ = bf16[256,2048]{1,0:T(8,128)(2,1)} custom-call(bf16[16,256,128]{2,1,0:T(8,128)(2,1)} %project_rest.8.refs_0_, bf16[16,272,384]{2,1,0:T(8,128)(2,1)} %all-to-all-done.refs_1_, f32[1,2048]{1,0:T(1,128)} %bitcast_convert_fusion.refs_2_, bf16[4,256,128]{2,1,0:T(8,128)(2,1)} %project_rest.6.refs_3_, ...), custom_call_target="tpu_custom_call" | custom-call | flops 7247757312 | bytes 3145728 | tf_op jit(solution)/shard_map/attend/pallas_call | solution.py:229
  115.9 6.2 %attend.11.x_ref = bf16[256,2048]{1,0:T(8,128)(2,1)} custom-call(bf16[16,256,128]{2,1,0:T(8,128)(2,1)} %project_rest.8.refs_0_, bf16[16,256,128]{2,1,0:T(8,128)(2,1)} %copy-done.3, f32[1,2048]{1,0:T(1,128)} %bitcast_convert_fusion.refs_2_, bf16[4,256,128]{2,1,0:T(8,128)(2,1)} %project_rest.6.refs_3_, ...), custom_call_target="tpu_custom_call", output_to_operand_aliasing={{}: (5, {})} | custom-call | flops 2415919104 | bytes 1048576 | tf_op jit(solution)/shard_map/attend/pallas_call | solution.py:229
  122.1 5.8 %project_out.5 = (bf16[128,2048]{1,0:T(8,128)(2,1)}, bf16[128,2048]{1,0:T(8,128)(2,1)}) custom-call(s32[1]{0:T(128)} %bitcast.cols, bf16[256,2048]{1,0:T(8,128)(2,1)} %attend.11.x_ref, bf16[2048,4096]{1,0:T(8,128)(2,1)} %w_ref.13), custom_call_target="tpu_custom_call" | custom-call | flops 2147483648 | bytes 10485760 | tf_op jit(solution)/shard_map/project_out/pallas_call | solution.py:257
  129.5 6.6 %attend.8.refs_7_ = bf16[256,2048]{1,0:T(8,128)(2,1)} custom-call(bf16[16,256,128]{2,1,0:T(8,128)(2,1)} %project_rest.11.refs_0_, bf16[16,272,384]{2,1,0:T(8,128)(2,1)} %all-to-all-done.refs_1_, f32[1,2048]{1,0:T(1,128)} %bitcast_convert_fusion.refs_2_, bf16[4,256,128]{2,1,0:T(8,128)(2,1)} %project_rest.6.refs_3_, ...), custom_call_target="tpu_custom_call", output_to_operand_aliasing={{}: (7, {})} | custom-call | flops 2684354560 | bytes 1048576 | tf_op jit(solution)/shard_map/attend/pallas_call | solution.py:229
  136.1 6.7 %attend.9.refs_7_ = bf16[256,2048]{1,0:T(8,128)(2,1)} custom-call(bf16[16,256,128]{2,1,0:T(8,128)(2,1)} %project_rest.11.refs_0_, bf16[16,272,384]{2,1,0:T(8,128)(2,1)} %all-to-all-done.refs_1_, f32[1,2048]{1,0:T(1,128)} %bitcast_convert_fusion.refs_2_, bf16[4,256,128]{2,1,0:T(8,128)(2,1)} %project_rest.6.refs_3_, ...), custom_call_target="tpu_custom_call", output_to_operand_aliasing={{}: (7, {})} | custom-call | flops 2684354560 | bytes 1048576 | tf_op jit(solution)/shard_map/attend/pallas_call | solution.py:229
  144.3 6.6 %attend.10.x_ref = bf16[256,2048]{1,0:T(8,128)(2,1)} custom-call(bf16[16,256,128]{2,1,0:T(8,128)(2,1)} %project_rest.11.refs_0_, bf16[16,256,128]{2,1,0:T(8,128)(2,1)} %copy-done.3, f32[1,2048]{1,0:T(1,128)} %bitcast_convert_fusion.refs_2_, bf16[4,256,128]{2,1,0:T(8,128)(2,1)} %project_rest.6.refs_3_, ...), custom_call_target="tpu_custom_call", output_to_operand_aliasing={{}: (7, {})} | custom-call | flops 2684354560 | bytes 1048576 | tf_op jit(solution)/shard_map/attend/pallas_call | solution.py:229
  150.9 5.8 %project_out.4 = (bf16[128,2048]{1,0:T(8,128)(2,1)}, bf16[128,2048]{1,0:T(8,128)(2,1)}) custom-call(s32[1]{0:T(128)} %bitcast.cols, bf16[256,2048]{1,0:T(8,128)(2,1)} %attend.10.x_ref, bf16[2048,4096]{1,0:T(8,128)(2,1)} %w_ref.13), custom_call_target="tpu_custom_call" | custom-call | flops 2147483648 | bytes 10485760 | tf_op jit(solution)/shard_map/project_out/pallas_call | solution.py:257
  158.0 6.0 %project_out.6 = (f32[128,2048]{1,0:T(8,128)}, f32[128,2048]{1,0:T(8,128)}) custom-call(s32[1]{0:T(128)} %bitcast.2.rows.cols, bf16[256,2048]{1,0:T(8,128)(2,1)} %attend.11.x_ref, bf16[2048,4096]{1,0:T(8,128)(2,1)} %w_ref.13), custom_call_target="tpu_custom_call" | custom-call | flops 2147483648 | bytes 10485760 | tf_op jit(solution)/shard_map/project_out/pallas_call | solution.py:257
  164.0 6.1 %project_out.7 = (f32[128,2048]{1,0:T(8,128)}, f32[128,2048]{1,0:T(8,128)}) custom-call(s32[1]{0:T(128)} %bitcast.2.rows.cols, bf16[256,2048]{1,0:T(8,128)(2,1)} %attend.10.x_ref, bf16[2048,4096]{1,0:T(8,128)(2,1)} %w_ref.13), custom_call_target="tpu_custom_call" | custom-call | flops 2147483648 | bytes 10485760 | tf_op jit(solution)/shard_map/project_out/pallas_call | solution.py:257
  177.9 5.6 %collective-permute-done.5.refs_1_ = bf16[128,2048]{1,0:T(8,128)(2,1)S(1)} collective-permute-done((bf16[128,2048]{1,0:T(8,128)(2,1)S(1)}, bf16[128,2048]{1,0:T(8,128)(2,1)S(1)}, u32[]{:S(2)}, u32[]{:S(2)}) %collective-permute-start.5) | collective-permute-done | bytes 524320 | tf_op jit(solution)/shard_map/ppermute | solution.py:346
  (47 shorter events, 32.7 us)
Async XLA Ops:
  5.2 6.4 %copy-start = (bf16[512,2048]{1,0:T(8,128)(2,1)S(1)}, bf16[512,2048]{1,0:T(8,128)(2,1)}, u32[]{:S(2)}) copy-start(bf16[512,2048]{1,0:T(8,128)(2,1)} %x_ref.5) | copy-start | bytes 6291460
  5.2 79.0 %all-to-all-start = ((bf16[16,272,384]{2,1,0:T(8,128)(2,1)}), bf16[16,272,384]{2,1,0:T(8,128)(2,1)}, u32[]{:S(2)}, u32[]{:S(2)}) async-start(bf16[16,272,384]{2,1,0:T(8,128)(2,1)} %pick_blocks.3), calls=%async_computation | async-start | bytes 6684672 | tf_op jit(solution)/shard_map/all_to_all | solution.py:343
  11.6 5.1 %copy-start.8 = (s32[16]{0:T(128)S(1)}, s32[16]{0:T(128)}, u32[]{:S(2)}) copy-start(s32[16]{0:T(128)} %lengths.3) | copy-start | bytes 196
  12.7 25.4 %collective-permute-start = (bf16[256,2048]{1,0:T(8,128)(2,1)}, bf16[256,2048]{1,0:T(8,128)(2,1)S(1)}, u32[]{:S(2)}, u32[]{:S(2)}) collective-permute-start(bf16[256,2048]{1,0:T(8,128)(2,1)} %get-tuple-element.67), channel_id=1, source_target_pairs={{0,1},{1,0},{2,3},{3,2},{4,5},{5,4},{6,7},{7,6},{8,9},{9,8},{10,11... | collective-permute-start | bytes 3145736 | tf_op jit(solution)/shard_map/ppermute | solution.py:346
  38.2 12.7 %copy-start.1 = (bf16[256,2048]{1,0:T(8,128)(2,1)}, bf16[256,2048]{1,0:T(8,128)(2,1)S(1)}, u32[]{:S(2)}) copy-start(bf16[256,2048]{1,0:T(8,128)(2,1)S(1)} %collective-permute-done.refs_0_) | copy-start | bytes 3145732
  38.2 27.7 %collective-permute-start.1 = (bf16[256,2048]{1,0:T(8,128)(2,1)S(1)}, bf16[256,2048]{1,0:T(8,128)(2,1)S(1)}, u32[]{:S(2)}, u32[]{:S(2)}) collective-permute-start(bf16[256,2048]{1,0:T(8,128)(2,1)S(1)} %get-tuple-element.37), channel_id=1, source_target_pairs={{0,1},{1,0},{2,3},{3,2},{4,5},{5,4},{6,7},{7,6},{8,9},{9,8},{10,11... | collective-permute-start | bytes 3145736 | tf_op jit(solution)/shard_map/ppermute | solution.py:346
  65.9 1.0 copy-start.2
  84.1 30.8 %all-to-all-start.1 = ((bf16[16,256,128]{2,1,0:T(8,128)(2,1)}), bf16[16,256,128]{2,1,0:T(8,128)(2,1)S(1)}, u32[]{:S(2)}, u32[]{:S(2)}) async-start(bf16[16,256,128]{2,1,0:T(8,128)(2,1)} %pick_blocks.2), calls=%async_computation.1 | async-start | bytes 2097152 | tf_op jit(solution)/shard_map/all_to_all | solution.py:343
  114.9 1.0 copy-start.3
  128.0 14.8 %collective-permute-start.2 = (bf16[128,2048]{1,0:T(8,128)(2,1)}, bf16[128,2048]{1,0:T(8,128)(2,1)S(1)}, u32[]{:S(2)}, u32[]{:S(2)}) collective-permute-start(bf16[128,2048]{1,0:T(8,128)(2,1)} %get-tuple-element.52), channel_id=1, source_target_pairs={{0,1},{1,0},{2,3},{3,2},{4,5},{5,4},{6,7},{7,6},{8,9},{9,8},{10,11... | collective-permute-start | bytes 1572872 | tf_op jit(solution)/shard_map/ppermute | solution.py:346
  136.1 6.7 %copy-start.10 = (bf16[128,2048]{1,0:T(8,128)(2,1)S(1)}, bf16[128,2048]{1,0:T(8,128)(2,1)}, u32[]{:S(2)}) copy-start(bf16[128,2048]{1,0:T(8,128)(2,1)} %get-tuple-element.53) | copy-start | bytes 1572868
  142.8 8.1 %copy-start.4 = (bf16[128,2048]{1,0:T(8,128)(2,1)}, bf16[128,2048]{1,0:T(8,128)(2,1)S(1)}, u32[]{:S(2)}) copy-start(bf16[128,2048]{1,0:T(8,128)(2,1)S(1)} %collective-permute-done.2.refs_1_) | copy-start | bytes 1572868
  142.8 14.4 %collective-permute-start.3 = (bf16[128,2048]{1,0:T(8,128)(2,1)S(1)}, bf16[128,2048]{1,0:T(8,128)(2,1)S(1)}, u32[]{:S(2)}, u32[]{:S(2)}) collective-permute-start(bf16[128,2048]{1,0:T(8,128)(2,1)S(1)} %copy-done.10), channel_id=1, source_target_pairs={{0,1},{1,0},{2,3},{3,2},{4,5},{5,4},{6,7},{7,6},{8,9},{9,8},{10,11... | collective-permute-start | bytes 1572872 | tf_op jit(solution)/shard_map/ppermute | solution.py:346
  157.2 6.8 %copy-start.5 = (bf16[128,2048]{1,0:T(8,128)(2,1)}, bf16[128,2048]{1,0:T(8,128)(2,1)S(1)}, u32[]{:S(2)}) copy-start(bf16[128,2048]{1,0:T(8,128)(2,1)S(1)} %collective-permute-done.3.refs_1_) | copy-start | bytes 1572868
  157.2 13.7 %collective-permute-start.4 = (bf16[128,2048]{1,0:T(8,128)(2,1)}, bf16[128,2048]{1,0:T(8,128)(2,1)S(1)}, u32[]{:S(2)}, u32[]{:S(2)}) collective-permute-start(bf16[128,2048]{1,0:T(8,128)(2,1)} %get-tuple-element.54), channel_id=1, source_target_pairs={{0,1},{1,0},{2,3},{3,2},{4,5},{5,4},{6,7},{7,6},{8,9},{9,8},{10,11... | collective-permute-start | bytes 1572872 | tf_op jit(solution)/shard_map/ppermute | solution.py:346
  164.0 6.9 %copy-start.9 = (bf16[128,2048]{1,0:T(8,128)(2,1)S(1)}, bf16[128,2048]{1,0:T(8,128)(2,1)}, u32[]{:S(2)}) copy-start(bf16[128,2048]{1,0:T(8,128)(2,1)} %get-tuple-element.60) | copy-start | bytes 1572868
  170.9 4.9 %copy-start.6 = (bf16[128,2048]{1,0:T(8,128)(2,1)}, bf16[128,2048]{1,0:T(8,128)(2,1)S(1)}, u32[]{:S(2)}) copy-start(bf16[128,2048]{1,0:T(8,128)(2,1)S(1)} %collective-permute-done.4.refs_1_) | copy-start | bytes 1572868
  170.9 12.6 %collective-permute-start.5 = (bf16[128,2048]{1,0:T(8,128)(2,1)S(1)}, bf16[128,2048]{1,0:T(8,128)(2,1)S(1)}, u32[]{:S(2)}, u32[]{:S(2)}) collective-permute-start(bf16[128,2048]{1,0:T(8,128)(2,1)S(1)} %copy-done.9), channel_id=1, source_target_pairs={{0,1},{1,0},{2,3},{3,2},{4,5},{5,4},{6,7},{7,6},{8,9},{9,8},{10,11... | collective-permute-start | bytes 1572872 | tf_op jit(solution)/shard_map/ppermute | solution.py:346
  183.6 0.8 copy-start.7

commit v3 on v2

--- a/solution.py
+++ b/solution.py
@@ -29,10 +29,10 @@
 
 def pick_blocks(page_table, cached_len, cache_keys, cache_values, first, count, seq, per_peer):
     masked = first == 0
-    width = count * HD
     blocks, block_len, _ = cache_keys.shape
     span = per_peer * block_len
-    rows = 2 * span + (16 if masked else 0)
+    rows = 2 * span * count + (8 if masked else 0)
+    width = count * HD
 
     def body(table, lengths, keys, values, out, index):
         for slot in range(seq * per_peer):
@@ -49,20 +49,23 @@
             return carry
 
         lax.fori_loop(0, blocks, place, 0)
-        lane = lax.broadcasted_iota(jnp.int32, (16, width), 1)
+        lane = lax.broadcasted_iota(jnp.int32, (8, HD), 1)
         for r in range(seq):
-            mask = jnp.full((16, width), masked_score, F32)
+            mask = jnp.full((8, HD), masked_score, F32)
             for k in range(per_peer):
                 b = index[r * per_peer + k]
-                out[r, k * block_len : (k + 1) * block_len, :] = keys[b]
-                out[r, span + k * block_len : span + (k + 1) * block_len, :] = values[b]
+                for h in range(count):
+                    at = 2 * h * span + k * block_len
+                    columns = slice(h * HD, (h + 1) * HD)
+                    out[r, at : at + block_len, :] = keys[b, :, columns]
+                    out[r, at + span : at + span + block_len, :] = values[b, :, columns]
                 if masked:
                     filled = jnp.minimum(lengths[r] - table[b, 1] * block_len, block_len)
                     filled = jnp.where(index[tally + r] > k, filled, 0)
                     inside = (lane >= k * block_len) & (lane < k * block_len + filled)
                     mask = jnp.where(inside, 0.0, mask)
             if masked:
-                out[r, 2 * span :, :] = mask.astype(BF16)
+                out[r, 2 * span * count :, :] = mask.astype(BF16)
 
     part = pl.BlockSpec((blocks, block_len, width), lambda i: (0, 0, first // count))
     return pl.pallas_call(
@@ -74,11 +77,11 @@
             part,
             part,
         ],
-        out_specs=pl.BlockSpec((seq, rows, width), lambda i: (0, 0, 0)),
-        out_shape=jax.ShapeDtypeStruct((seq, rows, width), BF16),
+        out_specs=pl.BlockSpec((seq, rows, HD), lambda i: (0, 0, 0)),
+        out_shape=jax.ShapeDtypeStruct((seq, rows, HD), BF16),
         scratch_shapes=[pltpu.SMEM((seq * per_peer + seq,), jnp.int32)],
         compiler_params=params(1),
-        cost_estimate=cost(0, 2 * seq * rows * width * 2),
+        cost_estimate=cost(0, 2 * seq * rows * HD * 2),
         name="pick_blocks",
     )(page_table, cached_len, cache_keys, cache_values)
 
@@ -160,10 +163,9 @@
 def attend(first, count, at, group, queries, fresh_keys, fresh_values, cached, bias, attended):
     heads, tokens, _ = queries.shape
     parts = len(fresh_keys)
-    sources, all_rows, _ = cached.shape
+    sources = cached.shape[0]
     keys_count = bias.shape[1]
     rows = keys_count // sources
-    early = tokens * (parts - 1)
     tile = 128
     contract = (((1,), (1,)), ((), ()))
 
@@ -172,22 +174,18 @@
         key_refs = refs[3 : 3 + parts]
         value_refs = refs[3 + parts : 3 + 2 * parts]
         o_ref, old_values, new_values = refs[-3:]
-
-        @pl.when(pl.program_id(0) % group == 0)
-        def _():
-            old_values[:, :HD] = c_ref[:, rows : 2 * rows].reshape(keys_count, HD)
-            old_values[:, HD:] = jnp.ones((keys_count, HD), BF16)
-            for i in range(parts):
-                new_values[i * tokens : (i + 1) * tokens, :HD] = value_refs[i][0]
-            new_values[:, HD:] = jnp.ones((tokens * parts, HD), BF16)
-
+        old_values[:, :HD] = c_ref[:, rows:].reshape(keys_count, HD)
+        old_values[:, HD:] = jnp.ones((keys_count, HD), BF16)
+        for i in range(parts):
+            new_values[i * tokens : (i + 1) * tokens, :HD] = value_refs[i][0]
+        new_values[:, HD:] = jnp.ones((tokens * parts, HD), BF16)
         cached_keys = c_ref[:, :rows].reshape(keys_count, HD)
 
         def product(q, keys):
             return lax.dot_general(q, keys, contract, preferred_element_type=F32)
 
-        def scores(t):
-            q = q_ref[0, t * tile : (t + 1) * tile]
+        def scores(g, t):
+            q = q_ref[g, t * tile : (t + 1) * tile]
             width = (t + 1) * tile
             out = [product(q, cached_keys) + b_ref[...]]
             out += [product(q, ref[0]) for ref in key_refs[:-1]]
@@ -196,11 +194,12 @@
             out.append(jnp.where(col <= row, product(q, key_refs[-1][0, :width]), masked_score))
             return out
 
-        ahead = scores(0)
-        for t in range(tokens // tile):
+        work = [(g, t) for g in range(group) for t in range(tokens // tile)]
+        ahead = scores(*work[0])
+        for i, (g, t) in enumerate(work):
             now = ahead
-            if (t + 1) * tile < tokens:
-                ahead = scores(t + 1)
+            if i + 1 < len(work):
+                ahead = scores(*work[i + 1])
             top = jnp.max(now[0], axis=1, keepdims=True)
             for part in now[1:]:
                 top = jnp.maximum(top, jnp.max(part, axis=1, keepdims=True))
@@ -211,13 +210,15 @@
                 values = new_values[start : start + part.shape[1]]
                 mixed = mixed + jnp.dot(part, values, preferred_element_type=F32)
                 start += part.shape[1]
-            o_ref[t * tile : (t + 1) * tile] = (mixed[:, :HD] / mixed[:, HD:]).astype(BF16)
-
-    head_spec = pl.BlockSpec((1, tokens, HD), lambda g: (first + g // group, 0, 0))
+            o_ref[t * tile : (t + 1) * tile, g * HD : (g + 1) * HD] = (
+                mixed[:, :HD] / mixed[:, HD:]
+            ).astype(BF16)
+
+    head_spec = pl.BlockSpec((1, tokens, HD), lambda h: (first + h, 0, 0))
     in_specs = [
-        pl.BlockSpec((1, tokens, HD), lambda g: (first * group + g, 0, 0)),
-        pl.BlockSpec((sources, all_rows, HD), lambda g: (0, 0, at + g // group)),
-        pl.BlockSpec((1, keys_count), lambda g: (0, 0)),
+        pl.BlockSpec((group, tokens, HD), lambda h: (first + h, 0, 0)),
+        pl.BlockSpec((sources, 2 * rows, HD), lambda h: (0, at + h, 0)),
+        pl.BlockSpec((1, keys_count), lambda h: (0, 0)),
     ] + [head_spec] * (2 * parts)
     operands = [queries, cached, bias] + list(fresh_keys) + list(fresh_values)
     aliases = {}
@@ -228,13 +229,13 @@
     pairs = count * group * tokens * (keys_count + tokens * parts)
     return pl.pallas_call(
         body,
-        grid=(count * group,),
+        grid=(count,),
         in_specs=in_specs,
-        out_specs=pl.BlockSpec((tokens, HD), lambda g: (0, first * group + g)),
+        out_specs=pl.BlockSpec((tokens, group * HD), lambda h: (0, first + h)),
         out_shape=jax.ShapeDtypeStruct((tokens, heads * HD), BF16),
         scratch_shapes=[
             pltpu.VMEM((keys_count, 2 * HD), BF16),
-            pltpu.VMEM((early + tokens, 2 * HD), BF16),
+            pltpu.VMEM((tokens * parts, 2 * HD), BF16),
         ],
         input_output_aliases=aliases,
         compiler_params=params(1),
@@ -243,33 +244,40 @@
     )(*operands)
 
 
-def project_out(col_block, attended, weight, width, strips, kind):
-    rows, depth = attended.shape
+def project_out(col_block, attended, weight, width, strips, kind, depth, at=0, add=None):
+    rows = attended.shape[0]
     strip = rows // strips
     step = min(1024, width)
     steps = width // step
 
-    def body(cols, x_ref, w_ref, *o_refs):
-        total = jnp.dot(x_ref[...], w_ref[...], preferred_element_type=F32).astype(kind)
+    def body(cols, x_ref, w_ref, *refs):
+        total = jnp.dot(x_ref[...], w_ref[...], preferred_element_type=F32)
+        if add is not None:
+            total = total + refs[0][...]
         for i in range(strips):
-            o_refs[i][...] = total[i * strip : (i + 1) * strip]
-
+            refs[i - strips][...] = total[i * strip : (i + 1) * strip].astype(kind)
+
+    in_specs = [
+        pl.BlockSpec((rows, depth), lambda n, cols: (0, at)),
+        pl.BlockSpec((depth, step), lambda n, cols: (at, cols[0] * steps + n)),
+    ]
+    operands = [attended, weight]
+    if add is not None:
+        in_specs.append(pl.BlockSpec((rows, step), lambda n, cols: (0, n)))
+        operands.append(add)
     return pl.pallas_call(
         body,
         grid_spec=pltpu.PrefetchScalarGridSpec(
             num_scalar_prefetch=1,
             grid=(steps,),
-            in_specs=[
-                pl.BlockSpec((rows, depth), lambda n, cols: (0, 0)),
-                pl.BlockSpec((depth, step), lambda n, cols: (0, cols[0] * steps + n)),
-            ],
+            in_specs=in_specs,
             out_specs=[pl.BlockSpec((strip, step), lambda n, cols: (0, n))] * strips,
         ),
         out_shape=[jax.ShapeDtypeStruct((strip, width), kind)] * strips,
         compiler_params=params(1),
         cost_estimate=cost(2 * rows * depth * width, depth * width * 2 + rows * width * 4),
         name="project_out",
-    )(col_block, attended, weight)
+    )(col_block, *operands)
 
 
 def combine(own, parts, index, total_rows, out):
@@ -373,7 +381,7 @@
             (pick(first, count), received[-1], fresh)
         )
         received.append(exchange(block))
-    bias = received[0][:, 2 * span, :span].astype(F32).reshape(1, seq * span)
+    bias = received[0][:, 2 * span * split[0][1], :span].astype(F32).reshape(1, seq * span)
     attended = [None, None]
 
     def run(first, count, half):
@@ -393,41 +401,42 @@
 
     width = w_out.shape[1] // tp
     targets = [jnp.reshape((rank + s) % tp, (1,)).astype(jnp.int32) for s in range(1, tp)]
-    strips = 2
-
-    def out_parts(half):
-        return [project_out(t, attended[half], w_out, width, strips, BF16) for t in targets]
+    features = query_heads * HD
+    per_head = group * HD
+    early = per_head * split[0][1] if len(split) > 1 else features
 
     run(*split[0], 0)
-    run(0, 1, 1)
+    sums = []
     if len(split) > 1:
-        received[1], attended[0], attended[1] = lax.optimization_barrier(
-            (received[1], attended[0], attended[1])
+        sums = [project_out(t, attended[0], w_out, width, 1, F32, early)[0] for t in targets]
+        received[1], attended, sums = lax.optimization_barrier(
+            (received[1], attended, sums)
         )
         run(*split[1], 0)
-    other = [out_parts(0)]
-    for head in range(1, kv_heads - 1):
-        run(head, 1, 1)
-    held = attended[1]
+        late = features - early
+        other = [
+            project_out(t, attended[0], w_out, width, 1, BF16, late, early // late, part)
+            for t, part in zip(targets, sums)
+        ]
+    else:
+        other = [project_out(t, attended[0], w_out, width, 1, BF16, features) for t in targets]
+    other = [[swap(part[0], shift + 1)] for shift, part in enumerate(other)]
+    run(*split[0], 1)
     if len(split) > 1:
         run(*split[1], 1)
-    other.append(out_parts(1))
-    own = [project_out(own_row, attended[half], w_out, width, strips, F32) for half in range(2)]
-    sums = [[] for _ in range(2 * strips)]
-    for shift in range(1, tp):
-        for i in range(2 * strips):
-            strip = other[i // strips][shift - 1][i % strips]
-            if tp == 2 and i > 0:
-                if i == 1:
-                    strip, sums[0], held = lax.optimization_barrier((strip, sums[0], held))
-                elif i == 2 * strips - 1:
-                    strip, sums[i - 1], own = lax.optimization_barrier((strip, sums[i - 1], own))
-                else:
-                    strip, sums[i - 1] = lax.optimization_barrier((strip, sums[i - 1]))
-            sums[i].append(swap(strip, shift))
+    strips = 2 if tp == 2 else 1
+    for shift, target in enumerate(targets):
+        parts = project_out(target, attended[1], w_out, width, strips, BF16, features)
+        if shift == 0 and tp == 2:
+            parts, other[0] = lax.optimization_barrier((parts, other[0]))
+        other[shift] += [swap(part, shift + 1) for part in parts]
+    own = project_out(own_row, attended[0], w_out, width, 1, F32, features)
+    own += project_out(own_row, attended[1], w_out, width, strips, F32, features)
     out = None
-    for i in range(2 * strips):
-        out = combine(own[i // strips][i % strips], sums[i], i, tokens, out)
+    row = 0
+    for i, part in enumerate(own):
+        out = combine(part, [arrived[i] for arrived in other], row // part.shape[0], tokens, out)
+        row += part.shape[0]
     return out
 
 

time: 187 us -> 177 us (0.947)
  Pallas kernels: 135 us -> 122 us
  waiting for transfers between devices: 21.3 us -> 25.3 us
  starting transfers between devices: 20.6 us -> 18.2 us
    pallas_call x6 -> x4, Pallas kernels: 48.3 us -> 34.1 us  [attend(): pl.pallas_call(body, grid=(count,), in_specs=in_specs, out_specs=pl.Block...]
    all_to_all x2, waiting for transfers between devices: 3.01 us -> 6.43 us  [exchange(): return lax.all_to_all(block, 'seq', 0, 0, tiled=True)]
    pallas_call x4 -> x5, Pallas kernels: 23.7 us -> 26.4 us  [project_out(): pl.pallas_call(body, grid_spec=pltpu.PrefetchScalarGridSpec(num_scalar_pr...]
    ppermute x6 -> x5, starting transfers between devices: 7.64 us -> 5.77 us  [swap(): return lax.ppermute(x, 'tp', [(i, (i + shift) % tp) for i in range(tp)])]
    pallas_call x4 -> x3, Pallas kernels: 8.38 us -> 6.9 us  [combine(): pl.pallas_call(body, grid=(width // step,), in_specs=in_specs, out_specs=...]
    unnamed x23 -> x17, local copies, waits for them, and re-layouts: 4.12 us -> 4.92 us
    ppermute x6 -> x5, waiting for transfers between devices: 18.3 us -> 18.9 us  [swap(): return lax.ppermute(x, 'tp', [(i, (i + shift) % tp) for i in range(tp)])]
  transfers between devices with their start and end apart: 8 -> 7, of which waited for: 6 -> 4; matrix products, arithmetic and copies ran while one was open for 3% -> 3% of each run, Pallas kernels for 63% -> 61%
where the time goes in v3:
time: 177 us; the launch traced here: 176 us
  Pallas kernels  122 us (69%)
  waiting for transfers between devices  25.3 us (14%)
  starting transfers between devices  18.2 us (10%)
  local copies, waits for them, and re-layouts  6.66 us (4%)
  other arithmetic  3.93 us (2%)
    pallas_call x4, Pallas kernels, attend(): pl.pallas_call(body, grid=(count,), in_specs=in_specs, out_specs=pl.Block...  34.1 us
    pallas_call x6, Pallas kernels, project_rest(): pl.pallas_call(body, grid_spec=pltpu.PrefetchScalarGridSpec(num_scalar_pr...  30 us
    pallas_call x5, Pallas kernels, project_out(): pl.pallas_call(body, grid_spec=pltpu.PrefetchScalarGridSpec(num_scalar_pr...  26.4 us
    ppermute x5, waiting for transfers between devices, swap(): return lax.ppermute(x, 'tp', [(i, (i + shift) % tp) for i in range(tp)])  18.9 us
    pallas_call x3, Pallas kernels, project_own(): pl.pallas_call(body, grid_spec=pltpu.PrefetchScalarGridSpec(num_scalar_pr...  18.2 us
    all_to_all x2, starting transfers between devices, exchange(): return lax.all_to_all(block, 'seq', 0, 0, tiled=True)  12.4 us
    pallas_call x3, Pallas kernels, combine(): pl.pallas_call(body, grid=(width // step,), in_specs=in_specs, out_specs=...  6.9 us
    pallas_call x2, Pallas kernels, pick_blocks(): pl.pallas_call(body, grid=(1,), in_specs=[pl.BlockSpec(memory_space=pltpu...  6.44 us
  transfers between devices with their start and end apart: 7, of which 4 were waited for; matrix products, arithmetic and copies ran while one was open for 3% of the time, Pallas kernels for 61%

profile of v3, /device:TPU:8, one launch (start us, length us, event | category | flops | bytes accessed | tf_op | source)
XLA Modules:
  0.0 176.2 jit_solution(10429192369984264283)
XLA Ops:
  1.3 4.1 %pick_blocks.3 = bf16[16,776,128]{2,1,0:T(8,128)(2,1)} custom-call(s32[16,2]{1,0:T(8,128)} %copy.14.table, s32[16]{0:T(128)} %lengths.3, bf16[16,64,512]{2,1,0:T(8,128)(2,1)} %keys.3, bf16[16,64,512]{2,1,0:T(8,128)(2,1)} %values.3), custom_call_target="tpu_custom_call" | custom-call | bytes 6356992 | tf_op jit(solution)/shard_map/pick_blocks/pallas_call | solution.py:71
  5.4 6.4 %all-to-all-start = ((bf16[16,776,128]{2,1,0:T(8,128)(2,1)}), bf16[16,776,128]{2,1,0:T(8,128)(2,1)}, u32[]{:S(2)}, u32[]{:S(2)}) async-start(bf16[16,776,128]{2,1,0:T(8,128)(2,1)} %pick_blocks.3), calls=%async_computation | async-start | bytes 6356992 | tf_op jit(solution)/shard_map/all_to_all | solution.py:351
  17.5 4.5 %project_own.3.refs_2_ = f32[512,512]{1,0:T(8,128)} custom-call(s32[1]{0:T(128)} %bitcast.rows.cols, bf16[512,2048]{1,0:T(8,128)(2,1)} %x_ref.5, bf16[4096,512]{1,0:T(8,128)(2,1)} %refs_1_.9), custom_call_target="tpu_custom_call" | custom-call | flops 1073741824 | bytes 3145728 | tf_op jit(solution)/shard_map/project_own/pallas_call | solution.py:97
  21.9 4.5 %project_own.4.refs_2_ = f32[512,512]{1,0:T(8,128)} custom-call(s32[1]{0:T(128)} %bitcast.rows.cols, bf16[512,2048]{1,0:T(8,128)(2,1)} %x_ref.5, bf16[4096,512]{1,0:T(8,128)(2,1)} %refs_1_.10), custom_call_target="tpu_custom_call" | custom-call | flops 1073741824 | bytes 3145728 | tf_op jit(solution)/shard_map/project_own/pallas_call | solution.py:97
  27.0 11.4 %collective-permute-done.refs_0_ = bf16[256,2048]{1,0:T(8,128)(2,1)S(1)} collective-permute-done((bf16[256,2048]{1,0:T(8,128)(2,1)}, bf16[256,2048]{1,0:T(8,128)(2,1)S(1)}, u32[]{:S(2)}, u32[]{:S(2)}) %collective-permute-start) | collective-permute-done | bytes 1048608 | tf_op jit(solution)/shard_map/ppermute | solution.py:354
  41.9 9.2 %project_own.5.refs_2_ = f32[512,2048]{1,0:T(8,128)} custom-call(s32[1]{0:T(128)} %bitcast.rows.cols, bf16[512,2048]{1,0:T(8,128)(2,1)} %x_ref.5, bf16[4096,2048]{1,0:T(8,128)(2,1)} %refs_1_.11), custom_call_target="tpu_custom_call" | custom-call | flops 4294967296 | bytes 12582912 | tf_op jit(solution)/shard_map/project_own/pallas_call | solution.py:97
  51.2 3.5 %project_rest.7.refs_4_.refs_5_ = bf16[4,256,128]{2,1,0:T(8,128)(2,1)} custom-call(s32[1]{0:T(128)} %bitcast.1.rows, bf16[256,2048]{1,0:T(8,128)(2,1)} %copy-done.1, bf16[4096,512]{1,0:T(8,128)(2,1)} %refs_1_.10, f32[512,512]{1,0:T(8,128)} %project_own.4.refs_2_, f32[512,128]{1,0:T(8,128)} %get-tuple-element.50.refs_3_, f32[512,128]{1,0:T(8,128)} %get-tuple-element.51.refs_4_), custom_call_target="tpu_custom_call" | custom-call | flops 536870912 | bytes 3145728 | tf_op jit(solution)/shard_map/project_rest/pallas_call | solution.py:140
  54.6 3.7 %project_rest.6.refs_3_ = bf16[4,256,128]{2,1,0:T(8,128)(2,1)} custom-call(s32[1]{0:T(128)} %bitcast.1.rows, bf16[256,2048]{1,0:T(8,128)(2,1)} %copy-done.1, bf16[4096,512]{1,0:T(8,128)(2,1)} %refs_1_.9, f32[512,512]{1,0:T(8,128)} %project_own.3.refs_2_, f32[512,128]{1,0:T(8,128)} %get-tuple-element.50.refs_3_, f32[512,128]{1,0:T(8,128)} %get-tuple-element.51.refs_4_), custom_call_target="tpu_custom_call" | custom-call | flops 536870912 | bytes 3145728 | tf_op jit(solution)/shard_map/project_rest/pallas_call | solution.py:140
  58.4 7.8 %project_rest.8.refs_0_ = bf16[16,256,128]{2,1,0:T(8,128)(2,1)} custom-call(s32[1]{0:T(128)} %bitcast.1.rows, bf16[256,2048]{1,0:T(8,128)(2,1)} %copy-done.1, bf16[4096,2048]{1,0:T(8,128)(2,1)} %refs_1_.11, f32[512,2048]{1,0:T(8,128)} %project_own.5.refs_2_, f32[512,128]{1,0:T(8,128)} %get-tuple-element.50.refs_3_, f32[512,128]{1,0:T(8,128)} %get-tuple-element.51.refs_4_), custom_call_target="tpu_custom_call" | custom-call | flops 2147483648 | bytes 12582912 | tf_op jit(solution)/shard_map/project_rest/pallas_call | solution.py:140
  67.2 3.7 %project_rest.9.refs_4_ = bf16[4,256,128]{2,1,0:T(8,128)(2,1)} custom-call(s32[1]{0:T(128)} %bitcast.1.rows, bf16[256,2048]{1,0:T(8,128)(2,1)} %copy-done.2, bf16[4096,512]{1,0:T(8,128)(2,1)} %refs_1_.9, f32[512,512]{1,0:T(8,128)} %project_own.3.refs_2_, f32[512,128]{1,0:T(8,128)} %get-tuple-element.50.refs_3_, f32[512,128]{1,0:T(8,128)} %get-tuple-element.51.refs_4_), custom_call_target="tpu_custom_call" | custom-call | flops 536870912 | bytes 3145728 | tf_op jit(solution)/shard_map/project_rest/pallas_call | solution.py:140
  70.9 3.5 %project_rest.10.refs_6_ = bf16[4,256,128]{2,1,0:T(8,128)(2,1)} custom-call(s32[1]{0:T(128)} %bitcast.1.rows, bf16[256,2048]{1,0:T(8,128)(2,1)} %copy-done.2, bf16[4096,512]{1,0:T(8,128)(2,1)} %refs_1_.10, f32[512,512]{1,0:T(8,128)} %project_own.4.refs_2_, f32[512,128]{1,0:T(8,128)} %get-tuple-element.50.refs_3_, f32[512,128]{1,0:T(8,128)} %get-tuple-element.51.refs_4_), custom_call_target="tpu_custom_call" | custom-call | flops 536870912 | bytes 3145728 | tf_op jit(solution)/shard_map/project_rest/pallas_call | solution.py:140
  74.4 7.8 %project_rest.11.refs_0_ = bf16[16,256,128]{2,1,0:T(8,128)(2,1)} custom-call(s32[1]{0:T(128)} %bitcast.1.rows, bf16[256,2048]{1,0:T(8,128)(2,1)} %copy-done.2, bf16[4096,2048]{1,0:T(8,128)(2,1)} %refs_1_.11, f32[512,2048]{1,0:T(8,128)} %project_own.5.refs_2_, f32[512,128]{1,0:T(8,128)} %get-tuple-element.50.refs_3_, f32[512,128]{1,0:T(8,128)} %get-tuple-element.51.refs_4_), custom_call_target="tpu_custom_call" | custom-call | flops 2147483648 | bytes 12582912 | tf_op jit(solution)/shard_map/project_rest/pallas_call | solution.py:140
  82.2 6.0 %all-to-all-start.1 = ((bf16[16,256,128]{2,1,0:T(8,128)(2,1)}), bf16[16,256,128]{2,1,0:T(8,128)(2,1)S(1)}, u32[]{:S(2)}, u32[]{:S(2)}) async-start(bf16[16,256,128]{2,1,0:T(8,128)(2,1)} %pick_blocks.2), calls=%async_computation.1 | async-start | bytes 2097152 | tf_op jit(solution)/shard_map/all_to_all | solution.py:351
  89.6 11.4 %attend.4.x_ref.refs_5_ = bf16[256,2048]{1,0:T(8,128)(2,1)} custom-call(bf16[16,256,128]{2,1,0:T(8,128)(2,1)} %project_rest.8.refs_0_, bf16[16,776,128]{2,1,0:T(8,128)(2,1)} %all-to-all-done.refs_1_, f32[1,2048]{1,0:T(1,128)} %bitcast_convert_fusion.refs_2_, bf16[4,256,128]{2,1,0:T(8,128)(2,1)} %project_rest.6.refs_3_, ...), custom_call_target="tpu_custom_call" | custom-call | flops 7247757312 | bytes 3145728 | tf_op jit(solution)/shard_map/attend/pallas_call | solution.py:230
  101.0 5.0 %project_out.5.refs_0_ = f32[256,2048]{1,0:T(8,128)} custom-call(s32[1]{0:T(128)} %bitcast.4.cols, bf16[256,2048]{1,0:T(8,128)(2,1)} %attend.4.x_ref.refs_5_, bf16[2048,4096]{1,0:T(8,128)(2,1)} %w_ref.15), custom_call_target="tpu_custom_call" | custom-call | flops 1610612736 | bytes 8388608 | tf_op jit(solution)/shard_map/project_out/pallas_call | solution.py:268
  106.0 6.4 %all-to-all-done.1.refs_1_ = bf16[16,256,128]{2,1,0:T(8,128)(2,1)S(1)} async-done(((bf16[16,256,128]{2,1,0:T(8,128)(2,1)}), bf16[16,256,128]{2,1,0:T(8,128)(2,1)S(1)}, u32[]{:S(2)}, u32[]{:S(2)}) %all-to-all-start.1) | async-done | bytes 1048608 | tf_op jit(solution)/shard_map/all_to_all | solution.py:351
  113.4 5.1 %attend.7.x_ref = bf16[256,2048]{1,0:T(8,128)(2,1)} custom-call(bf16[16,256,128]{2,1,0:T(8,128)(2,1)} %project_rest.8.refs_0_, bf16[16,256,128]{2,1,0:T(8,128)(2,1)} %copy-done.4, f32[1,2048]{1,0:T(1,128)} %bitcast_convert_fusion.refs_2_, bf16[4,256,128]{2,1,0:T(8,128)(2,1)} %project_rest.6.refs_3_, ...), custom_call_target="tpu_custom_call", output_to_operand_aliasing={{}: (5, {})} | custom-call | flops 2415919104 | bytes 1048576 | tf_op jit(solution)/shard_map/attend/pallas_call | solution.py:230
  118.5 3.5 %project_out.8 = bf16[256,2048]{1,0:T(8,128)(2,1)} custom-call(s32[1]{0:T(128)} %bitcast.4.cols, bf16[256,2048]{1,0:T(8,128)(2,1)} %attend.7.x_ref, bf16[2048,4096]{1,0:T(8,128)(2,1)} %w_ref.15, f32[256,2048]{1,0:T(8,128)} %project_out.5.refs_0_), custom_call_target="tpu_custom_call" | custom-call | flops 536870912 | bytes 4194304 | tf_op jit(solution)/shard_map/project_out/pallas_call | solution.py:268
  122.8 12.2 %attend.5.refs_7_ = bf16[256,2048]{1,0:T(8,128)(2,1)} custom-call(bf16[16,256,128]{2,1,0:T(8,128)(2,1)} %project_rest.11.refs_0_, bf16[16,776,128]{2,1,0:T(8,128)(2,1)} %all-to-all-done.refs_1_, f32[1,2048]{1,0:T(1,128)} %bitcast_convert_fusion.refs_2_, bf16[4,256,128]{2,1,0:T(8,128)(2,1)} %project_rest.6.refs_3_, bf16[4,256,128]{2,1,0:T(8,128)(2,1)} %project_rest.9.refs_4_, ...), custom_call_target="tpu_custom_call" | custom-call | flops 8053063680 | bytes 3145728 | tf_op jit(solution)/shard_map/attend/pallas_call | solution.py:230
  134.9 5.4 %attend.6.x_ref = bf16[256,2048]{1,0:T(8,128)(2,1)} custom-call(bf16[16,256,128]{2,1,0:T(8,128)(2,1)} %project_rest.11.refs_0_, bf16[16,256,128]{2,1,0:T(8,128)(2,1)} %copy-done.4, f32[1,2048]{1,0:T(1,128)} %bitcast_convert_fusion.refs_2_, bf16[4,256,128]{2,1,0:T(8,128)(2,1)} %project_rest.6.refs_3_, ...), custom_call_target="tpu_custom_call", output_to_operand_aliasing={{}: (7, {})} | custom-call | flops 2684354560 | bytes 1048576 | tf_op jit(solution)/shard_map/attend/pallas_call | solution.py:230
  140.3 5.8 %project_out.7 = (bf16[128,2048]{1,0:T(8,128)(2,1)}, bf16[128,2048]{1,0:T(8,128)(2,1)}) custom-call(s32[1]{0:T(128)} %bitcast.4.cols, bf16[256,2048]{1,0:T(8,128)(2,1)} %attend.6.x_ref, bf16[2048,4096]{1,0:T(8,128)(2,1)} %w_ref.15), custom_call_target="tpu_custom_call" | custom-call | flops 2147483648 | bytes 10485760 | tf_op jit(solution)/shard_map/project_out/pallas_call | solution.py:268
  150.1 6.0 %project_out.9.refs_0_ = f32[256,2048]{1,0:T(8,128)} custom-call(s32[1]{0:T(128)} %bitcast.rows.cols, bf16[256,2048]{1,0:T(8,128)(2,1)} %attend.7.x_ref, bf16[2048,4096]{1,0:T(8,128)(2,1)} %w_ref.15), custom_call_target="tpu_custom_call" | custom-call | flops 2147483648 | bytes 10485760 | tf_op jit(solution)/shard_map/project_out/pallas_call | solution.py:268
  156.1 6.0 %project_out.6 = (f32[128,2048]{1,0:T(8,128)}, f32[128,2048]{1,0:T(8,128)}) custom-call(s32[1]{0:T(128)} %bitcast.rows.cols, bf16[256,2048]{1,0:T(8,128)(2,1)} %attend.6.x_ref, bf16[2048,4096]{1,0:T(8,128)(2,1)} %w_ref.15), custom_call_target="tpu_custom_call" | custom-call | flops 2147483648 | bytes 10485760 | tf_op jit(solution)/shard_map/project_out/pallas_call | solution.py:268
  167.8 5.5 %collective-permute-done.3.refs_1_ = bf16[128,2048]{1,0:T(8,128)(2,1)S(1)} collective-permute-done((bf16[128,2048]{1,0:T(8,128)(2,1)}, bf16[128,2048]{1,0:T(8,128)(2,1)S(1)}, u32[]{:S(2)}, u32[]{:S(2)}) %collective-permute-start.3) | collective-permute-done | bytes 524320 | tf_op jit(solution)/shard_map/ppermute | solution.py:354
  (37 shorter events, 27.6 us)
Async XLA Ops:
  5.4 6.4 %copy-start = (bf16[512,2048]{1,0:T(8,128)(2,1)S(1)}, bf16[512,2048]{1,0:T(8,128)(2,1)}, u32[]{:S(2)}) copy-start(bf16[512,2048]{1,0:T(8,128)(2,1)} %x_ref.5) | copy-start | bytes 6291460
  5.4 76.8 %all-to-all-start = ((bf16[16,776,128]{2,1,0:T(8,128)(2,1)}), bf16[16,776,128]{2,1,0:T(8,128)(2,1)}, u32[]{:S(2)}, u32[]{:S(2)}) async-start(bf16[16,776,128]{2,1,0:T(8,128)(2,1)} %pick_blocks.3), calls=%async_computation | async-start | bytes 6356992 | tf_op jit(solution)/shard_map/all_to_all | solution.py:351
  11.8 5.1 %copy-start.7 = (s32[16]{0:T(128)S(1)}, s32[16]{0:T(128)}, u32[]{:S(2)}) copy-start(s32[16]{0:T(128)} %lengths.3) | copy-start | bytes 196
  13.0 25.4 %collective-permute-start = (bf16[256,2048]{1,0:T(8,128)(2,1)}, bf16[256,2048]{1,0:T(8,128)(2,1)S(1)}, u32[]{:S(2)}, u32[]{:S(2)}) collective-permute-start(bf16[256,2048]{1,0:T(8,128)(2,1)} %get-tuple-element.45), channel_id=1, source_target_pairs={{0,1},{1,0},{2,3},{3,2},{4,5},{5,4},{6,7},{7,6},{8,9},{9,8},{10,11... | collective-permute-start | bytes 3145736 | tf_op jit(solution)/shard_map/ppermute | solution.py:354
  38.4 12.8 %copy-start.1 = (bf16[256,2048]{1,0:T(8,128)(2,1)}, bf16[256,2048]{1,0:T(8,128)(2,1)S(1)}, u32[]{:S(2)}) copy-start(bf16[256,2048]{1,0:T(8,128)(2,1)S(1)} %collective-permute-done.refs_0_) | copy-start | bytes 3145732
  38.4 27.8 %collective-permute-start.1 = (bf16[256,2048]{1,0:T(8,128)(2,1)S(1)}, bf16[256,2048]{1,0:T(8,128)(2,1)S(1)}, u32[]{:S(2)}, u32[]{:S(2)}) collective-permute-start(bf16[256,2048]{1,0:T(8,128)(2,1)S(1)} %get-tuple-element.26), channel_id=1, source_target_pairs={{0,1},{1,0},{2,3},{3,2},{4,5},{5,4},{6,7},{7,6},{8,9},{9,8},{10,11... | collective-permute-start | bytes 3145736 | tf_op jit(solution)/shard_map/ppermute | solution.py:354
  66.2 1.0 copy-start.2
  82.2 30.2 %all-to-all-start.1 = ((bf16[16,256,128]{2,1,0:T(8,128)(2,1)}), bf16[16,256,128]{2,1,0:T(8,128)(2,1)S(1)}, u32[]{:S(2)}, u32[]{:S(2)}) async-start(bf16[16,256,128]{2,1,0:T(8,128)(2,1)} %pick_blocks.2), calls=%async_computation.1 | async-start | bytes 2097152 | tf_op jit(solution)/shard_map/all_to_all | solution.py:351
  112.4 1.0 copy-start.4
  122.1 26.0 %collective-permute-start.2 = (bf16[256,2048]{1,0:T(8,128)(2,1)}, bf16[256,2048]{1,0:T(8,128)(2,1)S(1)}, u32[]{:S(2)}, u32[]{:S(2)}) collective-permute-start(bf16[256,2048]{1,0:T(8,128)(2,1)} %project_out.8), channel_id=1, source_target_pairs={{0,1},{1,0},{2,3},{3,2},{4,5},{5,4},{6,7},{7,6},{8,9},{9,8},{10,11... | collective-permute-start | bytes 3145736 | tf_op jit(solution)/shard_map/ppermute | solution.py:354
  148.1 8.0 %copy-start.3 = (bf16[256,2048]{1,0:T(8,128)(2,1)}, bf16[256,2048]{1,0:T(8,128)(2,1)S(1)}, u32[]{:S(2)}) copy-start(bf16[256,2048]{1,0:T(8,128)(2,1)S(1)} %collective-permute-done.2.refs_1_) | copy-start | bytes 3145732
  148.1 16.8 %collective-permute-start.4 = (bf16[128,2048]{1,0:T(8,128)(2,1)}, bf16[128,2048]{1,0:T(8,128)(2,1)S(1)}, u32[]{:S(2)}, u32[]{:S(2)}) collective-permute-start(bf16[128,2048]{1,0:T(8,128)(2,1)} %get-tuple-element.43), channel_id=1, source_target_pairs={{0,1},{1,0},{2,3},{3,2},{4,5},{5,4},{6,7},{7,6},{8,9},{9,8},{10,11... | collective-permute-start | bytes 1572872 | tf_op jit(solution)/shard_map/ppermute | solution.py:354
  148.8 24.5 %collective-permute-start.3 = (bf16[128,2048]{1,0:T(8,128)(2,1)}, bf16[128,2048]{1,0:T(8,128)(2,1)S(1)}, u32[]{:S(2)}, u32[]{:S(2)}) collective-permute-start(bf16[128,2048]{1,0:T(8,128)(2,1)} %get-tuple-element.41), channel_id=1, source_target_pairs={{0,1},{1,0},{2,3},{3,2},{4,5},{5,4},{6,7},{7,6},{8,9},{9,8},{10,11... | collective-permute-start | bytes 1572872 | tf_op jit(solution)/shard_map/ppermute | solution.py:354
  164.9 0.8 copy-start.6
  173.3 0.8 copy-start.5

commit v4 on v3

--- a/solution.py
+++ b/solution.py
@@ -289,7 +289,7 @@
             total = total + ref[...].astype(F32)
         refs[-1][...] = total.astype(BF16)
 
-    step = min(1024, width)
+    step = width
     in_specs = [pl.BlockSpec((rows, step), lambda n: (0, n))] * (1 + len(parts))
     operands = [own] + list(parts)
     aliases = {}
@@ -427,14 +427,19 @@
     strips = 2 if tp == 2 else 1
     for shift, target in enumerate(targets):
         parts = project_out(target, attended[1], w_out, width, strips, BF16, features)
-        if shift == 0 and tp == 2:
-            parts, other[0] = lax.optimization_barrier((parts, other[0]))
         other[shift] += [swap(part, shift + 1) for part in parts]
+    if tp == 2:
+        other[0][0], attended = lax.optimization_barrier((other[0][0], attended))
     own = project_out(own_row, attended[0], w_out, width, 1, F32, features)
     own += project_out(own_row, attended[1], w_out, width, strips, F32, features)
     out = None
     row = 0
     for i, part in enumerate(own):
+        if i == len(own) - 1:
+            total = part
+            for arrived in other:
+                total = total + arrived[i].astype(F32)
+            return lax.dynamic_update_slice(out, total.astype(BF16), (row, 0))
         out = combine(part, [arrived[i] for arrived in other], row // part.shape[0], tokens, out)
         row += part.shape[0]
     return out

time: 177 us -> 174 us (0.983)
  waiting for transfers between devices: 25.3 us -> 23.2 us
    ppermute x5, waiting for transfers between devices: 18.9 us -> 16.7 us  [swap(): return lax.ppermute(x, 'tp', [(i, (i + shift) % tp) for i in range(tp)])]
    pallas_call x3 -> x2, Pallas kernels: 6.9 us -> 5.32 us  [combine(): pl.pallas_call(body, grid=(width // step,), in_specs=in_specs, out_specs=...]
  transfers between devices with their start and end apart: 7 -> 7, of which waited for: 4 -> 3; matrix products, arithmetic and copies ran while one was open for 3% -> 3% of each run, Pallas kernels for 61% -> 63%
where the time goes in v4:
time: 174 us; the launch traced here: 173 us
  Pallas kernels  121 us (70%)
  waiting for transfers between devices  23.2 us (13%)
  starting transfers between devices  18.2 us (10%)
  local copies, waits for them, and re-layouts  5.83 us (3%)
  other arithmetic  4.83 us (3%)
    pallas_call x4, Pallas kernels, attend(): pl.pallas_call(body, grid=(count,), in_specs=in_specs, out_specs=pl.Block...  34.1 us
    pallas_call x6, Pallas kernels, project_rest(): pl.pallas_call(body, grid_spec=pltpu.PrefetchScalarGridSpec(num_scalar_pr...  30 us
    pallas_call x5, Pallas kernels, project_out(): pl.pallas_call(body, grid_spec=pltpu.PrefetchScalarGridSpec(num_scalar_pr...  26.7 us
    pallas_call x3, Pallas kernels, project_own(): pl.pallas_call(body, grid_spec=pltpu.PrefetchScalarGridSpec(num_scalar_pr...  18.2 us
    ppermute x5, waiting for transfers between devices, swap(): return lax.ppermute(x, 'tp', [(i, (i + shift) % tp) for i in range(tp)])  16.7 us
    all_to_all x2, starting transfers between devices, exchange(): return lax.all_to_all(block, 'seq', 0, 0, tiled=True)  12.4 us
    pallas_call x2, Pallas kernels, pick_blocks(): pl.pallas_call(body, grid=(1,), in_specs=[pl.BlockSpec(memory_space=pltpu...  6.44 us
    all_to_all x2, waiting for transfers between devices, exchange(): return lax.all_to_all(block, 'seq', 0, 0, tiled=True)  6.42 us
  transfers between devices with their start and end apart: 7, of which 3 were waited for; matrix products, arithmetic and copies ran while one was open for 3% of the time, Pallas kernels for 63%

profile of v4, /device:TPU:8, one launch (start us, length us, event | category | flops | bytes accessed | tf_op | source)
XLA Modules:
  0.0 172.8 jit_solution(3395057643698479718)
XLA Ops:
  1.3 4.1 %pick_blocks.3 = bf16[16,776,128]{2,1,0:T(8,128)(2,1)} custom-call(s32[16,2]{1,0:T(8,128)} %copy.13.table, s32[16]{0:T(128)} %lengths.3, bf16[16,64,512]{2,1,0:T(8,128)(2,1)} %keys.3, bf16[16,64,512]{2,1,0:T(8,128)(2,1)} %values.3), custom_call_target="tpu_custom_call" | custom-call | bytes 6356992 | tf_op jit(solution)/shard_map/pick_blocks/pallas_call | solution.py:71
  5.4 6.4 %all-to-all-start = ((bf16[16,776,128]{2,1,0:T(8,128)(2,1)}), bf16[16,776,128]{2,1,0:T(8,128)(2,1)}, u32[]{:S(2)}, u32[]{:S(2)}) async-start(bf16[16,776,128]{2,1,0:T(8,128)(2,1)} %pick_blocks.3), calls=%async_computation | async-start | bytes 6356992 | tf_op jit(solution)/shard_map/all_to_all | solution.py:351
  17.5 4.5 %project_own.3.refs_2_ = f32[512,512]{1,0:T(8,128)} custom-call(s32[1]{0:T(128)} %bitcast.rows.cols, bf16[512,2048]{1,0:T(8,128)(2,1)} %x_ref.5, bf16[4096,512]{1,0:T(8,128)(2,1)} %refs_1_.9), custom_call_target="tpu_custom_call" | custom-call | flops 1073741824 | bytes 3145728 | tf_op jit(solution)/shard_map/project_own/pallas_call | solution.py:97
  21.9 4.5 %project_own.4.refs_2_ = f32[512,512]{1,0:T(8,128)} custom-call(s32[1]{0:T(128)} %bitcast.rows.cols, bf16[512,2048]{1,0:T(8,128)(2,1)} %x_ref.5, bf16[4096,512]{1,0:T(8,128)(2,1)} %refs_1_.10), custom_call_target="tpu_custom_call" | custom-call | flops 1073741824 | bytes 3145728 | tf_op jit(solution)/shard_map/project_own/pallas_call | solution.py:97
  27.0 11.4 %collective-permute-done.refs_0_ = bf16[256,2048]{1,0:T(8,128)(2,1)S(1)} collective-permute-done((bf16[256,2048]{1,0:T(8,128)(2,1)}, bf16[256,2048]{1,0:T(8,128)(2,1)S(1)}, u32[]{:S(2)}, u32[]{:S(2)}) %collective-permute-start) | collective-permute-done | bytes 1048608 | tf_op jit(solution)/shard_map/ppermute | solution.py:354
  41.9 9.2 %project_own.5.refs_2_ = f32[512,2048]{1,0:T(8,128)} custom-call(s32[1]{0:T(128)} %bitcast.rows.cols, bf16[512,2048]{1,0:T(8,128)(2,1)} %x_ref.5, bf16[4096,2048]{1,0:T(8,128)(2,1)} %refs_1_.11), custom_call_target="tpu_custom_call" | custom-call | flops 4294967296 | bytes 12582912 | tf_op jit(solution)/shard_map/project_own/pallas_call | solution.py:97
  51.2 3.5 %project_rest.7.refs_4_.refs_5_ = bf16[4,256,128]{2,1,0:T(8,128)(2,1)} custom-call(s32[1]{0:T(128)} %bitcast.2.rows, bf16[256,2048]{1,0:T(8,128)(2,1)} %copy-done.1, bf16[4096,512]{1,0:T(8,128)(2,1)} %refs_1_.10, f32[512,512]{1,0:T(8,128)} %project_own.4.refs_2_, f32[512,128]{1,0:T(8,128)} %get-tuple-element.50.refs_3_, f32[512,128]{1,0:T(8,128)} %get-tuple-element.51.refs_4_), custom_call_target="tpu_custom_call" | custom-call | flops 536870912 | bytes 3145728 | tf_op jit(solution)/shard_map/project_rest/pallas_call | solution.py:140
  54.6 3.7 %project_rest.6.refs_3_ = bf16[4,256,128]{2,1,0:T(8,128)(2,1)} custom-call(s32[1]{0:T(128)} %bitcast.2.rows, bf16[256,2048]{1,0:T(8,128)(2,1)} %copy-done.1, bf16[4096,512]{1,0:T(8,128)(2,1)} %refs_1_.9, f32[512,512]{1,0:T(8,128)} %project_own.3.refs_2_, f32[512,128]{1,0:T(8,128)} %get-tuple-element.50.refs_3_, f32[512,128]{1,0:T(8,128)} %get-tuple-element.51.refs_4_), custom_call_target="tpu_custom_call" | custom-call | flops 536870912 | bytes 3145728 | tf_op jit(solution)/shard_map/project_rest/pallas_call | solution.py:140
  58.4 7.8 %project_rest.8.refs_0_ = bf16[16,256,128]{2,1,0:T(8,128)(2,1)} custom-call(s32[1]{0:T(128)} %bitcast.2.rows, bf16[256,2048]{1,0:T(8,128)(2,1)} %copy-done.1, bf16[4096,2048]{1,0:T(8,128)(2,1)} %refs_1_.11, f32[512,2048]{1,0:T(8,128)} %project_own.5.refs_2_, f32[512,128]{1,0:T(8,128)} %get-tuple-element.50.refs_3_, f32[512,128]{1,0:T(8,128)} %get-tuple-element.51.refs_4_), custom_call_target="tpu_custom_call" | custom-call | flops 2147483648 | bytes 12582912 | tf_op jit(solution)/shard_map/project_rest/pallas_call | solution.py:140
  67.2 3.7 %project_rest.9.refs_4_ = bf16[4,256,128]{2,1,0:T(8,128)(2,1)} custom-call(s32[1]{0:T(128)} %bitcast.2.rows, bf16[256,2048]{1,0:T(8,128)(2,1)} %copy-done.2, bf16[4096,512]{1,0:T(8,128)(2,1)} %refs_1_.9, f32[512,512]{1,0:T(8,128)} %project_own.3.refs_2_, f32[512,128]{1,0:T(8,128)} %get-tuple-element.50.refs_3_, f32[512,128]{1,0:T(8,128)} %get-tuple-element.51.refs_4_), custom_call_target="tpu_custom_call" | custom-call | flops 536870912 | bytes 3145728 | tf_op jit(solution)/shard_map/project_rest/pallas_call | solution.py:140
  70.9 3.5 %project_rest.10.refs_6_ = bf16[4,256,128]{2,1,0:T(8,128)(2,1)} custom-call(s32[1]{0:T(128)} %bitcast.2.rows, bf16[256,2048]{1,0:T(8,128)(2,1)} %copy-done.2, bf16[4096,512]{1,0:T(8,128)(2,1)} %refs_1_.10, f32[512,512]{1,0:T(8,128)} %project_own.4.refs_2_, f32[512,128]{1,0:T(8,128)} %get-tuple-element.50.refs_3_, f32[512,128]{1,0:T(8,128)} %get-tuple-element.51.refs_4_), custom_call_target="tpu_custom_call" | custom-call | flops 536870912 | bytes 3145728 | tf_op jit(solution)/shard_map/project_rest/pallas_call | solution.py:140
  74.4 7.8 %project_rest.11.refs_0_ = bf16[16,256,128]{2,1,0:T(8,128)(2,1)} custom-call(s32[1]{0:T(128)} %bitcast.2.rows, bf16[256,2048]{1,0:T(8,128)(2,1)} %copy-done.2, bf16[4096,2048]{1,0:T(8,128)(2,1)} %refs_1_.11, f32[512,2048]{1,0:T(8,128)} %project_own.5.refs_2_, f32[512,128]{1,0:T(8,128)} %get-tuple-element.50.refs_3_, f32[512,128]{1,0:T(8,128)} %get-tuple-element.51.refs_4_), custom_call_target="tpu_custom_call" | custom-call | flops 2147483648 | bytes 12582912 | tf_op jit(solution)/shard_map/project_rest/pallas_call | solution.py:140
  82.2 6.0 %all-to-all-start.1 = ((bf16[16,256,128]{2,1,0:T(8,128)(2,1)}), bf16[16,256,128]{2,1,0:T(8,128)(2,1)S(1)}, u32[]{:S(2)}, u32[]{:S(2)}) async-start(bf16[16,256,128]{2,1,0:T(8,128)(2,1)} %pick_blocks.2), calls=%async_computation.1 | async-start | bytes 2097152 | tf_op jit(solution)/shard_map/all_to_all | solution.py:351
  89.6 11.4 %attend.4.x_ref.refs_5_ = bf16[256,2048]{1,0:T(8,128)(2,1)} custom-call(bf16[16,256,128]{2,1,0:T(8,128)(2,1)} %project_rest.8.refs_0_, bf16[16,776,128]{2,1,0:T(8,128)(2,1)} %all-to-all-done.refs_1_, f32[1,2048]{1,0:T(1,128)} %bitcast_convert_fusion.refs_2_, bf16[4,256,128]{2,1,0:T(8,128)(2,1)} %project_rest.6.refs_3_, ...), custom_call_target="tpu_custom_call" | custom-call | flops 7247757312 | bytes 3145728 | tf_op jit(solution)/shard_map/attend/pallas_call | solution.py:230
  101.0 5.0 %project_out.5.refs_0_ = f32[256,2048]{1,0:T(8,128)} custom-call(s32[1]{0:T(128)} %bitcast.1.cols, bf16[256,2048]{1,0:T(8,128)(2,1)} %attend.4.x_ref.refs_5_, bf16[2048,4096]{1,0:T(8,128)(2,1)} %w_ref.15), custom_call_target="tpu_custom_call" | custom-call | flops 1610612736 | bytes 8388608 | tf_op jit(solution)/shard_map/project_out/pallas_call | solution.py:268
  106.0 6.4 %all-to-all-done.1.refs_1_ = bf16[16,256,128]{2,1,0:T(8,128)(2,1)S(1)} async-done(((bf16[16,256,128]{2,1,0:T(8,128)(2,1)}), bf16[16,256,128]{2,1,0:T(8,128)(2,1)S(1)}, u32[]{:S(2)}, u32[]{:S(2)}) %all-to-all-start.1) | async-done | bytes 1048608 | tf_op jit(solution)/shard_map/all_to_all | solution.py:351
  113.4 5.1 %attend.5.x_ref = bf16[256,2048]{1,0:T(8,128)(2,1)} custom-call(bf16[16,256,128]{2,1,0:T(8,128)(2,1)} %project_rest.8.refs_0_, bf16[16,256,128]{2,1,0:T(8,128)(2,1)} %copy-done.4, f32[1,2048]{1,0:T(1,128)} %bitcast_convert_fusion.refs_2_, bf16[4,256,128]{2,1,0:T(8,128)(2,1)} %project_rest.6.refs_3_, ...), custom_call_target="tpu_custom_call", output_to_operand_aliasing={{}: (5, {})} | custom-call | flops 2415919104 | bytes 1048576 | tf_op jit(solution)/shard_map/attend/pallas_call | solution.py:230
  118.5 3.5 %project_out.6 = bf16[256,2048]{1,0:T(8,128)(2,1)} custom-call(s32[1]{0:T(128)} %bitcast.1.cols, bf16[256,2048]{1,0:T(8,128)(2,1)} %attend.5.x_ref, bf16[2048,4096]{1,0:T(8,128)(2,1)} %w_ref.15, f32[256,2048]{1,0:T(8,128)} %project_out.5.refs_0_), custom_call_target="tpu_custom_call" | custom-call | flops 536870912 | bytes 4194304 | tf_op jit(solution)/shard_map/project_out/pallas_call | solution.py:268
  122.7 12.2 %attend.6.refs_7_ = bf16[256,2048]{1,0:T(8,128)(2,1)} custom-call(bf16[16,256,128]{2,1,0:T(8,128)(2,1)} %project_rest.11.refs_0_, bf16[16,776,128]{2,1,0:T(8,128)(2,1)} %all-to-all-done.refs_1_, f32[1,2048]{1,0:T(1,128)} %bitcast_convert_fusion.refs_2_, bf16[4,256,128]{2,1,0:T(8,128)(2,1)} %project_rest.6.refs_3_, bf16[4,256,128]{2,1,0:T(8,128)(2,1)} %project_rest.9.refs_4_, ...), custom_call_target="tpu_custom_call" | custom-call | flops 8053063680 | bytes 3145728 | tf_op jit(solution)/shard_map/attend/pallas_call | solution.py:230
  134.9 5.4 %attend.7.x_ref = bf16[256,2048]{1,0:T(8,128)(2,1)} custom-call(bf16[16,256,128]{2,1,0:T(8,128)(2,1)} %project_rest.11.refs_0_, bf16[16,256,128]{2,1,0:T(8,128)(2,1)} %copy-done.4, f32[1,2048]{1,0:T(1,128)} %bitcast_convert_fusion.refs_2_, bf16[4,256,128]{2,1,0:T(8,128)(2,1)} %project_rest.6.refs_3_, ...), custom_call_target="tpu_custom_call", output_to_operand_aliasing={{}: (7, {})} | custom-call | flops 2684354560 | bytes 1048576 | tf_op jit(solution)/shard_map/attend/pallas_call | solution.py:230
  140.3 5.8 %project_out.8 = (bf16[128,2048]{1,0:T(8,128)(2,1)}, bf16[128,2048]{1,0:T(8,128)(2,1)}) custom-call(s32[1]{0:T(128)} %bitcast.1.cols, bf16[256,2048]{1,0:T(8,128)(2,1)} %attend.7.x_ref, bf16[2048,4096]{1,0:T(8,128)(2,1)} %w_ref.15), custom_call_target="tpu_custom_call" | custom-call | flops 2147483648 | bytes 10485760 | tf_op jit(solution)/shard_map/project_out/pallas_call | solution.py:268
  148.2 6.4 %project_out.9.refs_0_ = f32[256,2048]{1,0:T(8,128)} custom-call(s32[1]{0:T(128)} %bitcast.rows.cols, bf16[256,2048]{1,0:T(8,128)(2,1)} %attend.5.x_ref, bf16[2048,4096]{1,0:T(8,128)(2,1)} %w_ref.15), custom_call_target="tpu_custom_call" | custom-call | flops 2147483648 | bytes 10485760 | tf_op jit(solution)/shard_map/project_out/pallas_call | solution.py:268
  157.6 5.9 %project_out.7 = (f32[128,2048]{1,0:T(8,128)}, f32[128,2048]{1,0:T(8,128)}) custom-call(s32[1]{0:T(128)} %bitcast.rows.cols, bf16[256,2048]{1,0:T(8,128)(2,1)} %attend.7.x_ref, bf16[2048,4096]{1,0:T(8,128)(2,1)} %w_ref.15), custom_call_target="tpu_custom_call" | custom-call | flops 2147483648 | bytes 10485760 | tf_op jit(solution)/shard_map/project_out/pallas_call | solution.py:268
  166.6 5.3 %collective-permute-done.4 = bf16[128,2048]{1,0:T(8,128)(2,1)S(1)} collective-permute-done((bf16[128,2048]{1,0:T(8,128)(2,1)}, bf16[128,2048]{1,0:T(8,128)(2,1)S(1)}, u32[]{:S(2)}, u32[]{:S(2)}) %collective-permute-start.4) | collective-permute-done | bytes 524320 | tf_op jit(solution)/shard_map/ppermute | solution.py:354
  (37 shorter events, 24.2 us)
Async XLA Ops:
  5.4 6.4 %copy-start = (bf16[512,2048]{1,0:T(8,128)(2,1)S(1)}, bf16[512,2048]{1,0:T(8,128)(2,1)}, u32[]{:S(2)}) copy-start(bf16[512,2048]{1,0:T(8,128)(2,1)} %x_ref.5) | copy-start | bytes 6291460
  5.4 76.8 %all-to-all-start = ((bf16[16,776,128]{2,1,0:T(8,128)(2,1)}), bf16[16,776,128]{2,1,0:T(8,128)(2,1)}, u32[]{:S(2)}, u32[]{:S(2)}) async-start(bf16[16,776,128]{2,1,0:T(8,128)(2,1)} %pick_blocks.3), calls=%async_computation | async-start | bytes 6356992 | tf_op jit(solution)/shard_map/all_to_all | solution.py:351
  13.0 3.9 %copy-start.7 = (s32[16]{0:T(128)S(1)}, s32[16]{0:T(128)}, u32[]{:S(2)}) copy-start(s32[16]{0:T(128)} %lengths.3) | copy-start | bytes 196
  13.0 25.4 %collective-permute-start = (bf16[256,2048]{1,0:T(8,128)(2,1)}, bf16[256,2048]{1,0:T(8,128)(2,1)S(1)}, u32[]{:S(2)}, u32[]{:S(2)}) collective-permute-start(bf16[256,2048]{1,0:T(8,128)(2,1)} %get-tuple-element.45), channel_id=1, source_target_pairs={{0,1},{1,0},{2,3},{3,2},{4,5},{5,4},{6,7},{7,6},{8,9},{9,8},{10,11... | collective-permute-start | bytes 3145736 | tf_op jit(solution)/shard_map/ppermute | solution.py:354
  38.4 12.8 %copy-start.1 = (bf16[256,2048]{1,0:T(8,128)(2,1)}, bf16[256,2048]{1,0:T(8,128)(2,1)S(1)}, u32[]{:S(2)}) copy-start(bf16[256,2048]{1,0:T(8,128)(2,1)S(1)} %collective-permute-done.refs_0_) | copy-start | bytes 3145732
  38.4 27.8 %collective-permute-start.1 = (bf16[256,2048]{1,0:T(8,128)(2,1)S(1)}, bf16[256,2048]{1,0:T(8,128)(2,1)S(1)}, u32[]{:S(2)}, u32[]{:S(2)}) collective-permute-start(bf16[256,2048]{1,0:T(8,128)(2,1)S(1)} %get-tuple-element.26), channel_id=1, source_target_pairs={{0,1},{1,0},{2,3},{3,2},{4,5},{5,4},{6,7},{7,6},{8,9},{9,8},{10,11... | collective-permute-start | bytes 3145736 | tf_op jit(solution)/shard_map/ppermute | solution.py:354
  66.2 1.0 copy-start.2
  82.2 30.2 %all-to-all-start.1 = ((bf16[16,256,128]{2,1,0:T(8,128)(2,1)}), bf16[16,256,128]{2,1,0:T(8,128)(2,1)S(1)}, u32[]{:S(2)}, u32[]{:S(2)}) async-start(bf16[16,256,128]{2,1,0:T(8,128)(2,1)} %pick_blocks.2), calls=%async_computation.1 | async-start | bytes 2097152 | tf_op jit(solution)/shard_map/all_to_all | solution.py:351
  112.4 1.0 copy-start.4
  122.0 26.2 %collective-permute-start.2 = (bf16[256,2048]{1,0:T(8,128)(2,1)}, bf16[256,2048]{1,0:T(8,128)(2,1)S(1)}, u32[]{:S(2)}, u32[]{:S(2)}) collective-permute-start(bf16[256,2048]{1,0:T(8,128)(2,1)} %project_out.6), channel_id=1, source_target_pairs={{0,1},{1,0},{2,3},{3,2},{4,5},{5,4},{6,7},{7,6},{8,9},{9,8},{10,11... | collective-permute-start | bytes 3145736 | tf_op jit(solution)/shard_map/ppermute | solution.py:354
  146.2 17.4 %collective-permute-start.3 = (bf16[128,2048]{1,0:T(8,128)(2,1)}, bf16[128,2048]{1,0:T(8,128)(2,1)S(1)}, u32[]{:S(2)}, u32[]{:S(2)}) collective-permute-start(bf16[128,2048]{1,0:T(8,128)(2,1)} %get-tuple-element.40), channel_id=1, source_target_pairs={{0,1},{1,0},{2,3},{3,2},{4,5},{5,4},{6,7},{7,6},{8,9},{9,8},{10,11... | collective-permute-start | bytes 1572872 | tf_op jit(solution)/shard_map/ppermute | solution.py:354
  147.5 24.5 %collective-permute-start.4 = (bf16[128,2048]{1,0:T(8,128)(2,1)}, bf16[128,2048]{1,0:T(8,128)(2,1)S(1)}, u32[]{:S(2)}, u32[]{:S(2)}) collective-permute-start(bf16[128,2048]{1,0:T(8,128)(2,1)} %get-tuple-element.44), channel_id=1, source_target_pairs={{0,1},{1,0},{2,3},{3,2},{4,5},{5,4},{6,7},{7,6},{8,9},{9,8},{10,11... | collective-permute-start | bytes 1572872 | tf_op jit(solution)/shard_map/ppermute | solution.py:354
  148.2 6.4 %copy-start.3 = (bf16[256,2048]{1,0:T(8,128)(2,1)}, bf16[256,2048]{1,0:T(8,128)(2,1)S(1)}, u32[]{:S(2)}) copy-start(bf16[256,2048]{1,0:T(8,128)(2,1)S(1)} %collective-permute-done.2.refs_1_) | copy-start | bytes 3145732
  163.5 0.8 copy-start.6
  164.3 7.6 %copy-start.5 = (f32[128,2048]{1,0:T(8,128)S(1)}, f32[128,2048]{1,0:T(8,128)}, u32[]{:S(2)}) copy-start(f32[128,2048]{1,0:T(8,128)} %get-tuple-element.43) | copy-start | bytes 3145732

commit v5 on v4

--- a/solution.py
+++ b/solution.py
@@ -12,7 +12,7 @@
 CTX = 2048
 ROPE_BASE = 1000000.0
 masked_score = -1e30
-VMEM_LIMIT = 56 * 1024 * 1024
+VMEM_LIMIT = 40 * 1024 * 1024
 BF16 = jnp.bfloat16
 F32 = jnp.float32
 

time: 174 us -> 173 us (level)
  Pallas kernels: 121 us -> 84.1 us
  waiting for transfers between devices: 23.2 us -> 46.4 us
  local copies, waits for them, and re-layouts: 5.83 us -> 17.9 us
    pallas_call x6, Pallas kernels: 30 us -> 16.4 us  [project_rest(): pl.pallas_call(body, grid_spec=pltpu.PrefetchScalarGridSpec(num_scalar_pr...]
    ppermute x5, waiting for transfers between devices: 16.7 us -> 29.3 us  [swap(): return lax.ppermute(x, 'tp', [(i, (i + shift) % tp) for i in range(tp)])]
    unnamed x17 -> x49, local copies, waits for them, and re-layouts: 4.09 us -> 15.8 us
    all_to_all x2, waiting for transfers between devices: 6.42 us -> 17.2 us  [exchange(): return lax.all_to_all(block, 'seq', 0, 0, tiled=True)]
    pallas_call x3, Pallas kernels: 18.2 us -> 9.7 us  [project_own(): pl.pallas_call(body, grid_spec=pltpu.PrefetchScalarGridSpec(num_scalar_pr...]
    pallas_call x5, Pallas kernels: 26.7 us -> 20.8 us  [project_out(): pl.pallas_call(body, grid_spec=pltpu.PrefetchScalarGridSpec(num_scalar_pr...]
    pallas_call x2, Pallas kernels: 5.32 us -> 2.13 us  [combine(): pl.pallas_call(body, grid=(width // step,), in_specs=in_specs, out_specs=...]
    pallas_call x2, Pallas kernels: 6.44 us -> 3.56 us  [pick_blocks(): pl.pallas_call(body, grid=(1,), in_specs=[pl.BlockSpec(memory_space=pltpu...]
  transfers between devices with their start and end apart: 7 -> 7, of which waited for: 3 -> 7; matrix products, arithmetic and copies ran while one was open for 3% -> 3% of each run, Pallas kernels for 63% -> 44%
where the time goes in v5:
time: 173 us; the launch traced here: 172 us
  Pallas kernels  84.1 us (49%)
  waiting for transfers between devices  46.4 us (27%)
  starting transfers between devices  19.7 us (11%)
  local copies, waits for them, and re-layouts  17.9 us (10%)
  other arithmetic  3.42 us (2%)
    pallas_call x4, Pallas kernels, attend(): pl.pallas_call(body, grid=(count,), in_specs=in_specs, out_specs=pl.Block...  31.4 us
    ppermute x5, waiting for transfers between devices, swap(): return lax.ppermute(x, 'tp', [(i, (i + shift) % tp) for i in range(tp)])  29.3 us
    pallas_call x5, Pallas kernels, project_out(): pl.pallas_call(body, grid_spec=pltpu.PrefetchScalarGridSpec(num_scalar_pr...  20.8 us
    all_to_all x2, waiting for transfers between devices, exchange(): return lax.all_to_all(block, 'seq', 0, 0, tiled=True)  17.2 us
    pallas_call x6, Pallas kernels, project_rest(): pl.pallas_call(body, grid_spec=pltpu.PrefetchScalarGridSpec(num_scalar_pr...  16.4 us
    unnamed x49, local copies, waits for them, and re-layouts  15.8 us
    all_to_all x2, starting transfers between devices, exchange(): return lax.all_to_all(block, 'seq', 0, 0, tiled=True)  13 us
    pallas_call x3, Pallas kernels, project_own(): pl.pallas_call(body, grid_spec=pltpu.PrefetchScalarGridSpec(num_scalar_pr...  9.7 us
  transfers between devices with their start and end apart: 7, of which 7 were waited for; matrix products, arithmetic and copies ran while one was open for 3% of the time, Pallas kernels for 44%

profile of v5, /device:TPU:8, one launch (start us, length us, event | category | flops | bytes accessed | tf_op | source)
XLA Modules:
  0.0 171.8 jit_solution(17024308010576773310)
XLA Ops:
  3.9 1.6 pick_blocks.3
  5.5 1.7 copy-done.4
  7.1 6.4 %all-to-all-start = ((bf16[16,776,128]{2,1,0:T(8,128)(2,1)}), bf16[16,776,128]{2,1,0:T(8,128)(2,1)}, u32[]{:S(2)}, u32[]{:S(2)}) async-start(bf16[16,776,128]{2,1,0:T(8,128)(2,1)} %copy-done.4), calls=%async_computation | async-start | bytes 6356992 | tf_op jit(solution)/shard_map/all_to_all | solution.py:351
  19.1 2.0 %pick_blocks.2 = bf16[16,256,128]{2,1,0:T(8,128)(2,1)} custom-call(s32[16,2]{1,0:T(8,128)S(1)} %copy.13.table, s32[16]{0:T(128)S(1)} %copy-done.22, bf16[16,64,512]{2,1,0:T(8,128)(2,1)S(1)} %copy-done.6, bf16[16,64,512]{2,1,0:T(8,128)(2,1)S(1)} %copy-done.8), custom_call_target="tpu_custom_call" | custom-call | bytes 2097152 | tf_op jit(solution)/shard_map/pick_blocks/pallas_call | solution.py:71
  21.7 2.2 %copy-done = bf16[4096,512]{1,0:T(8,128)(2,1)S(1)} copy-done((bf16[4096,512]{1,0:T(8,128)(2,1)S(1)}, bf16[4096,512]{1,0:T(8,128)(2,1)}, u32[]{:S(2)}) %copy-start) | copy-done | bytes 4194328
  27.8 12.7 %collective-permute-done.refs_0_ = bf16[256,2048]{1,0:T(8,128)(2,1)S(1)} collective-permute-done((bf16[256,2048]{1,0:T(8,128)(2,1)}, bf16[256,2048]{1,0:T(8,128)(2,1)S(1)}, u32[]{:S(2)}, u32[]{:S(2)}) %collective-permute-start) | collective-permute-done | bytes 1048608 | tf_op jit(solution)/shard_map/ppermute | solution.py:354
  43.3 7.2 %project_own.5.refs_2_ = f32[512,2048]{1,0:T(8,128)S(1)} custom-call(s32[1]{0:T(128)} %bitcast.rows.cols, bf16[512,2048]{1,0:T(8,128)(2,1)S(1)} %copy-done.3, bf16[4096,2048]{1,0:T(8,128)(2,1)} %refs_1_.11), custom_call_target="tpu_custom_call" | custom-call | flops 4294967296 | bytes 12582912 | tf_op jit(solution)/shard_map/project_own/pallas_call | solution.py:97
  53.7 6.5 %project_rest.8.refs_0_ = bf16[16,256,128]{2,1,0:T(8,128)(2,1)S(1)} custom-call(s32[1]{0:T(128)} %bitcast.2.rows, bf16[256,2048]{1,0:T(8,128)(2,1)S(1)} %collective-permute-done.refs_0_, bf16[4096,2048]{1,0:T(8,128)(2,1)} %refs_1_.11, f32[512,2048]{1,0:T(8,128)S(1)} %project_own.5.refs_2_, f32[512,128]{1,0:T(8,128)S(1)} %get-tuple-element.50.refs_3_, ...), custom_call_target="tpu_custom_call" | custom-call | flops 2147483648 | bytes 12582912 | tf_op jit(solution)/shard_map/project_rest/pallas_call | solution.py:140
  60.2 4.8 %collective-permute-done.1.refs_0_ = bf16[256,2048]{1,0:T(8,128)(2,1)S(1)} collective-permute-done((bf16[256,2048]{1,0:T(8,128)(2,1)S(1)}, bf16[256,2048]{1,0:T(8,128)(2,1)S(1)}, u32[]{:S(2)}, u32[]{:S(2)}) %collective-permute-start.1) | collective-permute-done | bytes 1048608 | tf_op jit(solution)/shard_map/ppermute | solution.py:354
  66.8 6.5 %project_rest.11.refs_0_ = bf16[16,256,128]{2,1,0:T(8,128)(2,1)S(1)} custom-call(s32[1]{0:T(128)} %bitcast.2.rows, bf16[256,2048]{1,0:T(8,128)(2,1)S(1)} %collective-permute-done.1.refs_0_, bf16[4096,2048]{1,0:T(8,128)(2,1)} %refs_1_.11, f32[512,2048]{1,0:T(8,128)S(1)} %project_own.5.refs_2_, f32[512,128]{1,0:T(8,128)S(1)} %get-tuple-element.50.refs_3_, ...), custom_call_target="tpu_custom_call" | custom-call | flops 2147483648 | bytes 12582912 | tf_op jit(solution)/shard_map/project_rest/pallas_call | solution.py:140
  74.3 8.3 %all-to-all-done.refs_1_ = bf16[16,776,128]{2,1,0:T(8,128)(2,1)} async-done(((bf16[16,776,128]{2,1,0:T(8,128)(2,1)}), bf16[16,776,128]{2,1,0:T(8,128)(2,1)}, u32[]{:S(2)}, u32[]{:S(2)}) %all-to-all-start) | async-done | bytes 3178528 | tf_op jit(solution)/shard_map/all_to_all | solution.py:351
  82.6 6.6 %all-to-all-start.1 = ((bf16[16,256,128]{2,1,0:T(8,128)(2,1)}), bf16[16,256,128]{2,1,0:T(8,128)(2,1)}, u32[]{:S(2)}, u32[]{:S(2)}) async-start(bf16[16,256,128]{2,1,0:T(8,128)(2,1)} %pick_blocks.2), calls=%async_computation.1 | async-start | bytes 2097152 | tf_op jit(solution)/shard_map/all_to_all | solution.py:351
  89.9 10.6 %attend.4.x_ref.refs_5_ = bf16[256,2048]{1,0:T(8,128)(2,1)S(1)} custom-call(bf16[16,256,128]{2,1,0:T(8,128)(2,1)S(1)} %project_rest.8.refs_0_, bf16[16,776,128]{2,1,0:T(8,128)(2,1)} %all-to-all-done.refs_1_, f32[1,2048]{1,0:T(1,128)S(1)} %bitcast_convert_fusion.refs_2_, bf16[4,256,128]{2,1,0:T(8,128)(2,1)S(1)} %copy-done.14, ...), custom_call_target="tpu_custom_call" | custom-call | flops 7247757312 | bytes 3145728 | tf_op jit(solution)/shard_map/attend/pallas_call | solution.py:230
  100.6 4.0 %project_out.5.refs_0_ = f32[256,2048]{1,0:T(8,128)S(1)} custom-call(s32[1]{0:T(128)} %bitcast.1.cols, bf16[256,2048]{1,0:T(8,128)(2,1)S(1)} %attend.4.x_ref.refs_5_, bf16[2048,4096]{1,0:T(8,128)(2,1)} %w_ref.15), custom_call_target="tpu_custom_call" | custom-call | flops 1610612736 | bytes 8388608 | tf_op jit(solution)/shard_map/project_out/pallas_call | solution.py:268
  104.6 8.9 %all-to-all-done.1.refs_1_ = bf16[16,256,128]{2,1,0:T(8,128)(2,1)} async-done(((bf16[16,256,128]{2,1,0:T(8,128)(2,1)}), bf16[16,256,128]{2,1,0:T(8,128)(2,1)}, u32[]{:S(2)}, u32[]{:S(2)}) %all-to-all-start.1) | async-done | bytes 1048608 | tf_op jit(solution)/shard_map/all_to_all | solution.py:351
  115.7 4.3 %attend.5.x_ref = bf16[256,2048]{1,0:T(8,128)(2,1)S(1)} custom-call(bf16[16,256,128]{2,1,0:T(8,128)(2,1)S(1)} %copy-done.12, bf16[16,256,128]{2,1,0:T(8,128)(2,1)} %all-to-all-done.1.refs_1_, f32[1,2048]{1,0:T(1,128)S(1)} %bitcast_convert_fusion.refs_2_, bf16[4,256,128]{2,1,0:T(8,128)(2,1)S(1)} %copy-done.15, ...), custom_call_target="tpu_custom_call", output_to_operand_aliasing={{}: (5, {})} | custom-call | flops 2415919104 | bytes 1048576 | tf_op jit(solution)/shard_map/attend/pallas_call | solution.py:230
  120.1 2.4 %project_out.6 = bf16[256,2048]{1,0:T(8,128)(2,1)S(1)} custom-call(s32[1]{0:T(128)} %bitcast.1.cols, bf16[256,2048]{1,0:T(8,128)(2,1)S(1)} %attend.5.x_ref, bf16[2048,4096]{1,0:T(8,128)(2,1)} %w_ref.15, f32[256,2048]{1,0:T(8,128)S(1)} %project_out.5.refs_0_), custom_call_target="tpu_custom_call" | custom-call | flops 536870912 | bytes 4194304 | tf_op jit(solution)/shard_map/project_out/pallas_call | solution.py:268
  122.4 1.6 collective-permute-start.2
  124.0 11.8 %attend.6.refs_7_ = bf16[256,2048]{1,0:T(8,128)(2,1)S(1)} custom-call(bf16[16,256,128]{2,1,0:T(8,128)(2,1)S(1)} %copy-done.10, bf16[16,776,128]{2,1,0:T(8,128)(2,1)} %all-to-all-done.refs_1_, f32[1,2048]{1,0:T(1,128)S(1)} %bitcast_convert_fusion.refs_2_, bf16[4,256,128]{2,1,0:T(8,128)(2,1)S(1)} %copy-done.16, bf16[4,256,128]{2,1,0:T(8,128)(2,1)S(1)} %copy-done.18, ...), custom_call_target="tpu_custom_call" | custom-call | flops 8053063680 | bytes 3145728 | tf_op jit(solution)/shard_map/attend/pallas_call | solution.py:230
  135.8 4.7 %attend.7.x_ref = bf16[256,2048]{1,0:T(8,128)(2,1)S(1)} custom-call(bf16[16,256,128]{2,1,0:T(8,128)(2,1)S(1)} %copy-done.10, bf16[16,256,128]{2,1,0:T(8,128)(2,1)} %all-to-all-done.1.refs_1_, f32[1,2048]{1,0:T(1,128)S(1)} %bitcast_convert_fusion.refs_2_, bf16[4,256,128]{2,1,0:T(8,128)(2,1)S(1)} %copy-done.16, ...), custom_call_target="tpu_custom_call", output_to_operand_aliasing={{}: (7, {})} | custom-call | flops 2684354560 | bytes 1048576 | tf_op jit(solution)/shard_map/attend/pallas_call | solution.py:230
  140.5 4.8 %project_out.8 = (bf16[128,2048]{1,0:T(8,128)(2,1)S(1)}, bf16[128,2048]{1,0:T(8,128)(2,1)S(1)}) custom-call(s32[1]{0:T(128)} %bitcast.1.cols, bf16[256,2048]{1,0:T(8,128)(2,1)S(1)} %attend.7.x_ref, bf16[2048,4096]{1,0:T(8,128)(2,1)} %w_ref.15), custom_call_target="tpu_custom_call" | custom-call | flops 2147483648 | bytes 10485760 | tf_op jit(solution)/shard_map/project_out/pallas_call | solution.py:268
  148.3 4.8 %project_out.9.refs_0_ = f32[256,2048]{1,0:T(8,128)S(1)} custom-call(s32[1]{0:T(128)} %bitcast.rows.cols, bf16[256,2048]{1,0:T(8,128)(2,1)S(1)} %attend.5.x_ref, bf16[2048,4096]{1,0:T(8,128)(2,1)} %w_ref.15), custom_call_target="tpu_custom_call" | custom-call | flops 2147483648 | bytes 10485760 | tf_op jit(solution)/shard_map/project_out/pallas_call | solution.py:268
  154.4 4.8 %project_out.7 = (f32[128,2048]{1,0:T(8,128)S(1)}, f32[128,2048]{1,0:T(8,128)S(1)}) custom-call(s32[1]{0:T(128)} %bitcast.rows.cols, bf16[256,2048]{1,0:T(8,128)(2,1)S(1)} %attend.7.x_ref, bf16[2048,4096]{1,0:T(8,128)(2,1)} %w_ref.15), custom_call_target="tpu_custom_call" | custom-call | flops 2147483648 | bytes 10485760 | tf_op jit(solution)/shard_map/project_out/pallas_call | solution.py:268
  161.0 9.9 %collective-permute-done.4 = bf16[128,2048]{1,0:T(8,128)(2,1)S(1)} collective-permute-done((bf16[128,2048]{1,0:T(8,128)(2,1)S(1)}, bf16[128,2048]{1,0:T(8,128)(2,1)S(1)}, u32[]{:S(2)}, u32[]{:S(2)}) %collective-permute-start.4) | collective-permute-done | bytes 524320 | tf_op jit(solution)/shard_map/ppermute | solution.py:354
  (69 shorter events, 32.4 us)
Async XLA Ops:
  5.4 1.7 copy-start.4
  7.1 6.4 %copy-start.3 = (bf16[512,2048]{1,0:T(8,128)(2,1)S(1)}, bf16[512,2048]{1,0:T(8,128)(2,1)}, u32[]{:S(2)}) copy-start(bf16[512,2048]{1,0:T(8,128)(2,1)} %x_ref.5) | copy-start | bytes 6291460
  7.1 75.5 %all-to-all-start = ((bf16[16,776,128]{2,1,0:T(8,128)(2,1)}), bf16[16,776,128]{2,1,0:T(8,128)(2,1)}, u32[]{:S(2)}, u32[]{:S(2)}) async-start(bf16[16,776,128]{2,1,0:T(8,128)(2,1)} %copy-done.4), calls=%async_computation | async-start | bytes 6356992 | tf_op jit(solution)/shard_map/all_to_all | solution.py:351
  13.6 3.1 %copy-start.22 = (s32[16]{0:T(128)S(1)}, s32[16]{0:T(128)}, u32[]{:S(2)}) copy-start(s32[16]{0:T(128)} %lengths.3) | copy-start | bytes 196
  15.1 25.4 %collective-permute-start = (bf16[256,2048]{1,0:T(8,128)(2,1)}, bf16[256,2048]{1,0:T(8,128)(2,1)S(1)}, u32[]{:S(2)}, u32[]{:S(2)}) collective-permute-start(bf16[256,2048]{1,0:T(8,128)(2,1)} %get-tuple-element.45), channel_id=1, source_target_pairs={{0,1},{1,0},{2,3},{3,2},{4,5},{5,4},{6,7},{7,6},{8,9},{9,8},{10,11... | collective-permute-start | bytes 3145736 | tf_op jit(solution)/shard_map/ppermute | solution.py:354
  16.7 1.2 copy-start.6
  21.6 2.2 %copy-start = (bf16[4096,512]{1,0:T(8,128)(2,1)S(1)}, bf16[4096,512]{1,0:T(8,128)(2,1)}, u32[]{:S(2)}) copy-start(bf16[4096,512]{1,0:T(8,128)(2,1)} %refs_1_.9) | copy-start | bytes 12582916
  23.8 2.2 %copy-start.2 = (bf16[4096,512]{1,0:T(8,128)(2,1)S(1)}, bf16[4096,512]{1,0:T(8,128)(2,1)}, u32[]{:S(2)}) copy-start(bf16[4096,512]{1,0:T(8,128)(2,1)} %refs_1_.10) | copy-start | bytes 12582916
  26.0 14.5 %copy-start.23 = (bf16[256,2048]{1,0:T(8,128)(2,1)S(1)}, bf16[256,2048]{1,0:T(8,128)(2,1)}, u32[]{:S(2)}) copy-start(bf16[256,2048]{1,0:T(8,128)(2,1)} %get-tuple-element.26) | copy-start | bytes 3145732
  40.6 24.5 %collective-permute-start.1 = (bf16[256,2048]{1,0:T(8,128)(2,1)S(1)}, bf16[256,2048]{1,0:T(8,128)(2,1)S(1)}, u32[]{:S(2)}, u32[]{:S(2)}) collective-permute-start(bf16[256,2048]{1,0:T(8,128)(2,1)S(1)} %copy-done.23), channel_id=1, source_target_pairs={{0,1},{1,0},{2,3},{3,2},{4,5},{5,4},{6,7},{7,6},{8,9},{9,8},{10,11... | collective-permute-start | bytes 3145736 | tf_op jit(solution)/shard_map/ppermute | solution.py:354
  50.5 2.2 %copy-start.1 = (bf16[4096,512]{1,0:T(8,128)(2,1)S(1)}, bf16[4096,512]{1,0:T(8,128)(2,1)}, u32[]{:S(2)}) copy-start(bf16[4096,512]{1,0:T(8,128)(2,1)} %refs_1_.9) | copy-start | bytes 12582916
  53.7 6.5 %copy-start.13 = (bf16[4,256,128]{2,1,0:T(8,128)(2,1)}, bf16[4,256,128]{2,1,0:T(8,128)(2,1)S(1)}, u32[]{:S(2)}) copy-start(bf16[4,256,128]{2,1,0:T(8,128)(2,1)S(1)} %project_rest.6.refs_3_) | copy-start | bytes 786436
  60.2 29.7 %copy-start.11 = (bf16[16,256,128]{2,1,0:T(8,128)(2,1)}, bf16[16,256,128]{2,1,0:T(8,128)(2,1)S(1)}, u32[]{:S(2)}) copy-start(bf16[16,256,128]{2,1,0:T(8,128)(2,1)S(1)} %project_rest.8.refs_0_) | copy-start | bytes 3145732
  66.8 6.5 %copy-start.19 = (bf16[4,256,128]{2,1,0:T(8,128)(2,1)}, bf16[4,256,128]{2,1,0:T(8,128)(2,1)S(1)}, u32[]{:S(2)}) copy-start(bf16[4,256,128]{2,1,0:T(8,128)(2,1)S(1)} %project_rest.10.refs_6_) | copy-start | bytes 786436
  74.3 15.6 %copy-start.14 = (bf16[4,256,128]{2,1,0:T(8,128)(2,1)S(1)}, bf16[4,256,128]{2,1,0:T(8,128)(2,1)}, u32[]{:S(2)}) copy-start(bf16[4,256,128]{2,1,0:T(8,128)(2,1)} %copy-done.13) | copy-start | bytes 786436
  82.6 30.9 %all-to-all-start.1 = ((bf16[16,256,128]{2,1,0:T(8,128)(2,1)}), bf16[16,256,128]{2,1,0:T(8,128)(2,1)}, u32[]{:S(2)}, u32[]{:S(2)}) async-start(bf16[16,256,128]{2,1,0:T(8,128)(2,1)} %pick_blocks.2), calls=%async_computation.1 | async-start | bytes 2097152 | tf_op jit(solution)/shard_map/all_to_all | solution.py:351
  113.5 1.2 copy-start.12
  120.0 4.0 %copy-start.10 = (bf16[16,256,128]{2,1,0:T(8,128)(2,1)S(1)}, bf16[16,256,128]{2,1,0:T(8,128)(2,1)}, u32[]{:S(2)}) copy-start(bf16[16,256,128]{2,1,0:T(8,128)(2,1)} %copy-done.9) | copy-start | bytes 3145732
  120.0 4.0 %copy-start.16 = (bf16[4,256,128]{2,1,0:T(8,128)(2,1)S(1)}, bf16[4,256,128]{2,1,0:T(8,128)(2,1)}, u32[]{:S(2)}) copy-start(bf16[4,256,128]{2,1,0:T(8,128)(2,1)} %copy-done.13) | copy-start | bytes 786436
  120.0 4.0 %copy-start.18 = (bf16[4,256,128]{2,1,0:T(8,128)(2,1)S(1)}, bf16[4,256,128]{2,1,0:T(8,128)(2,1)}, u32[]{:S(2)}) copy-start(bf16[4,256,128]{2,1,0:T(8,128)(2,1)} %copy-done.17) | copy-start | bytes 786436
  120.1 4.0 %copy-start.20 = (bf16[4,256,128]{2,1,0:T(8,128)(2,1)S(1)}, bf16[4,256,128]{2,1,0:T(8,128)(2,1)}, u32[]{:S(2)}) copy-start(bf16[4,256,128]{2,1,0:T(8,128)(2,1)} %copy-done.19) | copy-start | bytes 786436
  122.4 25.9 %collective-permute-start.2 = (bf16[256,2048]{1,0:T(8,128)(2,1)S(1)}, bf16[256,2048]{1,0:T(8,128)(2,1)S(1)}, u32[]{:S(2)}, u32[]{:S(2)}) collective-permute-start(bf16[256,2048]{1,0:T(8,128)(2,1)S(1)} %project_out.6), channel_id=1, source_target_pairs={{0,1},{1,0},{2,3},{3,2},{4,5},{5,4},{6,7},{7,6},{8,9},{9,8},{10,11... | collective-permute-start | bytes 3145736 | tf_op jit(solution)/shard_map/ppermute | solution.py:354
  145.3 14.8 %collective-permute-start.3 = (bf16[128,2048]{1,0:T(8,128)(2,1)S(1)}, bf16[128,2048]{1,0:T(8,128)(2,1)S(1)}, u32[]{:S(2)}, u32[]{:S(2)}) collective-permute-start(bf16[128,2048]{1,0:T(8,128)(2,1)S(1)} %get-tuple-element.40), channel_id=1, source_target_pairs={{0,1},{1,0},{2,3},{3,2},{4,5},{5,4},{6,7},{7,6},{8,9},{9,8},{10,11... | collective-permute-start | bytes 1572872 | tf_op jit(solution)/shard_map/ppermute | solution.py:354
  145.9 25.0 %collective-permute-start.4 = (bf16[128,2048]{1,0:T(8,128)(2,1)S(1)}, bf16[128,2048]{1,0:T(8,128)(2,1)S(1)}, u32[]{:S(2)}, u32[]{:S(2)}) collective-permute-start(bf16[128,2048]{1,0:T(8,128)(2,1)S(1)} %get-tuple-element.44), channel_id=1, source_target_pairs={{0,1},{1,0},{2,3},{3,2},{4,5},{5,4},{6,7},{7,6},{8,9},{9,8},{10,11... | collective-permute-start | bytes 1572872 | tf_op jit(solution)/shard_map/ppermute | solution.py:354
  (7 other events, 7.0 us)

commit v6 on v5

--- a/solution.py
+++ b/solution.py
@@ -247,7 +247,7 @@
 def project_out(col_block, attended, weight, width, strips, kind, depth, at=0, add=None):
     rows = attended.shape[0]
     strip = rows // strips
-    step = min(1024, width)
+    step = min(1024 if depth > 512 else 512, width)
     steps = width // step
 
     def body(cols, x_ref, w_ref, *refs):

time: 173 us -> 174 us (level)
  no operation moved by 1% of the time
where the time goes in v6:
time: 174 us; the launch traced here: 173 us
  Pallas kernels  85 us (49%)
  waiting for transfers between devices  46.4 us (27%)
  starting transfers between devices  19.7 us (11%)
  local copies, waits for them, and re-layouts  17.9 us (10%)
  other arithmetic  3.42 us (2%)
    pallas_call x4, Pallas kernels, attend(): pl.pallas_call(body, grid=(count,), in_specs=in_specs, out_specs=pl.Block...  31.4 us
    ppermute x5, waiting for transfers between devices, swap(): return lax.ppermute(x, 'tp', [(i, (i + shift) % tp) for i in range(tp)])  29.3 us
    pallas_call x5, Pallas kernels, project_out(): pl.pallas_call(body, grid_spec=pltpu.PrefetchScalarGridSpec(num_scalar_pr...  21.8 us
    all_to_all x2, waiting for transfers between devices, exchange(): return lax.all_to_all(block, 'seq', 0, 0, tiled=True)  17.2 us
    pallas_call x6, Pallas kernels, project_rest(): pl.pallas_call(body, grid_spec=pltpu.PrefetchScalarGridSpec(num_scalar_pr...  16.4 us
    unnamed x49, local copies, waits for them, and re-layouts  15.8 us
    all_to_all x2, starting transfers between devices, exchange(): return lax.all_to_all(block, 'seq', 0, 0, tiled=True)  13 us
    pallas_call x3, Pallas kernels, project_own(): pl.pallas_call(body, grid_spec=pltpu.PrefetchScalarGridSpec(num_scalar_pr...  9.7 us
  transfers between devices with their start and end apart: 7, of which 7 were waited for; matrix products, arithmetic and copies ran while one was open for 3% of the time, Pallas kernels for 44%

profile of v6, /device:TPU:8, one launch (start us, length us, event | category | flops | bytes accessed | tf_op | source)
XLA Modules:
  0.0 172.8 jit_solution(16091394657879570471)
XLA Ops:
  3.9 1.6 pick_blocks.3
  5.5 1.7 copy-done.4
  7.1 6.4 %all-to-all-start = ((bf16[16,776,128]{2,1,0:T(8,128)(2,1)}), bf16[16,776,128]{2,1,0:T(8,128)(2,1)}, u32[]{:S(2)}, u32[]{:S(2)}) async-start(bf16[16,776,128]{2,1,0:T(8,128)(2,1)} %copy-done.4), calls=%async_computation | async-start | bytes 6356992 | tf_op jit(solution)/shard_map/all_to_all | solution.py:351
  19.1 2.0 %pick_blocks.2 = bf16[16,256,128]{2,1,0:T(8,128)(2,1)} custom-call(s32[16,2]{1,0:T(8,128)S(1)} %copy.13.table, s32[16]{0:T(128)S(1)} %copy-done.22, bf16[16,64,512]{2,1,0:T(8,128)(2,1)S(1)} %copy-done.6, bf16[16,64,512]{2,1,0:T(8,128)(2,1)S(1)} %copy-done.8), custom_call_target="tpu_custom_call" | custom-call | bytes 2097152 | tf_op jit(solution)/shard_map/pick_blocks/pallas_call | solution.py:71
  21.7 2.2 %copy-done = bf16[4096,512]{1,0:T(8,128)(2,1)S(1)} copy-done((bf16[4096,512]{1,0:T(8,128)(2,1)S(1)}, bf16[4096,512]{1,0:T(8,128)(2,1)}, u32[]{:S(2)}) %copy-start) | copy-done | bytes 4194328
  27.8 12.7 %collective-permute-done.refs_0_ = bf16[256,2048]{1,0:T(8,128)(2,1)S(1)} collective-permute-done((bf16[256,2048]{1,0:T(8,128)(2,1)}, bf16[256,2048]{1,0:T(8,128)(2,1)S(1)}, u32[]{:S(2)}, u32[]{:S(2)}) %collective-permute-start) | collective-permute-done | bytes 1048608 | tf_op jit(solution)/shard_map/ppermute | solution.py:354
  43.3 7.2 %project_own.5.refs_2_ = f32[512,2048]{1,0:T(8,128)S(1)} custom-call(s32[1]{0:T(128)} %bitcast.rows.cols, bf16[512,2048]{1,0:T(8,128)(2,1)S(1)} %copy-done.3, bf16[4096,2048]{1,0:T(8,128)(2,1)} %refs_1_.11), custom_call_target="tpu_custom_call" | custom-call | flops 4294967296 | bytes 12582912 | tf_op jit(solution)/shard_map/project_own/pallas_call | solution.py:97
  53.7 6.5 %project_rest.8.refs_0_ = bf16[16,256,128]{2,1,0:T(8,128)(2,1)S(1)} custom-call(s32[1]{0:T(128)} %bitcast.2.rows, bf16[256,2048]{1,0:T(8,128)(2,1)S(1)} %collective-permute-done.refs_0_, bf16[4096,2048]{1,0:T(8,128)(2,1)} %refs_1_.11, f32[512,2048]{1,0:T(8,128)S(1)} %project_own.5.refs_2_, f32[512,128]{1,0:T(8,128)S(1)} %get-tuple-element.50.refs_3_, ...), custom_call_target="tpu_custom_call" | custom-call | flops 2147483648 | bytes 12582912 | tf_op jit(solution)/shard_map/project_rest/pallas_call | solution.py:140
  60.2 4.8 %collective-permute-done.1.refs_0_ = bf16[256,2048]{1,0:T(8,128)(2,1)S(1)} collective-permute-done((bf16[256,2048]{1,0:T(8,128)(2,1)S(1)}, bf16[256,2048]{1,0:T(8,128)(2,1)S(1)}, u32[]{:S(2)}, u32[]{:S(2)}) %collective-permute-start.1) | collective-permute-done | bytes 1048608 | tf_op jit(solution)/shard_map/ppermute | solution.py:354
  66.8 6.5 %project_rest.11.refs_0_ = bf16[16,256,128]{2,1,0:T(8,128)(2,1)S(1)} custom-call(s32[1]{0:T(128)} %bitcast.2.rows, bf16[256,2048]{1,0:T(8,128)(2,1)S(1)} %collective-permute-done.1.refs_0_, bf16[4096,2048]{1,0:T(8,128)(2,1)} %refs_1_.11, f32[512,2048]{1,0:T(8,128)S(1)} %project_own.5.refs_2_, f32[512,128]{1,0:T(8,128)S(1)} %get-tuple-element.50.refs_3_, ...), custom_call_target="tpu_custom_call" | custom-call | flops 2147483648 | bytes 12582912 | tf_op jit(solution)/shard_map/project_rest/pallas_call | solution.py:140
  74.3 8.3 %all-to-all-done.refs_1_ = bf16[16,776,128]{2,1,0:T(8,128)(2,1)} async-done(((bf16[16,776,128]{2,1,0:T(8,128)(2,1)}), bf16[16,776,128]{2,1,0:T(8,128)(2,1)}, u32[]{:S(2)}, u32[]{:S(2)}) %all-to-all-start) | async-done | bytes 3178528 | tf_op jit(solution)/shard_map/all_to_all | solution.py:351
  82.6 6.6 %all-to-all-start.1 = ((bf16[16,256,128]{2,1,0:T(8,128)(2,1)}), bf16[16,256,128]{2,1,0:T(8,128)(2,1)}, u32[]{:S(2)}, u32[]{:S(2)}) async-start(bf16[16,256,128]{2,1,0:T(8,128)(2,1)} %pick_blocks.2), calls=%async_computation.1 | async-start | bytes 2097152 | tf_op jit(solution)/shard_map/all_to_all | solution.py:351
  89.9 10.6 %attend.4.x_ref.refs_5_ = bf16[256,2048]{1,0:T(8,128)(2,1)S(1)} custom-call(bf16[16,256,128]{2,1,0:T(8,128)(2,1)S(1)} %project_rest.8.refs_0_, bf16[16,776,128]{2,1,0:T(8,128)(2,1)} %all-to-all-done.refs_1_, f32[1,2048]{1,0:T(1,128)S(1)} %bitcast_convert_fusion.refs_2_, bf16[4,256,128]{2,1,0:T(8,128)(2,1)S(1)} %copy-done.14, ...), custom_call_target="tpu_custom_call" | custom-call | flops 7247757312 | bytes 3145728 | tf_op jit(solution)/shard_map/attend/pallas_call | solution.py:230
  100.6 4.0 %project_out.5.refs_0_ = f32[256,2048]{1,0:T(8,128)S(1)} custom-call(s32[1]{0:T(128)} %bitcast.1.cols, bf16[256,2048]{1,0:T(8,128)(2,1)S(1)} %attend.4.x_ref.refs_5_, bf16[2048,4096]{1,0:T(8,128)(2,1)} %w_ref.15), custom_call_target="tpu_custom_call" | custom-call | flops 1610612736 | bytes 8388608 | tf_op jit(solution)/shard_map/project_out/pallas_call | solution.py:268
  104.6 8.9 %all-to-all-done.1.refs_1_ = bf16[16,256,128]{2,1,0:T(8,128)(2,1)} async-done(((bf16[16,256,128]{2,1,0:T(8,128)(2,1)}), bf16[16,256,128]{2,1,0:T(8,128)(2,1)}, u32[]{:S(2)}, u32[]{:S(2)}) %all-to-all-start.1) | async-done | bytes 1048608 | tf_op jit(solution)/shard_map/all_to_all | solution.py:351
  115.7 4.3 %attend.5.x_ref = bf16[256,2048]{1,0:T(8,128)(2,1)S(1)} custom-call(bf16[16,256,128]{2,1,0:T(8,128)(2,1)S(1)} %copy-done.12, bf16[16,256,128]{2,1,0:T(8,128)(2,1)} %all-to-all-done.1.refs_1_, f32[1,2048]{1,0:T(1,128)S(1)} %bitcast_convert_fusion.refs_2_, bf16[4,256,128]{2,1,0:T(8,128)(2,1)S(1)} %copy-done.15, ...), custom_call_target="tpu_custom_call", output_to_operand_aliasing={{}: (5, {})} | custom-call | flops 2415919104 | bytes 1048576 | tf_op jit(solution)/shard_map/attend/pallas_call | solution.py:230
  120.1 3.3 %project_out.6 = bf16[256,2048]{1,0:T(8,128)(2,1)S(1)} custom-call(s32[1]{0:T(128)} %bitcast.1.cols, bf16[256,2048]{1,0:T(8,128)(2,1)S(1)} %attend.5.x_ref, bf16[2048,4096]{1,0:T(8,128)(2,1)} %w_ref.15, f32[256,2048]{1,0:T(8,128)S(1)} %project_out.5.refs_0_), custom_call_target="tpu_custom_call" | custom-call | flops 536870912 | bytes 4194304 | tf_op jit(solution)/shard_map/project_out/pallas_call | solution.py:268
  123.4 1.6 collective-permute-start.2
  125.0 11.8 %attend.6.refs_7_ = bf16[256,2048]{1,0:T(8,128)(2,1)S(1)} custom-call(bf16[16,256,128]{2,1,0:T(8,128)(2,1)S(1)} %copy-done.10, bf16[16,776,128]{2,1,0:T(8,128)(2,1)} %all-to-all-done.refs_1_, f32[1,2048]{1,0:T(1,128)S(1)} %bitcast_convert_fusion.refs_2_, bf16[4,256,128]{2,1,0:T(8,128)(2,1)S(1)} %copy-done.16, bf16[4,256,128]{2,1,0:T(8,128)(2,1)S(1)} %copy-done.18, ...), custom_call_target="tpu_custom_call" | custom-call | flops 8053063680 | bytes 3145728 | tf_op jit(solution)/shard_map/attend/pallas_call | solution.py:230
  136.8 4.7 %attend.7.x_ref = bf16[256,2048]{1,0:T(8,128)(2,1)S(1)} custom-call(bf16[16,256,128]{2,1,0:T(8,128)(2,1)S(1)} %copy-done.10, bf16[16,256,128]{2,1,0:T(8,128)(2,1)} %all-to-all-done.1.refs_1_, f32[1,2048]{1,0:T(1,128)S(1)} %bitcast_convert_fusion.refs_2_, bf16[4,256,128]{2,1,0:T(8,128)(2,1)S(1)} %copy-done.16, ...), custom_call_target="tpu_custom_call", output_to_operand_aliasing={{}: (7, {})} | custom-call | flops 2684354560 | bytes 1048576 | tf_op jit(solution)/shard_map/attend/pallas_call | solution.py:230
  141.5 4.8 %project_out.8 = (bf16[128,2048]{1,0:T(8,128)(2,1)S(1)}, bf16[128,2048]{1,0:T(8,128)(2,1)S(1)}) custom-call(s32[1]{0:T(128)} %bitcast.1.cols, bf16[256,2048]{1,0:T(8,128)(2,1)S(1)} %attend.7.x_ref, bf16[2048,4096]{1,0:T(8,128)(2,1)} %w_ref.15), custom_call_target="tpu_custom_call" | custom-call | flops 2147483648 | bytes 10485760 | tf_op jit(solution)/shard_map/project_out/pallas_call | solution.py:268
  149.3 4.8 %project_out.9.refs_0_ = f32[256,2048]{1,0:T(8,128)S(1)} custom-call(s32[1]{0:T(128)} %bitcast.rows.cols, bf16[256,2048]{1,0:T(8,128)(2,1)S(1)} %attend.5.x_ref, bf16[2048,4096]{1,0:T(8,128)(2,1)} %w_ref.15), custom_call_target="tpu_custom_call" | custom-call | flops 2147483648 | bytes 10485760 | tf_op jit(solution)/shard_map/project_out/pallas_call | solution.py:268
  155.3 4.8 %project_out.7 = (f32[128,2048]{1,0:T(8,128)S(1)}, f32[128,2048]{1,0:T(8,128)S(1)}) custom-call(s32[1]{0:T(128)} %bitcast.rows.cols, bf16[256,2048]{1,0:T(8,128)(2,1)S(1)} %attend.7.x_ref, bf16[2048,4096]{1,0:T(8,128)(2,1)} %w_ref.15), custom_call_target="tpu_custom_call" | custom-call | flops 2147483648 | bytes 10485760 | tf_op jit(solution)/shard_map/project_out/pallas_call | solution.py:268
  162.0 9.9 %collective-permute-done.4 = bf16[128,2048]{1,0:T(8,128)(2,1)S(1)} collective-permute-done((bf16[128,2048]{1,0:T(8,128)(2,1)S(1)}, bf16[128,2048]{1,0:T(8,128)(2,1)S(1)}, u32[]{:S(2)}, u32[]{:S(2)}) %collective-permute-start.4) | collective-permute-done | bytes 524320 | tf_op jit(solution)/shard_map/ppermute | solution.py:354
  (69 shorter events, 32.4 us)
Async XLA Ops:
  5.4 1.7 copy-start.4
  7.1 6.4 %copy-start.3 = (bf16[512,2048]{1,0:T(8,128)(2,1)S(1)}, bf16[512,2048]{1,0:T(8,128)(2,1)}, u32[]{:S(2)}) copy-start(bf16[512,2048]{1,0:T(8,128)(2,1)} %x_ref.5) | copy-start | bytes 6291460
  7.1 75.5 %all-to-all-start = ((bf16[16,776,128]{2,1,0:T(8,128)(2,1)}), bf16[16,776,128]{2,1,0:T(8,128)(2,1)}, u32[]{:S(2)}, u32[]{:S(2)}) async-start(bf16[16,776,128]{2,1,0:T(8,128)(2,1)} %copy-done.4), calls=%async_computation | async-start | bytes 6356992 | tf_op jit(solution)/shard_map/all_to_all | solution.py:351
  13.6 3.1 %copy-start.22 = (s32[16]{0:T(128)S(1)}, s32[16]{0:T(128)}, u32[]{:S(2)}) copy-start(s32[16]{0:T(128)} %lengths.3) | copy-start | bytes 196
  15.1 25.4 %collective-permute-start = (bf16[256,2048]{1,0:T(8,128)(2,1)}, bf16[256,2048]{1,0:T(8,128)(2,1)S(1)}, u32[]{:S(2)}, u32[]{:S(2)}) collective-permute-start(bf16[256,2048]{1,0:T(8,128)(2,1)} %get-tuple-element.45), channel_id=1, source_target_pairs={{0,1},{1,0},{2,3},{3,2},{4,5},{5,4},{6,7},{7,6},{8,9},{9,8},{10,11... | collective-permute-start | bytes 3145736 | tf_op jit(solution)/shard_map/ppermute | solution.py:354
  16.7 1.2 copy-start.6
  21.6 2.2 %copy-start = (bf16[4096,512]{1,0:T(8,128)(2,1)S(1)}, bf16[4096,512]{1,0:T(8,128)(2,1)}, u32[]{:S(2)}) copy-start(bf16[4096,512]{1,0:T(8,128)(2,1)} %refs_1_.9) | copy-start | bytes 12582916
  23.8 2.2 %copy-start.2 = (bf16[4096,512]{1,0:T(8,128)(2,1)S(1)}, bf16[4096,512]{1,0:T(8,128)(2,1)}, u32[]{:S(2)}) copy-start(bf16[4096,512]{1,0:T(8,128)(2,1)} %refs_1_.10) | copy-start | bytes 12582916
  26.0 14.5 %copy-start.23 = (bf16[256,2048]{1,0:T(8,128)(2,1)S(1)}, bf16[256,2048]{1,0:T(8,128)(2,1)}, u32[]{:S(2)}) copy-start(bf16[256,2048]{1,0:T(8,128)(2,1)} %get-tuple-element.26) | copy-start | bytes 3145732
  40.6 24.5 %collective-permute-start.1 = (bf16[256,2048]{1,0:T(8,128)(2,1)S(1)}, bf16[256,2048]{1,0:T(8,128)(2,1)S(1)}, u32[]{:S(2)}, u32[]{:S(2)}) collective-permute-start(bf16[256,2048]{1,0:T(8,128)(2,1)S(1)} %copy-done.23), channel_id=1, source_target_pairs={{0,1},{1,0},{2,3},{3,2},{4,5},{5,4},{6,7},{7,6},{8,9},{9,8},{10,11... | collective-permute-start | bytes 3145736 | tf_op jit(solution)/shard_map/ppermute | solution.py:354
  50.5 2.2 %copy-start.1 = (bf16[4096,512]{1,0:T(8,128)(2,1)S(1)}, bf16[4096,512]{1,0:T(8,128)(2,1)}, u32[]{:S(2)}) copy-start(bf16[4096,512]{1,0:T(8,128)(2,1)} %refs_1_.9) | copy-start | bytes 12582916
  53.7 6.5 %copy-start.13 = (bf16[4,256,128]{2,1,0:T(8,128)(2,1)}, bf16[4,256,128]{2,1,0:T(8,128)(2,1)S(1)}, u32[]{:S(2)}) copy-start(bf16[4,256,128]{2,1,0:T(8,128)(2,1)S(1)} %project_rest.6.refs_3_) | copy-start | bytes 786436
  60.2 29.7 %copy-start.11 = (bf16[16,256,128]{2,1,0:T(8,128)(2,1)}, bf16[16,256,128]{2,1,0:T(8,128)(2,1)S(1)}, u32[]{:S(2)}) copy-start(bf16[16,256,128]{2,1,0:T(8,128)(2,1)S(1)} %project_rest.8.refs_0_) | copy-start | bytes 3145732
  66.8 6.5 %copy-start.19 = (bf16[4,256,128]{2,1,0:T(8,128)(2,1)}, bf16[4,256,128]{2,1,0:T(8,128)(2,1)S(1)}, u32[]{:S(2)}) copy-start(bf16[4,256,128]{2,1,0:T(8,128)(2,1)S(1)} %project_rest.10.refs_6_) | copy-start | bytes 786436
  74.3 15.6 %copy-start.14 = (bf16[4,256,128]{2,1,0:T(8,128)(2,1)S(1)}, bf16[4,256,128]{2,1,0:T(8,128)(2,1)}, u32[]{:S(2)}) copy-start(bf16[4,256,128]{2,1,0:T(8,128)(2,1)} %copy-done.13) | copy-start | bytes 786436
  82.6 30.9 %all-to-all-start.1 = ((bf16[16,256,128]{2,1,0:T(8,128)(2,1)}), bf16[16,256,128]{2,1,0:T(8,128)(2,1)}, u32[]{:S(2)}, u32[]{:S(2)}) async-start(bf16[16,256,128]{2,1,0:T(8,128)(2,1)} %pick_blocks.2), calls=%async_computation.1 | async-start | bytes 2097152 | tf_op jit(solution)/shard_map/all_to_all | solution.py:351
  113.5 1.2 copy-start.12
  120.0 4.9 %copy-start.10 = (bf16[16,256,128]{2,1,0:T(8,128)(2,1)S(1)}, bf16[16,256,128]{2,1,0:T(8,128)(2,1)}, u32[]{:S(2)}) copy-start(bf16[16,256,128]{2,1,0:T(8,128)(2,1)} %copy-done.9) | copy-start | bytes 3145732
  120.0 4.9 %copy-start.16 = (bf16[4,256,128]{2,1,0:T(8,128)(2,1)S(1)}, bf16[4,256,128]{2,1,0:T(8,128)(2,1)}, u32[]{:S(2)}) copy-start(bf16[4,256,128]{2,1,0:T(8,128)(2,1)} %copy-done.13) | copy-start | bytes 786436
  120.0 4.9 %copy-start.18 = (bf16[4,256,128]{2,1,0:T(8,128)(2,1)S(1)}, bf16[4,256,128]{2,1,0:T(8,128)(2,1)}, u32[]{:S(2)}) copy-start(bf16[4,256,128]{2,1,0:T(8,128)(2,1)} %copy-done.17) | copy-start | bytes 786436
  120.1 4.9 %copy-start.20 = (bf16[4,256,128]{2,1,0:T(8,128)(2,1)S(1)}, bf16[4,256,128]{2,1,0:T(8,128)(2,1)}, u32[]{:S(2)}) copy-start(bf16[4,256,128]{2,1,0:T(8,128)(2,1)} %copy-done.19) | copy-start | bytes 786436
  123.4 25.9 %collective-permute-start.2 = (bf16[256,2048]{1,0:T(8,128)(2,1)S(1)}, bf16[256,2048]{1,0:T(8,128)(2,1)S(1)}, u32[]{:S(2)}, u32[]{:S(2)}) collective-permute-start(bf16[256,2048]{1,0:T(8,128)(2,1)S(1)} %project_out.6), channel_id=1, source_target_pairs={{0,1},{1,0},{2,3},{3,2},{4,5},{5,4},{6,7},{7,6},{8,9},{9,8},{10,11... | collective-permute-start | bytes 3145736 | tf_op jit(solution)/shard_map/ppermute | solution.py:354
  146.3 14.8 %collective-permute-start.3 = (bf16[128,2048]{1,0:T(8,128)(2,1)S(1)}, bf16[128,2048]{1,0:T(8,128)(2,1)S(1)}, u32[]{:S(2)}, u32[]{:S(2)}) collective-permute-start(bf16[128,2048]{1,0:T(8,128)(2,1)S(1)} %get-tuple-element.40), channel_id=1, source_target_pairs={{0,1},{1,0},{2,3},{3,2},{4,5},{5,4},{6,7},{7,6},{8,9},{9,8},{10,11... | collective-permute-start | bytes 1572872 | tf_op jit(solution)/shard_map/ppermute | solution.py:354
  146.8 25.0 %collective-permute-start.4 = (bf16[128,2048]{1,0:T(8,128)(2,1)S(1)}, bf16[128,2048]{1,0:T(8,128)(2,1)S(1)}, u32[]{:S(2)}, u32[]{:S(2)}) collective-permute-start(bf16[128,2048]{1,0:T(8,128)(2,1)S(1)} %get-tuple-element.44), channel_id=1, source_target_pairs={{0,1},{1,0},{2,3},{3,2},{4,5},{5,4},{6,7},{7,6},{8,9},{9,8},{10,11... | collective-permute-start | bytes 1572872 | tf_op jit(solution)/shard_map/ppermute | solution.py:354
  (7 other events, 7.0 us)
